TPU v7x, 32 devices: a whole 2x2x4 slice. The times are simulated.
32 devices in a mesh: dp: 8 (over y, x, core), seq: 4 (over z).
Axes of the slice: x: 2, y: 2, z: 4, core: 2. Of those that a mesh axis runs over, the one named last changes fastest.
Arguments:
- inputs: bfloat16 [24, 1024, 768], P('dp', 'seq'), may hold values from -6 to 6
- cotangent: bfloat16 [24, 1024, 768], P('dp', 'seq'), may hold values from -6 to 6
- lengths: int32 [24], P('dp'), may hold values from 100 to 1024, as said below
- predicted: int32 [24, 1024], P('dp', 'seq'), may hold values from 0 to 69
- norm1_gain: float32 [768], replicated, may hold values from 0.1 to 1.9
- norm1_shift: float32 [768], replicated, may hold values from -4 to 4
- w_query: bfloat16 [768, 768], replicated, may hold values from -0.3125 to 0.3125
- b_query: float32 [768], replicated, may hold values from -6 to 6
- w_key: bfloat16 [768, 768], replicated, may hold values from -0.3125 to 0.3125
- b_key: float32 [768], replicated, may hold values from -6 to 6
- w_value: bfloat16 [768, 768], replicated, may hold values from -0.21875 to 0.21875
- b_value: float32 [768], replicated, may hold values from -6 to 6
- w_out: bfloat16 [768, 768], replicated, may hold values from -2 to 2
- b_out: float32 [768], replicated, may hold values from -6 to 6
- norm2_gain: float32 [768], replicated, may hold values from 0.1 to 1.9
- norm2_shift: float32 [768], replicated, may hold values from -4 to 4
- w_up: bfloat16 [768, 3072], replicated, may hold values from -0.21875 to 0.21875
- b_up: float32 [3072], replicated, may hold values from -6 to 6
- w_down: bfloat16 [3072, 768], replicated, may hold values from -0.109375 to 0.109375
- b_down: float32 [768], replicated, may hold values from -6 to 6
Outputs:
- result: bfloat16 [24, 1024, 768], P('dp', 'seq')
- grad_inputs: bfloat16 [24, 1024, 768], P('dp', 'seq')
- grad_norm1_gain: float32 [768], replicated
- grad_norm1_shift: float32 [768], replicated
- grad_w_query: float32 [768, 768], replicated
- grad_b_query: float32 [768], replicated
- grad_w_key: float32 [768, 768], replicated
- grad_b_key: float32 [768], replicated
- grad_w_value: float32 [768, 768], replicated
- grad_b_value: float32 [768], replicated
- grad_w_out: float32 [768, 768], replicated
- grad_b_out: float32 [768], replicated
- grad_norm2_gain: float32 [768], replicated
- grad_norm2_shift: float32 [768], replicated
- grad_w_up: float32 [768, 3072], replicated
- grad_b_up: float32 [3072], replicated
- grad_w_down: float32 [3072, 768], replicated
- grad_b_down: float32 [768], replicated
- histogram: int32 [70], replicated
Inputs may be any that keep to these rules, and one draw needn't show every extreme that they name: Some sequence has 1024 real codons and some has 100; the codons from position lengths[s] on are padding.
All inputs are finite; a program needn't handle non-finite values.
Results may differ from a plain program's by a relative error of at most 0.014.
The roundings to bfloat16 on the way count: a program that leaves them out, or rounds other values in their place, can miss the bound.
Values may be sent and summed in bfloat16 or wider, within the bound.
No kernel may reach another device: no remote copies, remote signals or barrier semaphores. Data moves between devices by JAX's collectives and lax.ppermute only.
A program may use at most 192 MiB of HBM per device.

v0:
```python
import jax
import jax.numpy as jnp
from jax import lax
from jax.sharding import PartitionSpec as P

HEAD = 64
CLASSES = 70


epsilon = 1e-05


def matmul(left, right):
    return jnp.dot(left, right, preferred_element_type=jnp.float32)


def matmul_left(left, right):
    return lax.dot_general(
        left, right, (((0,), (0,)), ((), ())), preferred_element_type=jnp.float32
    )


def matmul_right(left, right):
    return lax.dot_general(
        left, right, (((1,), (1,)), ((), ())), preferred_element_type=jnp.float32
    )


def layer_norm(value, gain, shift):
    centre = value - jnp.mean(value, axis=-1, keepdims=True)
    scale = lax.rsqrt(jnp.mean(centre * centre, axis=-1, keepdims=True) + epsilon)
    return centre * scale * gain + shift


def gelu(value):
    return jax.nn.gelu(value, approximate=False)


def rotate(value, direction):
    count = value.shape[-3]
    half = value.shape[-1] // 2
    frequency = 10000.0 ** (-jnp.arange(half, dtype=jnp.float32) / half)
    angle = jnp.arange(count, dtype=jnp.float32)[:, None] * frequency[None, :]
    cosine = jnp.cos(angle)[:, None, :]
    sine = direction * jnp.sin(angle)[:, None, :]
    first = value[..., :half]
    second = value[..., half:]
    return jnp.concatenate(
        [first * cosine - second * sine, second * cosine + first * sine], axis=-1
    )


def attend_forward(query, key, value, valid, block):
    count, heads, size = query.shape
    scale = HEAD ** (-0.5)
    blocks = query.reshape(count // block, block, heads, size)

    def visit(query_block):
        scores = (
            jnp.einsum("qhd,khd->hqk", query_block, key, preferred_element_type=jnp.float32) * scale
        )
        scores = jnp.where(valid[None, None, :], scores, -1e30)
        peak = jnp.max(scores, axis=-1, keepdims=True)
        total = jnp.sum(jnp.exp(scores - peak), axis=-1, keepdims=True)
        logsum = peak + jnp.log(total)
        weights = jnp.exp(scores - logsum).astype(jnp.bfloat16)
        mixed = jnp.einsum("hqk,khd->qhd", weights, value, preferred_element_type=jnp.float32)
        return (mixed.astype(jnp.bfloat16), logsum[..., 0])

    mixed, logsum = lax.map(visit, blocks)
    return (mixed.reshape(count, heads * size), logsum)


def attend_backward(query, key, value, valid, logsum, grad_mixed, block):
    count, heads, size = query.shape
    number = count // block
    scale = HEAD ** (-0.5)
    query_blocks = query.reshape(number, block, heads, size)
    grad_blocks = grad_mixed.reshape(number, block, heads, size)

    def visit(carry, item):
        grad_key, grad_value = carry
        query_block, grad_block, logsum_block = item
        scores = (
            jnp.einsum("qhd,khd->hqk", query_block, key, preferred_element_type=jnp.float32) * scale
        )
        scores = jnp.where(valid[None, None, :], scores, -1e30)
        weights = jnp.exp(scores - logsum_block[..., None])
        weights_low = weights.astype(jnp.bfloat16)
        grad_weights = jnp.einsum(
            "qhd,khd->hqk", grad_block, value, preferred_element_type=jnp.float32
        )
        inner = jnp.sum(weights * grad_weights, axis=-1, keepdims=True)
        grad_scores = (weights * (grad_weights - inner)).astype(jnp.bfloat16)
        grad_query = (
            jnp.einsum("hqk,khd->qhd", grad_scores, key, preferred_element_type=jnp.float32) * scale
        )
        grad_key = (
            grad_key
            + jnp.einsum(
                "hqk,qhd->khd", grad_scores, query_block, preferred_element_type=jnp.float32
            )
            * scale
        )
        grad_value = grad_value + jnp.einsum(
            "hqk,qhd->khd", weights_low, grad_block, preferred_element_type=jnp.float32
        )
        return ((grad_key, grad_value), grad_query)

    start = jnp.zeros((count, heads, size), jnp.float32)
    (grad_key, grad_value), grad_query = lax.scan(
        visit, (start, start), (query_blocks, grad_blocks, logsum)
    )
    grad_query = rotate(grad_query.reshape(count, heads, size), -1.0).astype(jnp.bfloat16)
    grad_key = rotate(grad_key, -1.0).astype(jnp.bfloat16)
    grad_value = grad_value.astype(jnp.bfloat16)
    return (
        grad_query.reshape(count, heads * size),
        grad_key.reshape(count, heads * size),
        grad_value.reshape(count, heads * size),
    )


def on_device(
    inputs,
    cotangent,
    lengths,
    predicted,
    norm1_gain,
    norm1_shift,
    w_query,
    b_query,
    w_key,
    b_key,
    w_value,
    b_value,
    w_out,
    b_out,
    norm2_gain,
    norm2_shift,
    w_up,
    b_up,
    w_down,
    b_down,
):
    seqs, span, width = inputs.shape
    tokens = seqs * span
    hidden_width = w_up.shape[1]
    flat_in = inputs.reshape(tokens, width).astype(jnp.float32)
    normed_full, norm1_back = jax.vjp(layer_norm, flat_in, norm1_gain, norm1_shift)
    normed = normed_full.astype(jnp.bfloat16)
    query = (matmul(normed, w_query) + b_query).astype(jnp.bfloat16).reshape(seqs, span, width)
    key = (matmul(normed, w_key) + b_key).astype(jnp.bfloat16).reshape(seqs, span, width)
    value = (matmul(normed, w_value) + b_value).astype(jnp.bfloat16).reshape(seqs, span, width)
    head_query, head_key, head_value = (
        lax.all_to_all(query, "seq", split_axis=2, concat_axis=1, tiled=True),
        lax.all_to_all(key, "seq", split_axis=2, concat_axis=1, tiled=True),
        lax.all_to_all(value, "seq", split_axis=2, concat_axis=1, tiled=True),
    )
    count = head_query.shape[1]
    heads = head_query.shape[2] // HEAD
    shaped = (seqs, count, heads, HEAD)
    rot_query = rotate(head_query.reshape(shaped).astype(jnp.float32), 1.0).astype(jnp.bfloat16)
    rot_key = rotate(head_key.reshape(shaped).astype(jnp.float32), 1.0).astype(jnp.bfloat16)
    head_value = head_value.reshape(shaped)
    valid = jnp.arange(count)[None, :] < lengths[:, None]
    block = min(count, 512)
    mixed, logsum = lax.map(
        lambda item: attend_forward(item[0], item[1], item[2], item[3], block),
        (rot_query, rot_key, head_value, valid),
    )
    attended = lax.all_to_all(mixed, "seq", split_axis=1, concat_axis=2, tiled=True).reshape(
        tokens, width
    )
    middle = flat_in + matmul(attended, w_out) + b_out
    normed2_full, norm2_back = jax.vjp(layer_norm, middle, norm2_gain, norm2_shift)
    normed2 = normed2_full.astype(jnp.bfloat16)
    hidden_in = matmul(normed2, w_up) + b_up
    hidden = gelu(hidden_in).astype(jnp.bfloat16)
    result = (
        (middle + matmul(hidden, w_down) + b_down).astype(jnp.bfloat16).reshape(seqs, span, width)
    )
    grad_result = cotangent.reshape(tokens, width)
    grad_result_full = grad_result.astype(jnp.float32)
    grad_w_down = matmul_left(hidden, grad_result)
    grad_b_down = jnp.sum(grad_result_full, axis=0)
    unused, gelu_back = jax.vjp(gelu, hidden_in)
    grad_hidden_in = gelu_back(matmul_right(grad_result, w_down))[0].astype(jnp.bfloat16)
    grad_w_up = matmul_left(normed2, grad_hidden_in)
    grad_b_up = jnp.sum(grad_hidden_in.astype(jnp.float32), axis=0)
    grad_from_norm2, grad_norm2_gain, grad_norm2_shift = norm2_back(
        matmul_right(grad_hidden_in, w_up)
    )
    grad_middle = grad_result_full + grad_from_norm2
    grad_branch = grad_middle.astype(jnp.bfloat16)
    grad_w_out = matmul_left(attended, grad_branch)
    grad_b_out = jnp.sum(grad_middle, axis=0)
    grad_attended = matmul_right(grad_branch, w_out).astype(jnp.bfloat16).reshape(seqs, span, width)
    grad_mixed = lax.all_to_all(
        grad_attended, "seq", split_axis=2, concat_axis=1, tiled=True
    ).reshape(shaped)
    grad_query, grad_key, grad_value = lax.map(
        lambda item: attend_backward(item[0], item[1], item[2], item[3], item[4], item[5], block),
        (rot_query, rot_key, head_value, valid, logsum, grad_mixed),
    )
    back_query, back_key, back_value = (
        lax.all_to_all(grad_query, "seq", split_axis=1, concat_axis=2, tiled=True),
        lax.all_to_all(grad_key, "seq", split_axis=1, concat_axis=2, tiled=True),
        lax.all_to_all(grad_value, "seq", split_axis=1, concat_axis=2, tiled=True),
    )
    back_query = back_query.reshape(tokens, width)
    back_key = back_key.reshape(tokens, width)
    back_value = back_value.reshape(tokens, width)
    grad_w_query = matmul_left(normed, back_query)
    grad_w_key = matmul_left(normed, back_key)
    grad_w_value = matmul_left(normed, back_value)
    grad_b_query = jnp.sum(back_query.astype(jnp.float32), axis=0)
    grad_b_key = jnp.sum(back_key.astype(jnp.float32), axis=0)
    grad_b_value = jnp.sum(back_value.astype(jnp.float32), axis=0)
    grad_normed = (
        matmul_right(back_query, w_query)
        + matmul_right(back_key, w_key)
        + matmul_right(back_value, w_value)
    )
    grad_from_norm1, grad_norm1_gain, grad_norm1_shift = norm1_back(grad_normed)
    grad_inputs = (grad_middle + grad_from_norm1).astype(jnp.bfloat16).reshape(seqs, span, width)
    position = lax.axis_index("seq") * span + jnp.arange(span)
    live = position[None, :] < lengths[:, None]
    classes = jnp.arange(CLASSES)
    counts = jnp.sum(
        jnp.where(live[:, :, None] & (predicted[:, :, None] == classes), 1.0, 0.0), axis=(0, 1)
    )
    (
        grad_norm1_gain,
        grad_norm1_shift,
        grad_b_query,
        grad_b_key,
        grad_b_value,
        grad_b_out,
        grad_norm2_gain,
        grad_norm2_shift,
        grad_b_up,
        grad_b_down,
        counts,
    ) = lax.psum(
        (
            grad_norm1_gain,
            grad_norm1_shift,
            grad_b_query,
            grad_b_key,
            grad_b_value,
            grad_b_out,
            grad_norm2_gain,
            grad_norm2_shift,
            grad_b_up,
            grad_b_down,
            counts,
        ),
        ("dp", "seq"),
    )
    part_query = grad_w_query.reshape(-1)
    part_key = grad_w_key.reshape(-1)
    part_value = grad_w_value.reshape(-1)
    part_out = grad_w_out.reshape(-1)
    part_up = grad_w_up.reshape(-1)
    part_down = grad_w_down.reshape(-1)
    part_query, part_key, part_value, part_out, part_up, part_down = (
        lax.psum_scatter(part_query, ("dp", "seq"), scatter_dimension=0, tiled=True),
        lax.psum_scatter(part_key, ("dp", "seq"), scatter_dimension=0, tiled=True),
        lax.psum_scatter(part_value, ("dp", "seq"), scatter_dimension=0, tiled=True),
        lax.psum_scatter(part_out, ("dp", "seq"), scatter_dimension=0, tiled=True),
        lax.psum_scatter(part_up, ("dp", "seq"), scatter_dimension=0, tiled=True),
        lax.psum_scatter(part_down, ("dp", "seq"), scatter_dimension=0, tiled=True),
    )
    part_query, part_key, part_value, part_out, part_up, part_down = (
        lax.all_gather(part_query, ("dp", "seq"), axis=0, tiled=True),
        lax.all_gather(part_key, ("dp", "seq"), axis=0, tiled=True),
        lax.all_gather(part_value, ("dp", "seq"), axis=0, tiled=True),
        lax.all_gather(part_out, ("dp", "seq"), axis=0, tiled=True),
        lax.all_gather(part_up, ("dp", "seq"), axis=0, tiled=True),
        lax.all_gather(part_down, ("dp", "seq"), axis=0, tiled=True),
    )
    return (
        result,
        grad_inputs,
        grad_norm1_gain,
        grad_norm1_shift,
        part_query.reshape(width, width),
        grad_b_query,
        part_key.reshape(width, width),
        grad_b_key,
        part_value.reshape(width, width),
        grad_b_value,
        part_out.reshape(width, width),
        grad_b_out,
        grad_norm2_gain,
        grad_norm2_shift,
        part_up.reshape(width, hidden_width),
        grad_b_up,
        part_down.reshape(hidden_width, width),
        grad_b_down,
        counts.astype(jnp.int32),
    )


def solution(mesh):
    return jax.shard_map(
        on_device,
        mesh=mesh,
        in_specs=(
            P("dp", "seq", None),
            P("dp", "seq", None),
            P("dp"),
            P("dp", "seq"),
            P(),
            P(),
            P(),
            P(),
            P(),
            P(),
            P(),
            P(),
            P(),
            P(),
            P(),
            P(),
            P(),
            P(),
            P(),
            P(),
        ),
        out_specs=(
            P("dp", "seq", None),
            P("dp", "seq", None),
            P(),
            P(),
            P(),
            P(),
            P(),
            P(),
            P(),
            P(),
            P(),
            P(),
            P(),
            P(),
            P(),
            P(),
            P(),
            P(),
            P(),
        ),
        check_vma=False,
    )
```

profile of v0, /device:TPU:0, one launch (start us, length us, event | category | flops | bytes accessed | tf_op | source)
XLA Modules:
  0.0 1592.6 jit_solution(14903146880478550544)
XLA Ops:
  29.5 29.6 %all-to-all-done.1 = bf16[3,256,768]{1,0,2:T(4,128)(2,1)S(1)} async-done(((bf16[3,256,768]{1,0,2:T(4,128)(2,1)}), bf16[3,256,768]{1,0,2:T(4,128)(2,1)S(1)}, u32[]{:S(2)}, u32[]{:S(2)}) %all-to-all-start.1) | async-done | bytes 1179680 | tf_op jit(solution)/shard_map/all_to_all | solution.py:157
  70.5 29.5 %all-to-all-done = bf16[3,256,768]{1,0,2:T(4,128)(2,1)} async-done(((bf16[3,256,768]{1,0,2:T(4,128)(2,1)}), bf16[3,256,768]{1,0,2:T(4,128)(2,1)}, u32[]{:S(2)}, u32[]{:S(2)}) %all-to-all-start) | async-done | bytes 1179680 | tf_op jit(solution)/shard_map/all_to_all | solution.py:156
  115.8 25.4 %all-to-all-done.2 = bf16[3,256,768]{1,0,2:T(4,128)(2,1)} async-done(((bf16[3,256,768]{1,0,2:T(4,128)(2,1)}), bf16[3,256,768]{1,0,2:T(4,128)(2,1)}, u32[]{:S(2)}, u32[]{:S(2)}) %all-to-all-start.2) | async-done | bytes 1179680 | tf_op jit(solution)/shard_map/all_to_all | solution.py:158
  153.4 43.9 %while.54 = (s32[]{:T(128)}, bf16[3,1024,192]{1,2,0:T(8,128)(2,1)}, f32[3,2,3,512]{3,2,1,0:T(4,128)}, bf16[3,1024,3,64]{1,3,2,0:T(8,128)(2,1)}, bf16[3,1024,3,64...) while((s32[]{:T(128)}, bf16[3,1024,192]{1,2,0:T(8,128)(2,1)}, ...), condition=%wide.region_7.8_spmd, body=%wide.region_2.7_spmd.sunk | while | flops 420051456 | bytes 28114308 | solution.py:168
  201.5 51.3 %all_to_all.108 = bf16[3,1024,192]{2,0,1:T(4,128)(2,1)S(1)} all-to-all(bf16[3,1024,192]{2,0,1:T(4,128)(2,1)} %copy.117), channel_id=1, replica_groups=mesh['dp'=8,'seq'=4] {'seq'}, dimensions={1} | all-to-all | bytes 2359296 | tf_op jit(solution)/shard_map/all_to_all | solution.py:172
  269.5 27.6 %convert_reduce_fusion = (f32[3072]{0:T(1024)}, bf16[768,3072]{1,0:T(8,128)(2,1)S(1)}, f32[768,3072]{1,0:T(8,128)}) fusion(f32[768,3072]{1,0:T(8,128)S(1)} %fusion.73, f32[3072]{0:T(1024)S(1)} %copy-done.58, bf16[768,768]{1,0:T(8,128)(2,1)S(1)} %bitcast.247, bf16[3072,768]{1,0:T(8,128)(2,1)S(1)} %bitcast.262), kind=kOutput, calls=%fused_computation.74 | convolution fusion | flops 3800822784 | bytes 29515776 | tf_op jit(solution)/shard_map/dot_general | solution.py:24
  311.3 36.0 %all-to-all-done.4 = bf16[3,256,768]{1,0,2:T(4,128)(2,1)S(1)} async-done(((bf16[3,256,768]{1,0,2:T(4,128)(2,1)}), bf16[3,256,768]{1,0,2:T(4,128)(2,1)S(1)}, u32[]{:S(2)}, u32[]{:S(2)}) %all-to-all-start.4) | async-done | bytes 1179680 | tf_op jit(solution)/shard_map/all_to_all | solution.py:199
  352.7 180.7 %while.56 = (s32[]{:T(128)}, bf16[3,1024,192]{1,2,0:T(8,128)(2,1)}, bf16[3,1024,192]{1,2,0:T(8,128)(2,1)}, bf16[3,1024,192]{1,2,0:T(8,128)(2,1)}, bf16[3,1024,3,...) while((s32[]{:T(128)}, bf16[3,1024,192]{1,2,0:T(8,128)(2,1)}, ...), condition=%wide.region_16.17_spmd, body=%wide.region_12.16_spmd.sunk | while | flops 1034713664 | bytes 145711024 | solution.py:202
  359.7 48.1 %while.58 = (s32[]{:T(128)}, f32[1024,3,64]{0,2,1:T(8,128)S(1)}, f32[1024,3,64]{0,2,1:T(8,128)}, f32[2,512,3,64]{1,0,3,2:T(2,128)}, bf16[2,512,3,64]{1,3,2,0:T(8...) while((s32[]{:T(128)}, f32[1024,3,64]{0,2,1:T(8,128)S(1)}, ...), condition=%wide.region_15.15_spmd.clone, body=%wide.region_13.14_spmd.clone.sunk | while | flops 1031305728 | bytes 117228824 | solution.py:111
  420.0 48.1 %while.58 = (s32[]{:T(128)}, f32[1024,3,64]{0,2,1:T(8,128)S(1)}, f32[1024,3,64]{0,2,1:T(8,128)}, f32[2,512,3,64]{1,0,3,2:T(2,128)}, bf16[2,512,3,64]{1,3,2,0:T(8...) while((s32[]{:T(128)}, f32[1024,3,64]{0,2,1:T(8,128)S(1)}, ...), condition=%wide.region_15.15_spmd.clone, body=%wide.region_13.14_spmd.clone.sunk | while | flops 1031305728 | bytes 117228824 | solution.py:111
  480.2 48.1 %while.58 = (s32[]{:T(128)}, f32[1024,3,64]{0,2,1:T(8,128)S(1)}, f32[1024,3,64]{0,2,1:T(8,128)}, f32[2,512,3,64]{1,0,3,2:T(2,128)}, bf16[2,512,3,64]{1,3,2,0:T(8...) while((s32[]{:T(128)}, f32[1024,3,64]{0,2,1:T(8,128)S(1)}, ...), condition=%wide.region_15.15_spmd.clone, body=%wide.region_13.14_spmd.clone.sunk | while | flops 1031305728 | bytes 117228824 | solution.py:111
  546.2 43.7 %all-to-all-done.7 = bf16[3,1024,192]{2,0,1:T(4,128)(2,1)} async-done(((bf16[3,1024,192]{2,0,1:T(4,128)(2,1)}), bf16[3,1024,192]{2,0,1:T(4,128)(2,1)}, u32[]{:S(2)}, u32[]{:S(2)}) %all-to-all-start.7) | async-done | bytes 1179680 | tf_op jit(solution)/shard_map/all_to_all | solution.py:209
  594.6 10.9 convolution_bitcast_fusion
  605.5 11.0 multiply_convert_fusion.1
  619.0 23.2 %all-to-all-done.5 = bf16[3,1024,192]{2,0,1:T(4,128)(2,1)} async-done(((bf16[3,1024,192]{2,0,1:T(4,128)(2,1)}), bf16[3,1024,192]{2,0,1:T(4,128)(2,1)}, u32[]{:S(2)}, u32[]{:S(2)}) %all-to-all-start.5) | async-done | bytes 1179680 | tf_op jit(solution)/shard_map/all_to_all | solution.py:207
  732.2 436.6 %all-reduce.10.cloned.1.call-done = (f32[589824]{0:T(1024)}, f32[589824]{0:T(1024)}, f32[589824]{0:T(1024)}, f32[589824]{0:T(1024)}, f32[2359296]{0:T(1024)}, /*index=5*/f32[2359296]{0:T(1024)}) async-done(((f32[589824]{0:T(1024)}, f32[589824]{0:T(1024)}, f32[589824]{0:T(1024)}, f32[589824]{0:T(1024)}, f32[2359296]{0:T(1024)}, /*index=5*/f32[2359296]{0:T(1024)}), (f32[589824]{0:T(1024)}, f32[589824]{0:T(1024)}, ...) | async-done | bytes 28311568
  1199.9 41.9 %all-reduce.6 = (f32[768]{0:T(1024)}, f32[768]{0:T(1024)}, f32[768]{0:T(1024)}, f32[768]{0:T(1024)}, f32[768]{0:T(1024)}, /*index=5*/f32[768]{0:T(1024)}, f32[76...) all-reduce(f32[768]{0:T(1024)S(1)} %get-tuple-element.328, ...), channel_id=1, replica_groups=mesh['dp'=8,'seq'=4] {'dp','seq'}, use_global_device_ids=true, to_apply=%region_20.21 | all-reduce | flops 10054 | bytes 80432 | tf_op jit(solution)/shard_map/psum | solution.py:245
  1249.9 38.9 %all-gather.9.cloned.1.call-done = f32[589824]{0:T(1024)} async-done(((f32[18432]{0:T(1024)}), f32[589824]{0:T(1024)}) %all-gather.9.cloned.1.call-update) | async-done | bytes 2359312 | tf_op jit(solution)/shard_map/all_gather | solution.py:277
  1292.1 55.6 %all-gather.11.cloned.1.call-done = f32[589824]{0:T(1024)} async-done(((f32[18432]{0:T(1024)}), f32[589824]{0:T(1024)}) %all-gather.11.cloned.1.call-update) | async-done | bytes 2359312 | tf_op jit(solution)/shard_map/all_gather | solution.py:278
  1351.0 55.6 %all-gather.13.cloned.1.call-done = f32[589824]{0:T(1024)} async-done(((f32[18432]{0:T(1024)}), f32[589824]{0:T(1024)}) %all-gather.13.cloned.1.call-update) | async-done | bytes 2359312 | tf_op jit(solution)/shard_map/all_gather | solution.py:279
  1409.9 80.8 %all-gather.15.cloned.1.call-done = f32[2359296]{0:T(1024)} async-done(((f32[73728]{0:T(1024)}), f32[2359296]{0:T(1024)}) %all-gather.15.cloned.1.call-update) | async-done | bytes 9437200 | tf_op jit(solution)/shard_map/all_gather | solution.py:280
  1490.8 10.9 reshape.501
  1501.7 72.6 %all-gather.17.cloned.1.call-done = f32[2359296]{0:T(1024)} async-done(((f32[73728]{0:T(1024)}), f32[2359296]{0:T(1024)}) %all-gather.17.cloned.1.call-update) | async-done | bytes 9437200 | tf_op jit(solution)/shard_map/all_gather | solution.py:281
  1574.2 11.3 reshape.503
  (542 shorter events, 509.1 us)
Async XLA Ops:
  7.2 56.4 %copy-start = (bf16[768,768]{1,0:T(8,128)(2,1)S(1)}, bf16[768,768]{1,0:T(8,128)(2,1)}, u32[]{:S(2)}) copy-start(bf16[768,768]{1,0:T(8,128)(2,1)} %param.38) | copy-start | bytes 3538948
  15.9 43.3 %all-to-all-start.1 = ((bf16[3,256,768]{1,0,2:T(4,128)(2,1)}), bf16[3,256,768]{1,0,2:T(4,128)(2,1)S(1)}, u32[]{:S(2)}, u32[]{:S(2)}) async-start(bf16[3,256,768]{1,0,2:T(4,128)(2,1)} %copy.111), calls=%async_computation.1 | async-start | bytes 3145728 | tf_op jit(solution)/shard_map/all_to_all | solution.py:157
  59.2 40.9 %all-to-all-start = ((bf16[3,256,768]{1,0,2:T(4,128)(2,1)}), bf16[3,256,768]{1,0,2:T(4,128)(2,1)}, u32[]{:S(2)}, u32[]{:S(2)}) async-start(bf16[3,256,768]{1,0,2:T(4,128)(2,1)} %copy.108), calls=%async_computation | async-start | bytes 3145728 | tf_op jit(solution)/shard_map/all_to_all | solution.py:156
  100.1 41.1 %all-to-all-start.2 = ((bf16[3,256,768]{1,0,2:T(4,128)(2,1)}), bf16[3,256,768]{1,0,2:T(4,128)(2,1)}, u32[]{:S(2)}, u32[]{:S(2)}) async-start(bf16[3,256,768]{1,0,2:T(4,128)(2,1)} %copy.114), calls=%async_computation.2 | async-start | bytes 3145728 | tf_op jit(solution)/shard_map/all_to_all | solution.py:158
  197.3 55.5 %copy-start.7 = (bf16[3,1024,3,64]{1,3,2,0:T(8,128)(2,1)}, bf16[3,1024,3,64]{1,3,2,0:T(8,128)(2,1)S(1)}, u32[]{:S(2)}) copy-start(bf16[3,1024,3,64]{1,3,2,0:T(8,128)(2,1)S(1)} %get-tuple-element.910) | copy-start | bytes 3538948
  197.3 55.5 %copy-start.30 = (pred[3,1024]{1,0:T(4,128)(4,1)}, pred[3,1024]{1,0:T(4,128)(4,1)S(1)}, u32[]{:S(2)}) copy-start(pred[3,1024]{1,0:T(4,128)(4,1)S(1)} %get-tuple-element.943) | copy-start | bytes 9220
  261.5 40.5 %copy-start.8 = (f32[768,768]{1,0:T(8,128)}, f32[768,768]{1,0:T(8,128)S(1)}, u32[]{:S(2)}) copy-start(f32[768,768]{1,0:T(8,128)S(1)} %get-tuple-element.462) | copy-start | bytes 7077892
  261.6 40.4 %copy-start.35 = (f32[768]{0:T(1024)}, f32[768]{0:T(1024)S(1)}, u32[]{:S(2)}) copy-start(f32[768]{0:T(1024)S(1)} %broadcast_multiply_fusion) | copy-start | bytes 9220
  307.5 39.7 %all-to-all-start.4 = ((bf16[3,256,768]{1,0,2:T(4,128)(2,1)}), bf16[3,256,768]{1,0,2:T(4,128)(2,1)S(1)}, u32[]{:S(2)}, u32[]{:S(2)}) async-start(bf16[3,256,768]{1,0,2:T(4,128)(2,1)} %copy.119), calls=%async_computation.4 | async-start | bytes 3145728 | tf_op jit(solution)/shard_map/all_to_all | solution.py:199
  537.5 52.3 %all-to-all-start.7 = ((bf16[3,1024,192]{2,0,1:T(4,128)(2,1)}), bf16[3,1024,192]{2,0,1:T(4,128)(2,1)}, u32[]{:S(2)}, u32[]{:S(2)}) async-start(bf16[3,1024,192]{2,0,1:T(4,128)(2,1)} %copy.126), calls=%async_computation.7 | async-start | bytes 4194304 | tf_op jit(solution)/shard_map/all_to_all | solution.py:209
  546.2 48.4 %copy-start.36 = (f32[768]{0:T(1024)S(1)}, f32[768]{0:T(1024)}, u32[]{:S(2)}) copy-start(f32[768]{0:T(1024)} %copy-done.35) | copy-start | bytes 9220
  546.2 48.4 %copy-start.38 = (f32[768]{0:T(1024)S(1)}, f32[768]{0:T(1024)}, u32[]{:S(2)}) copy-start(f32[768]{0:T(1024)} %copy-done.37) | copy-start | bytes 9220
  546.2 48.4 %copy-start.40 = (f32[768]{0:T(1024)S(1)}, f32[768]{0:T(1024)}, u32[]{:S(2)}) copy-start(f32[768]{0:T(1024)} %param.42) | copy-start | bytes 9220
  546.2 48.4 %copy-start.42 = (f32[768]{0:T(1024)S(1)}, f32[768]{0:T(1024)}, u32[]{:S(2)}) copy-start(f32[768]{0:T(1024)} %param.43) | copy-start | bytes 9220
  589.8 52.4 %all-to-all-start.5 = ((bf16[3,1024,192]{2,0,1:T(4,128)(2,1)}), bf16[3,1024,192]{2,0,1:T(4,128)(2,1)}, u32[]{:S(2)}, u32[]{:S(2)}) async-start(bf16[3,1024,192]{2,0,1:T(4,128)(2,1)} %copy.122), calls=%async_computation.5 | async-start | bytes 4194304 | tf_op jit(solution)/shard_map/all_to_all | solution.py:207
  642.3 58.6 %all-to-all-start.6 = ((bf16[3,1024,192]{2,0,1:T(4,128)(2,1)}), bf16[3,1024,192]{2,0,1:T(4,128)(2,1)}, u32[]{:S(2)}, u32[]{:S(2)}) async-start(bf16[3,1024,192]{2,0,1:T(4,128)(2,1)} %copy.124), calls=%async_computation.6 | async-start | bytes 4194304 | tf_op jit(solution)/shard_map/all_to_all | solution.py:208
  646.7 522.0 %all-reduce.10.cloned.1.call-start = ((), (), s32[]{:S(2)}) async-start(), calls=%async_computation.14 | async-start | bytes 56623104
  732.1 447.3 %copy-start.63 = (s32[3,256]{1,0:T(4,128)S(1)}, s32[3,256]{1,0:T(4,128)}, u32[]{:S(2)}) copy-start(s32[3,256]{1,0:T(4,128)} %param.31) | copy-start | bytes 9220
  732.1 514.4 %all-gather.7.cloned.1.call-start = ((), (), s32[]{:S(2)}) async-start(), calls=%async_computation.8 | async-start | bytes 2433024 | tf_op jit(solution)/shard_map/all_gather | solution.py:276
  1170.3 118.5 %all-gather.9.cloned.1.call-start = ((), (), s32[]{:S(2)}) async-start(), calls=%async_computation.9 | async-start | bytes 2433024 | tf_op jit(solution)/shard_map/all_gather | solution.py:277
  1171.9 175.8 %all-gather.11.cloned.1.call-start = ((), (), s32[]{:S(2)}) async-start(), calls=%async_computation.10 | async-start | bytes 2433024 | tf_op jit(solution)/shard_map/all_gather | solution.py:278
  1173.5 233.1 %all-gather.13.cloned.1.call-start = ((), (), s32[]{:S(2)}) async-start(), calls=%async_computation.11 | async-start | bytes 2433024 | tf_op jit(solution)/shard_map/all_gather | solution.py:279
  1175.1 315.7 %all-gather.15.cloned.1.call-start = ((), (), s32[]{:S(2)}) async-start(), calls=%async_computation.12 | async-start | bytes 9732096 | tf_op jit(solution)/shard_map/all_gather | solution.py:280
  1176.9 397.4 %all-gather.17.cloned.1.call-start = ((), (), s32[]{:S(2)}) async-start(), calls=%async_computation.13 | async-start | bytes 9732096 | tf_op jit(solution)/shard_map/all_gather | solution.py:281
  (110 other events, 565.9 us)
Sparse Core Ops, SparseCore 0:
  732.3 436.4 all-reduce.9
  1172.1 57.0 all-gather.6
  1232.6 56.1 all-gather.8
  1291.4 56.2 all-gather.10
  1350.3 56.2 all-gather.12
  1409.8 80.9 all-gather.14
  1493.6 80.6 all-gather.16
where the time goes:
time: 1600 us; the launch traced here: 1590 us
  waiting for transfers between devices  928 us (58%)
  local copies, waits for them, and re-layouts  257 us (16%)
  matrix products  188 us (12%)
  blocking collectives  93.2 us (6%)
  other arithmetic  77.4 us (5%)
  starting transfers between devices  33 us (2%)
    unnamed x8, waiting for transfers between devices  437 us
    all_gather x1, waiting for transfers between devices, on_device(): lax.all_gather(part_up, ('dp', 'seq'), axis=0, tiled=True)  80.8 us
    all_gather x1, waiting for transfers between devices, on_device(): lax.all_gather(part_down, ('dp', 'seq'), axis=0, tiled=True)  72.6 us
    all_gather x1, waiting for transfers between devices, on_device(): lax.all_gather(part_value, ('dp', 'seq'), axis=0, tiled=True)  55.6 us
    all_gather x1, waiting for transfers between devices, on_device(): lax.all_gather(part_out, ('dp', 'seq'), axis=0, tiled=True)  55.6 us
    all_to_all x1, blocking collectives, on_device(): lax.all_to_all(mixed, 'seq', split_axis=1, concat_axis=2, tiled=True)  51.3 us
    dynamic_update_slice x12, local copies, waits for them, and re-layouts, attend_backward(): lax.scan(visit, (start, start), (query_blocks, grad_blocks, logsum))  50.6 us
    all_to_all x1, waiting for transfers between devices, on_device(): lax.all_to_all(grad_value, 'seq', split_axis=1, concat_axis=2, tiled=True)  43.7 us
  transfers between devices with their start and end apart: 14, of which 12 were waited for; matrix products, arithmetic and copies ran while one was open for 10% of the time, Pallas kernels for 0%

commit v1 on v0

v1 whole, which is shorter than its diff:
```python
import functools

import jax
import jax.numpy as jnp
from jax import lax
from jax.experimental import pallas as pl
from jax.experimental.pallas import tpu as pltpu
from jax.sharding import PartitionSpec as P

HEAD = 64
CLASSES = 70
PAIR = 2 * HEAD
BLOCK = 256

epsilon = 1e-05
low = jnp.bfloat16
full = jnp.float32


def matmul(left, right):
    return lax.dot_general(
        left, right, (((1,), (0,)), ((), ())), preferred_element_type=full
    )


def matmul_left(left, right):
    return lax.dot_general(
        left, right, (((0,), (0,)), ((), ())), preferred_element_type=full
    )


def matmul_right(left, right):
    return lax.dot_general(
        left, right, (((1,), (1,)), ((), ())), preferred_element_type=full
    )


def whiten(value):
    centre = value - jnp.mean(value, axis=-1, keepdims=True)
    scale = lax.rsqrt(jnp.mean(centre * centre, axis=-1, keepdims=True) + epsilon)
    return centre * scale, scale


def whiten_back(grad, hat, scale):
    mean = jnp.mean(grad, axis=-1, keepdims=True)
    along = jnp.mean(grad * hat, axis=-1, keepdims=True)
    return scale * (grad - mean - hat * along)


def rotate(value, cosine, sine):
    lane = lax.broadcasted_iota(jnp.int32, value.shape, 1)
    ahead = pltpu.roll(value, PAIR - HEAD // 2, 1)
    behind = pltpu.roll(value, HEAD // 2, 1)
    swapped = jnp.where(lane % HEAD < HEAD // 2, ahead, behind)
    return value * cosine + swapped * sine


def call(kernel, grid, scalars, inputs, outputs, scratch=(), flops=0, special=0):
    moved = sum(array.size * array.dtype.itemsize for array, _ in inputs)
    moved += sum(shape.size * shape.dtype.itemsize for shape, _ in outputs)
    return pl.pallas_call(
        kernel,
        grid_spec=pltpu.PrefetchScalarGridSpec(
            num_scalar_prefetch=1,
            grid=grid,
            in_specs=[spec for _, spec in inputs],
            out_specs=[spec for _, spec in outputs],
            scratch_shapes=list(scratch),
        ),
        out_shape=[shape for shape, _ in outputs],
        compiler_params=pltpu.CompilerParams(
            dimension_semantics=("arbitrary",) * len(grid), vmem_limit_bytes=60 << 20
        ),
        cost_estimate=pl.CostEstimate(
            flops=int(flops), transcendentals=int(special), bytes_accessed=int(moved)
        ),
    )(scalars, *[array for array, _ in inputs])


def whole(array):
    rank = len(array.shape)
    return (array, pl.BlockSpec(array.shape, lambda *_: (0,) * rank))


def fresh(shape, kind):
    return jax.ShapeDtypeStruct(shape, kind)


def pack_kernel(order, first, second, to_first, to_second):
    to_first[...] = first[...]
    to_second[...] = second[...]


def pack(array, order):
    seqs, span, width = array.shape
    half = span // 2
    blocks = array.reshape(2 * seqs, half, width)
    shape = fresh((seqs * half, width), array.dtype)
    spot = pl.BlockSpec((half, width), lambda j, order: (j, 0))
    return call(
        pack_kernel,
        (seqs,),
        order,
        [
            (blocks, pl.BlockSpec((None, half, width), lambda j, order: (order[j], 0, 0))),
            (blocks, pl.BlockSpec((None, half, width), lambda j, order: (order[seqs + j], 0, 0))),
        ],
        [(shape, spot), (shape, spot)],
    )


def unpack_kernel(order, first, second, out):
    take = order[pl.program_id(0)] == 0

    @pl.when(take)
    def _():
        out[...] = first[...]

    @pl.when(jnp.logical_not(take))
    def _():
        out[...] = second[...]


def unpack(first, second, order, seqs):
    rows, width = first.shape
    half = rows // seqs
    spot = pl.BlockSpec((half, width), lambda i, order: (order[2 * seqs + i], 0))
    blocks = call(
        unpack_kernel,
        (2 * seqs,),
        order,
        [(first, spot), (second, spot)],
        [
            (
                fresh((2 * seqs, half, width), first.dtype),
                pl.BlockSpec((None, half, width), lambda i, order: (i, 0, 0)),
            )
        ],
    )[0]
    return blocks.reshape(seqs, 2 * half, width)


def join(first, second, span):
    return jnp.concatenate(
        [first[:span], second[:span], first[span:], second[span:]], axis=0
    )


def project_kernel(
    place, first, second, gain, shift, w_query, w_key, w_value, b_query, b_key, b_value,
    cosine, sine, query, both, shared, normed,
):
    width = first.shape[1]
    span = 2 * first.shape[0] // 3
    half = span // 2
    for slot, message in enumerate((first, second)):
        own = slice(slot * span, (slot + 1) * span)
        mixed = slice(2 * span + slot * half, 2 * span + (slot + 1) * half)
        hat, _ = whiten(message[...].astype(full))
        item = (hat * gain[...] + shift[...]).astype(low)
        normed[own, :] = item[:span]
        normed[mixed, :] = item[span:]
        at = pl.ds(pl.multiple_of(place[slot], half), span)
        at_mixed = pl.ds(pl.multiple_of(place[2 + slot], half), half)
        cos = jnp.concatenate([cosine[at, :], cosine[at_mixed, :]], axis=0)
        sin = jnp.concatenate([sine[at, :], sine[at_mixed, :]], axis=0)
        raw = (matmul(item, w_query[...]) + b_query[...]).astype(low).astype(full)
        for column in range(0, width, PAIR):
            spot = slice(column, column + PAIR)
            turned = rotate(raw[:, spot], cos, sin).astype(low) * low(HEAD**-0.5)
            query[own, spot] = turned[:span]
            query[mixed, spot] = turned[span:]
        raw = (matmul(item, w_key[...]) + b_key[...]).astype(low).astype(full)
        for column in range(0, width, PAIR):
            spot = slice(column, column + PAIR)
            turned = rotate(raw[:, spot], cos, sin).astype(low)
            both[0, own, spot] = turned[:span]
            both[0, mixed, spot] = turned[span:]
            shared[0, slot * half : (slot + 1) * half, spot] = turned[span:]
        raw = (matmul(item, w_value[...]) + b_value[...]).astype(low)
        both[1, own, :] = raw[:span]
        both[1, mixed, :] = raw[span:]
        shared[1, slot * half : (slot + 1) * half, :] = raw[span:]


def load_pieces(place, pieces, keys, values):
    for index, piece in enumerate(pieces):
        rows = piece.shape[1] // 2
        for slot in range(2):
            at = pl.ds(pl.multiple_of(place[1 + 2 * index + slot], rows), rows)
            keys[at, :] = piece[0, slot * rows : (slot + 1) * rows, :]
            values[at, :] = piece[1, slot * rows : (slot + 1) * rows, :]


def head_masks(value):
    lane = lax.broadcasted_iota(jnp.int32, value.shape, 1)
    wide = value.astype(full)
    return (
        jnp.where(lane < HEAD, wide, 0.0).astype(low),
        jnp.where(lane < HEAD, 0.0, wide).astype(low),
    )


def attend_kernel(count, place, query, *refs):
    pieces = refs[:count]
    out, logsum, keys, values = refs[count:]
    load_pieces(place, pieces, keys, values)
    length = place[0]
    masked = head_masks(query[...])
    rows = query.shape[0]

    def visit(block, state, left=None):
        at = pl.ds(pl.multiple_of(block * BLOCK, BLOCK), BLOCK)
        key = keys[at, :]
        value = values[at, :].T
        fresh_state = []
        for head in range(2):
            peak, total, mixed = state[3 * head : 3 * head + 3]
            scores = matmul_right(key, masked[head])
            if left is not None:
                index = lax.broadcasted_iota(jnp.int32, scores.shape, 0)
                scores = jnp.where(index < left, scores, -1e30)
            top = jnp.maximum(peak, jnp.max(scores, axis=0, keepdims=True))
            weights = jnp.exp(scores - top)
            fade = jnp.exp(peak - top)
            total = total * fade + jnp.sum(weights, axis=0, keepdims=True)
            mixed = mixed * fade + matmul(
                value[head * HEAD : (head + 1) * HEAD, :], weights.astype(low)
            )
            fresh_state += [top, total, mixed]
        return tuple(fresh_state)

    start = (
        jnp.full((1, rows), -1e30, full),
        jnp.zeros((1, rows), full),
        jnp.zeros((HEAD, rows), full),
    )
    number = length // BLOCK
    state = lax.fori_loop(0, number, visit, start + start)
    state = lax.cond(
        length % BLOCK > 0,
        lambda given: visit(number, given, length % BLOCK),
        lambda given: given,
        state,
    )
    out[...] = (
        jnp.concatenate([state[2] / state[1], state[5] / state[4]], axis=0).T.astype(low)
    )
    logsum[0:1, :] = state[0] + jnp.log(state[1])
    logsum[1:2, :] = state[3] + jnp.log(state[4])


def attend_back_kernel(count, kept, place, query, grad, mixed, logsum, cosine, sine, *refs):
    pieces = refs[:count]
    grad_query, *grad_pieces = refs[count : 1 + 2 * count]
    keys, values, grad_keys, grad_values, grad_turned = refs[1 + 2 * count :]
    load_pieces(place, pieces, keys, values)
    length = place[0]
    grad_low = grad[...]
    masked = head_masks(query[...])
    masked_grad = head_masks(grad_low)
    inner = (grad_low.astype(full) * mixed[...].astype(full)).T
    delta = [
        jnp.sum(inner[head * HEAD : (head + 1) * HEAD, :], axis=0, keepdims=True)
        for head in range(2)
    ]
    grad_turned[...] = jnp.zeros_like(grad_turned)

    def visit(block, left=None):
        at = pl.ds(pl.multiple_of(block * BLOCK, BLOCK), BLOCK)
        key = keys[at, :]
        value = values[at, :]
        turned = key.T
        grad_key = jnp.zeros((BLOCK, PAIR), full)
        grad_value = jnp.zeros((BLOCK, PAIR), full)
        for head in range(2):
            spot = slice(head * HEAD, (head + 1) * HEAD)
            scores = matmul_right(key, masked[head])
            weights = jnp.exp(scores - logsum[head : head + 1, :])
            if left is not None:
                index = lax.broadcasted_iota(jnp.int32, scores.shape, 0)
                weights = jnp.where(index < left, weights, 0.0)
            grad_weights = matmul_right(value, masked_grad[head])
            grad_scores = (weights * (grad_weights - delta[head])).astype(low)
            grad_value += matmul(weights.astype(low), masked_grad[head])
            grad_key += matmul(grad_scores, masked[head])
            grad_turned[spot, :] += matmul(turned[spot, :], grad_scores)
        grad_keys[at, :] = rotate(grad_key, cosine[at, :], -sine[at, :]).astype(low)
        grad_values[at, :] = grad_value.astype(low)

    def visit_whole(block, carry):
        visit(block)
        return carry

    def clear(block, carry):
        at = pl.ds(pl.multiple_of(block * BLOCK, BLOCK), BLOCK)
        grad_keys[at, :] = jnp.zeros((BLOCK, PAIR), low)
        grad_values[at, :] = jnp.zeros((BLOCK, PAIR), low)
        return carry

    number = length // BLOCK
    lax.fori_loop(0, number, visit_whole, 0)

    @pl.when(length % BLOCK > 0)
    def _():
        visit(number, length % BLOCK)

    lax.fori_loop(pl.cdiv(length, BLOCK), keys.shape[0] // BLOCK, clear, 0)
    rows = query.shape[0]
    step = rows // 2
    back = grad_turned[...].T * HEAD**-0.5
    for slot in range(2):
        at = pl.ds(pl.multiple_of(place[1 + 2 * count + slot], step), step)
        part = slice(slot * step, (slot + 1) * step)
        grad_query[part, :] = rotate(back[part], cosine[at, :], -sine[at, :]).astype(low)
    for index, piece in enumerate(grad_pieces):
        rows = piece.shape[1] // 2
        for slot in range(2):
            at = pl.ds(pl.multiple_of(place[1 + 2 * index + slot], rows), rows)
            piece[0, slot * rows : (slot + 1) * rows, :] = grad_keys[at, :]
            piece[1, slot * rows : (slot + 1) * rows, :] = grad_values[at, :]


def hidden_tile(normed, cot, w_up, b_up, w_down, result, grad_normed, hidden, grad_hidden):
    count = normed.shape[0]
    step = min(count, 256)
    total = jnp.zeros((1, w_up.shape[1]), full)
    for row in range(0, count, step):
        spot = slice(row, row + step)
        hidden_in = matmul(normed[spot, :], w_up[...]) + b_up[...]
        back = matmul_right(cot[spot, :], w_down[...])
        share = 0.5 * (1.0 + lax.erf(hidden_in * 0.5**0.5))
        item = (hidden_in * share).astype(low)
        slope = share + hidden_in * jnp.exp(-0.5 * hidden_in * hidden_in) * 0.3989422804014327
        grad_item = (back * slope).astype(low)
        hidden[spot, :] = item
        grad_hidden[spot, :] = grad_item
        total += jnp.sum(grad_item.astype(full), axis=0, keepdims=True)
        result[spot, :] += matmul(item, w_down[...])
        grad_normed[spot, :] += matmul_right(grad_item, w_up[...])
    return total


def forward_kernel(
    tiles, own, mixed, first, second, cot_first, cot_second, w_out, b_out, gain, shift,
    w_up, b_up, w_down, middle, result, grad_normed, normed, cot, sent, grad_b_up,
    hidden, grad_hidden,
):
    span = 2 * first.shape[0] // 3

    @pl.when(pl.program_id(0) == 0)
    def _():
        cot[...] = join(cot_first[...], cot_second[...], span)
        attended = jnp.concatenate([own[...], mixed[...]], axis=0)
        value = join(first[...], second[...], span).astype(full)
        value = value + matmul(attended, w_out[...]) + b_out[...]
        middle[...] = value
        hat, _ = whiten(value)
        normed[...] = (hat * gain[...] + shift[...]).astype(low)
        result[...] = jnp.zeros_like(result)
        grad_normed[...] = jnp.zeros_like(grad_normed)

    grad_b_up[0:1, :] = hidden_tile(
        normed, cot, w_up, b_up, w_down, result, grad_normed, hidden, grad_hidden
    )
    sent[0, ...] = matmul_left(hidden[...], cot[...]).astype(low)
    sent[1, ...] = matmul_left(normed[...], grad_hidden[...]).astype(low)


def backward_kernel(
    tiles, own, mixed, middle, result_in, grad_normed_in, normed, cot, w_out, gain, w_up, b_up,
    w_down, b_down, kept, grad_b_up, to_first, to_second, grad_middle, grad_own, grad_mixed,
    out_kept, out_sent, rows_out, result, grad_normed, hidden, grad_hidden, grad_out,
):
    span = 2 * to_first.shape[0] // 3
    half = span // 2

    @pl.when(pl.program_id(0) == 0)
    def _():
        result[...] = result_in[...]
        grad_normed[...] = grad_normed_in[...]

    grad_b_up[0:1, :] = hidden_tile(
        normed, cot, w_up, b_up, w_down, result, grad_normed, hidden, grad_hidden
    )
    kept[0, ...] = matmul_left(hidden[...], cot[...]).astype(low)
    kept[1, ...] = matmul_left(normed[...], grad_hidden[...]).astype(low)

    @pl.when(pl.program_id(0) == pl.num_programs(0) - 1)
    def _():
        value = middle[...]
        done = (value + result[...] + b_down[...]).astype(low)
        to_first[:span, :] = done[:span]
        to_second[:span, :] = done[span : 2 * span]
        to_first[span:, :] = done[2 * span : 2 * span + half]
        to_second[span:, :] = done[2 * span + half :]
        hat, scale = whiten(value)
        grad = grad_normed[...]
        cot_full = cot[...].astype(full)
        rows_out[0:1, :] = jnp.sum(cot_full, axis=0, keepdims=True)
        rows_out[2:3, :] = jnp.sum(grad * hat, axis=0, keepdims=True)
        rows_out[3:4, :] = jnp.sum(grad, axis=0, keepdims=True)
        total = cot_full + whiten_back(grad * gain[...], hat, scale)
        rows_out[1:2, :] = jnp.sum(total, axis=0, keepdims=True)
        rows_out[4:8, :] = jnp.zeros_like(rows_out[4:8, :])
        grad_middle[...] = total
        branch = total.astype(low)
        back = matmul_right(branch, w_out[...]).astype(low)
        grad_own[...] = back[: 2 * span]
        grad_mixed[...] = back[2 * span :]
        attended = jnp.concatenate([own[...], mixed[...]], axis=0)
        grad_out[...] = matmul_left(attended, branch).astype(low)
        size = out_kept.shape[0]
        core = tiles[2]
        out_kept[...] = grad_out[pl.ds(pl.multiple_of(core * size, size), size), :]
        out_sent[...] = grad_out[pl.ds(pl.multiple_of((1 - core) * size, size), size), :]


def weight_kernel(
    core, normed, query_own, query_mixed, own_kept, own_sent, mixed_kept, mixed_sent,
    kept, sent, both, rows_out, whole_grad,
):
    grad_query = jnp.concatenate([query_own[...], query_mixed[...]], axis=0)
    parts = [grad_query]
    for index in range(2):
        own = own_kept[index].astype(full) + own_sent[index].astype(full)
        mixed = mixed_kept[index].astype(full) + mixed_sent[index].astype(full)
        part = jnp.concatenate([own, mixed], axis=0).astype(low)
        both[index] = part
        parts.append(part)
    size = kept.shape[1]
    for index, part in enumerate(parts):
        rows_out[index : index + 1, :] = jnp.sum(part.astype(full), axis=0, keepdims=True)
        whole_grad[...] = matmul_left(normed[...], part).astype(low)
        kept[index] = whole_grad[pl.ds(pl.multiple_of(core[0] * size, size), size), :]
        sent[index] = whole_grad[pl.ds(pl.multiple_of((1 - core[0]) * size, size), size), :]
    rows_out[3:8, :] = jnp.zeros_like(rows_out[3:8, :])


def input_kernel(
    core, query_own, query_mixed, both, w_query, w_key, w_value, first, second, gain,
    grad_middle, to_first, to_second, rows_out,
):
    span = 2 * first.shape[0] // 3
    half = span // 2
    grad_query = jnp.concatenate([query_own[...], query_mixed[...]], axis=0)
    grad = (
        matmul_right(grad_query, w_query[...])
        + matmul_right(both[0], w_key[...])
        + matmul_right(both[1], w_value[...])
    )
    hat, scale = whiten(join(first[...], second[...], span).astype(full))
    rows_out[0:1, :] = jnp.sum(grad * hat, axis=0, keepdims=True)
    rows_out[1:2, :] = jnp.sum(grad, axis=0, keepdims=True)
    rows_out[2:8, :] = jnp.zeros_like(rows_out[2:8, :])
    done = (grad_middle[...] + whiten_back(grad * gain[...], hat, scale)).astype(low)
    to_first[:span, :] = done[:span]
    to_second[:span, :] = done[span : 2 * span]
    to_first[span:, :] = done[2 * span : 2 * span + half]
    to_second[span:, :] = done[2 * span + half :]


def expand_kernel(halves, order, *refs):
    sources = refs[:4]
    outs = refs[4:]
    index = pl.program_id(0)
    for place, out in enumerate(outs):
        core = index // halves
        half = index % halves if halves > 1 else place
        choice = 2 * (core ^ order[0]) + (half ^ order[1])
        for number, source in enumerate(sources):

            @pl.when(choice == number)
            def _(source=source, out=out):
                out[...] = source[...].astype(full)


def on_device(
    inputs, cotangent, lengths, predicted, norm1_gain, norm1_shift, w_query, b_query, w_key,
    b_key, w_value, b_value, w_out, b_out, norm2_gain, norm2_shift, w_up, b_up, w_down, b_down,
):
    seqs, span, width = inputs.shape
    half = span // 2
    tokens = seqs * span
    hidden_width = w_up.shape[1]
    groups = lax.axis_size("dp")
    assert seqs == 3 and lax.axis_size("seq") == 4 and hidden_width == 4 * width
    bits = [1 << place for place in range(1, groups.bit_length() - 1)]
    group = lax.axis_index("dp")
    depth = lax.axis_index("seq")
    core = group & 1
    side = depth & 1
    pair = depth >> 1
    count = 4 * span

    def flip(value, bit):
        return lax.ppermute(value, "dp", [(i, i ^ bit) for i in range(groups)])

    def flip_depth(value, bit):
        return lax.ppermute(value, "seq", [(i, i ^ bit) for i in range(4)])

    def route(turn):
        moves = []
        for at in range(groups):
            for z in range(4):
                to = (at & ~1) | (z & 1)
                to_z = 2 * (at & 1) + (turn ^ (z >> 1))
                moves.append((at * 4 + z, to * 4 + to_z))
        return moves

    def send(value, turn):
        return lax.ppermute(value, ("dp", "seq"), route(turn))

    def send_back(value, turn):
        return lax.ppermute(value, ("dp", "seq"), [(b, a) for a, b in route(turn)])

    def ranks(sizes):
        longest = jnp.argmax(sizes).astype(jnp.int32)
        return (
            jnp.where(longest == 0, 1, 0),
            jnp.where(longest == 2, 1, 2),
            longest,
        )

    low_own, high_own, mixed_at = ranks(lengths)
    near = jnp.where(pair == 0, low_own, high_own)
    other = jnp.where(pair == 0, high_own, low_own)
    index = jnp.arange(2 * seqs)
    turn = index // seqs
    spot = index % seqs
    chosen = jnp.where(turn == 0, near, other)
    order = jnp.where(spot < 2, 2 * chosen + spot, 2 * mixed_at + (turn ^ pair))
    first, second = pack(inputs, order)
    first, second = send(first, 0), send(second, 1)
    seq_at = index // 2
    part = index % 2
    from_turn = jnp.where(seq_at == mixed_at, part, (seq_at == high_own).astype(jnp.int32)) ^ pair
    from_row = jnp.where(seq_at == mixed_at, 2, part)
    order_back = jnp.concatenate([from_turn, from_row])

    sibling_lengths = flip(lengths, 1)
    sizes = jnp.where(core == pair, lengths, sibling_lengths)
    low_here, high_here, mixed_here = ranks(sizes)
    own_length = sizes[jnp.where(side == 0, low_here, high_here)]
    mixed_length = sizes[mixed_here]

    def starts(at_side, at_core):
        slots = jnp.arange(2)
        quarter = 2 * (slots ^ at_side) + at_core
        return quarter * span, quarter * span + at_side * half

    own_at, mixed_start = starts(side, core)
    own_sibling, mixed_sibling = starts(side, 1 - core)
    _, mixed_far = starts(1 - side, core)
    _, mixed_far_sibling = starts(1 - side, 1 - core)
    own_place = jnp.concatenate([own_length[None], own_at, own_sibling, own_at])
    mixed_place = jnp.concatenate(
        [mixed_length[None], mixed_start, mixed_sibling, mixed_far, mixed_far_sibling, mixed_start]
    )

    frequency = 10000.0 ** (-jnp.arange(HEAD // 2, dtype=full) / (HEAD // 2))
    angle = jnp.arange(count, dtype=full)[:, None] * frequency[None, :]
    cosine = jnp.tile(jnp.cos(angle), (1, 4))
    sine = jnp.sin(angle)
    sine = jnp.tile(jnp.concatenate([-sine, sine], axis=1), (1, 2))

    def row(vector):
        return vector.reshape(1, -1)

    gain1, shift1 = row(norm1_gain), row(norm1_shift)
    gain2, shift2 = row(norm2_gain), row(norm2_shift)

    query, both, shared, normed = call(
        project_kernel,
        (1,),
        jnp.concatenate([own_at, mixed_start]),
        [
            whole(item)
            for item in (
                first, second, gain1, shift1, w_query, w_key, w_value, row(b_query), row(b_key),
                row(b_value), cosine, sine,
            )
        ],
        [
            whole(fresh((tokens, width), low)),
            whole(fresh((2, tokens, width), low)),
            whole(fresh((2, span, width), low)),
            whole(fresh((tokens, width), low)),
        ],
        flops=6 * tokens * width * width,
    )
    both_sibling = flip(both, 1)
    shared_far = flip_depth(shared, 1)
    shared_far_sibling = flip(shared_far, 1)

    cot_in, _, _ = lax.optimization_barrier((cotangent, first, second))
    cot_first, cot_second = pack(cot_in, order)
    cot_first, cot_second = send(cot_first, 0), send(cot_second, 1)

    pairs = width // PAIR

    def columns(array, rows, at):
        if len(array.shape) == 2:
            return (array, pl.BlockSpec((rows, PAIR), lambda h, _: (at, h)))
        return (array, pl.BlockSpec((2, rows, PAIR), lambda h, _: (0, at, h)))

    own_pieces = [columns(both, 2 * span, 0), columns(both_sibling, 2 * span, 0)]
    mixed_pieces = [
        columns(both, span, 2),
        columns(both_sibling, span, 2),
        columns(shared_far, span, 0),
        columns(shared_far_sibling, span, 0),
    ]

    def attend(place, rows, at, pieces):
        return call(
            functools.partial(attend_kernel, len(pieces)),
            (pairs,),
            place,
            [columns(query, rows, at), *pieces],
            [
                columns(fresh((rows, width), low), rows, 0),
                (
                    fresh((pairs, 8, rows), full),
                    pl.BlockSpec((None, 8, rows), lambda h, _: (h, 0, 0)),
                ),
            ],
            [pltpu.VMEM((count, PAIR), low), pltpu.VMEM((count, PAIR), low)],
            flops=4 * rows * count * width,
            special=rows * count * width // HEAD,
        )

    own, own_logsum = attend(own_place, 2 * span, 0, own_pieces)
    mixed, mixed_logsum = attend(mixed_place, span, 2, mixed_pieces)

    tiles_sent = jnp.stack([2 * (1 - core), 2 * (1 - core) + 1, core])
    tiles_kept = jnp.stack([2 * core, 2 * core + 1, core])
    square = (width, width)

    def tiled():
        return [
            (w_up, pl.BlockSpec(square, lambda j, tiles: (0, tiles[j]))),
            (row(b_up), pl.BlockSpec((1, width), lambda j, tiles: (0, tiles[j]))),
            (w_down, pl.BlockSpec(square, lambda j, tiles: (tiles[j], 0))),
        ]

    def tile_outs():
        return [
            (
                fresh((2, 2, width, width), low),
                pl.BlockSpec((2, None, width, width), lambda j, tiles: (0, j, 0, 0)),
            ),
            (
                fresh((2, 8, width), full),
                pl.BlockSpec((None, 8, width), lambda j, tiles: (j, 0, 0)),
            ),
        ]

    tile_scratch = [pltpu.VMEM((tokens, width), low), pltpu.VMEM((tokens, width), low)]
    middle, result, grad_normed2, normed2, cot, up_sent, b_up_sent = call(
        forward_kernel,
        (2,),
        tiles_sent,
        [
            whole(item)
            for item in (
                own, mixed, first, second, cot_first, cot_second, w_out, row(b_out), gain2, shift2,
            )
        ]
        + tiled(),
        [
            whole(fresh((tokens, width), full)),
            whole(fresh((tokens, width), full)),
            whole(fresh((tokens, width), full)),
            whole(fresh((tokens, width), low)),
            whole(fresh((tokens, width), low)),
        ]
        + tile_outs(),
        tile_scratch,
        flops=26 * tokens * width * width,
        special=4 * tokens * width,
    )
    up_received = flip(up_sent, 1)
    (
        up_kept, b_up_kept, result_first, result_second, grad_middle, grad_own, grad_mixed,
        out_kept, out_sent, rows_middle,
    ) = call(
        backward_kernel,
        (2,),
        tiles_kept,
        [
            whole(item)
            for item in (
                own, mixed, middle, result, grad_normed2, normed2, cot, w_out, gain2,
            )
        ]
        + tiled()
        + [whole(row(b_down))],
        tile_outs()
        + [
            whole(fresh((tokens // 2, width), low)),
            whole(fresh((tokens // 2, width), low)),
            whole(fresh((tokens, width), full)),
            whole(fresh((2 * span, width), low)),
            whole(fresh((span, width), low)),
            whole(fresh((width // 2, width), low)),
            whole(fresh((width // 2, width), low)),
            whole(fresh((8, width), full)),
        ],
        [pltpu.VMEM((tokens, width), full), pltpu.VMEM((tokens, width), full)]
        + tile_scratch
        + [pltpu.VMEM(square, low)],
        flops=28 * tokens * width * width,
        special=4 * tokens * width,
    )
    out_received = flip(out_sent, 1)
    result = unpack(send_back(result_first, 0), send_back(result_second, 1), order_back, seqs)

    def bit_of(bit):
        return (group & bit) // bit

    def split(addends, at):
        rows = addends[0].shape[0] // 2

        def part(which):
            items = [
                lax.dynamic_slice_in_dim(item, which * rows, rows, 0).astype(full)
                for item in addends
            ]
            return sum(items[1:], items[0]).astype(low)

        return part(at), part(1 - at)

    def added(addends):
        return (addends[0].astype(full) + addends[1].astype(full)).astype(low)

    def ordered(at, mine, theirs):
        return jnp.where(
            at == 0,
            jnp.concatenate([mine, theirs], axis=0),
            jnp.concatenate([theirs, mine], axis=0),
        )

    def reduce(left, right):
        for near_bit, far_bit in zip(bits, bits[::-1]):
            keep, give = split(left, bit_of(near_bit))
            left = [keep, flip(give, near_bit)]
            keep, give = split(right, bit_of(far_bit))
            right = [keep, flip(give, far_bit)]
        left, right = added(left), added(right)
        keep = jnp.where(side == 0, left, right)
        give = jnp.where(side == 0, right, left)
        keep, give = split([keep, flip_depth(give, 1)], pair)
        return added([keep, flip_depth(give, 2)])

    def gather(piece):
        piece = ordered(pair, piece, flip_depth(piece, 2))
        far = flip_depth(piece, 1)
        left = jnp.where(side == 0, piece, far)
        right = jnp.where(side == 0, far, piece)
        for near_bit, far_bit in list(zip(bits, bits[::-1]))[:0:-1]:
            left = ordered(bit_of(near_bit), left, flip(left, near_bit))
            right = ordered(bit_of(far_bit), right, flip(right, far_bit))
        left = [left, flip(left, bits[0])]
        right = [right, flip(right, bits[-1])]
        left = left + [flip(item, 1) for item in left]
        right = right + [flip(item, 1) for item in right]
        return left, right

    def expand(sources, bit, halves, outs):
        rows, columns_in = sources[0].shape
        return call(
            functools.partial(expand_kernel, halves),
            (2 * halves,),
            jnp.stack([core, bit_of(bit)]),
            [whole(item) for item in sources],
            [
                (
                    fresh(shape, full),
                    pl.BlockSpec(
                        (rows, columns_in),
                        (lambda i, _: (i, 0)) if shape[1] == columns_in else (lambda i, _: (0, i)),
                    ),
                )
                for shape in outs
            ],
        )

    up_pieces = reduce(
        [item[0].reshape(2 * width, width) for item in (up_kept, up_received)],
        [item[1].reshape(2 * width, width) for item in (up_kept, up_received)],
    )
    down_left, up_right = gather(up_pieces)
    grad_w_down = expand(down_left, bits[0], 2, [(hidden_width, width)])[0]
    grad_w_up = expand(up_right, bits[-1], 2, [(width, hidden_width)])[0]

    def attend_back(place, rows, at, pieces, grad, out, logsum):
        return call(
            functools.partial(attend_back_kernel, len(pieces), rows // span),
            (pairs,),
            place,
            [
                columns(query, rows, at),
                columns(grad, rows, 0),
                columns(out, rows, 0),
                (logsum, pl.BlockSpec((None, 8, rows), lambda h, _: (h, 0, 0))),
                whole(cosine),
                whole(sine),
                *pieces,
            ],
            [columns(fresh((rows, width), low), rows, 0)]
            + [columns(fresh((2, rows, width), low), rows, 0) for _ in pieces],
            [
                pltpu.VMEM((count, PAIR), low),
                pltpu.VMEM((count, PAIR), low),
                pltpu.VMEM((count, PAIR), low),
                pltpu.VMEM((count, PAIR), low),
                pltpu.VMEM((PAIR, rows), full),
            ],
            flops=10 * rows * count * width,
            special=rows * count * width // HEAD,
        )

    query_mixed, mixed_here_grad, mixed_sibling_grad, far_grad, far_sibling_grad = attend_back(
        mixed_place, span, 2, mixed_pieces, grad_mixed, mixed, mixed_logsum
    )
    near_sum = added([mixed_here_grad, flip(mixed_sibling_grad, 1)])
    far_sum = added([far_grad, flip(far_sibling_grad, 1)])
    far_received = flip_depth(far_sum, 1)
    query_own, own_kept, own_sent = attend_back(
        own_place, 2 * span, 0, own_pieces, grad_own, own, own_logsum
    )
    own_received = flip(own_sent, 1)

    weight_kept, weight_sent, both_grad, rows_weight = call(
        weight_kernel,
        (1,),
        core[None],
        [
            whole(item)
            for item in (
                normed, query_own, query_mixed, own_kept, own_received, near_sum, far_received,
            )
        ],
        [
            whole(fresh((3, width // 2, width), low)),
            whole(fresh((3, width // 2, width), low)),
            whole(fresh((2, tokens, width), low)),
            whole(fresh((8, width), full)),
        ],
        [pltpu.VMEM(square, low)],
        flops=6 * tokens * width * width,
    )
    weight_received = flip(weight_sent, 1)
    back_first, back_second, rows_input = call(
        input_kernel,
        (1,),
        core[None],
        [
            whole(item)
            for item in (
                query_own, query_mixed, both_grad, w_query, w_key, w_value, first, second, gain1,
                grad_middle,
            )
        ],
        [
            whole(fresh((tokens // 2, width), low)),
            whole(fresh((tokens // 2, width), low)),
            whole(fresh((8, width), full)),
        ],
        flops=6 * tokens * width * width,
    )
    grad_inputs = unpack(send_back(back_first, 0), send_back(back_second, 1), order_back, seqs)

    left, right = gather(
        reduce(
            [item[0:2].reshape(width, width) for item in (weight_kept, weight_received)],
            [
                jnp.concatenate([item[2], extra], axis=0)
                for item, extra in ((weight_kept, out_kept), (weight_received, out_received))
            ],
        )
    )
    grad_w_query, grad_w_key = expand(left, bits[0], 1, [(width, width)] * 2)
    grad_w_value, grad_w_out = expand(right, bits[-1], 1, [(width, width)] * 2)

    live = (depth * span + jnp.arange(span))[None, :] < lengths[:, None]
    counts = jnp.sum(
        jnp.where(live[:, :, None] & (predicted[:, :, None] == jnp.arange(CLASSES)), 1.0, 0.0),
        axis=(0, 1),
    )
    counts = jnp.zeros((1, width), full).at[0, :CLASSES].set(counts)
    b_up_sent, b_up_kept = b_up_sent[:, 0], b_up_kept[:, 0]
    rows_up = jnp.where(
        core == 0,
        jnp.concatenate([b_up_kept, b_up_sent]),
        jnp.concatenate([b_up_sent, b_up_kept]),
    )
    small = jnp.concatenate(
        [rows_middle[:4], rows_up, rows_weight[:3], rows_input[:2], counts], axis=0
    )
    for bit in [1, *bits]:
        small = small + flip(small, bit)
    for bit in (1, 2):
        small = small + flip_depth(small, bit)

    return (
        result,
        grad_inputs,
        small[11],
        small[12],
        grad_w_query,
        small[8],
        grad_w_key,
        small[9],
        grad_w_value,
        small[10],
        grad_w_out,
        small[1],
        small[2],
        small[3],
        grad_w_up,
        small[4:8].reshape(-1),
        grad_w_down,
        small[0],
        small[13, :CLASSES].astype(jnp.int32),
    )


def solution(mesh):
    tokens = P("dp", "seq", None)
    return jax.shard_map(
        on_device,
        mesh=mesh,
        in_specs=(tokens, tokens, P("dp"), P("dp", "seq")) + (P(),) * 16,
        out_specs=(tokens, tokens) + (P(),) * 17,
        check_vma=False,
    )
```

time: 1600 us -> 503 us (0.31)
  waiting for transfers between devices: 928 us -> 174 us
  local copies, waits for them, and re-layouts: 257 us -> 27.1 us
  matrix products: 188 us -> 0 us
  Pallas kernels: 0 us -> 178 us
  blocking collectives: 93.2 us -> 0 us
  starting transfers between devices: 33 us -> 81 us
  other arithmetic: 77.4 us -> 29.7 us
    unnamed x8 -> x0, waiting for transfers between devices: 437 us -> none
    all_gather x6 -> x0, waiting for transfers between devices: 303 us -> none  [the longest x1 80.8 us: on_device(): lax.all_gather(part_up, ('dp', 'seq'), axis=0, tiled=True)]
    dot_general x60 -> x0, matrix products: 188 us -> none  [the longest x6 38.8 us: matmul_right(): lax.dot_general(left, right, (((1,), (1,)), ((), ())), preferred_element_...]
    all_to_all x7 -> x0, waiting for transfers between devices: 187 us -> none  [the longest x1 43.7 us: on_device(): lax.all_to_all(grad_value, 'seq', split_axis=1, concat_axis=2, tiled=True)]
    pallas_call x0 -> x17, Pallas kernels: none -> 178 us  [call(): pl.pallas_call(kernel, grid_spec=pltpu.PrefetchScalarGridSpec(num_scalar_...]
    ppermute x0 -> x56, waiting for transfers between devices: none -> 174 us  [the longest x12 74.4 us: flip_depth(): return lax.ppermute(value, 'seq', [(i, i ^ bit) for i in range(4)])]
    reshape x33 -> x10, local copies, waits for them, and re-layouts: 101 us -> 5.89 us  [the longest x9 5.28 us: row(): return vector.reshape(1, -1)]
    ppermute x0 -> x56, starting transfers between devices: none -> 81 us  [the longest x36 42.7 us: flip(): return lax.ppermute(value, 'dp', [(i, i ^ bit) for i in range(groups)])]
  transfers between devices with their start and end apart: 14 -> 56, of which waited for: 12 -> 20; matrix products, arithmetic and copies ran while one was open for 10% -> 10% of each run, Pallas kernels for 0% -> 28%
where the time goes in v1:
time: 503 us; the launch traced here: 497 us
  Pallas kernels  178 us (35%)
  waiting for transfers between devices  174 us (35%)
  starting transfers between devices  81 us (16%)
  other arithmetic  29.7 us (6%)
  local copies, waits for them, and re-layouts  27.1 us (5%)
  between operations  6.85 us (1%)
    pallas_call x17, Pallas kernels, call(): pl.pallas_call(kernel, grid_spec=pltpu.PrefetchScalarGridSpec(num_scalar_...  178 us
    ppermute x12, waiting for transfers between devices, flip_depth(): return lax.ppermute(value, 'seq', [(i, i ^ bit) for i in range(4)])  74.4 us
    ppermute x36, waiting for transfers between devices, flip(): return lax.ppermute(value, 'dp', [(i, i ^ bit) for i in range(groups)])  71.3 us
    ppermute x36, starting transfers between devices, flip(): return lax.ppermute(value, 'dp', [(i, i ^ bit) for i in range(groups)])  42.7 us
    ppermute x4, waiting for transfers between devices, send(): return lax.ppermute(value, ('dp', 'seq'), route(turn))  22.2 us
    ppermute x12, starting transfers between devices, flip_depth(): return lax.ppermute(value, 'seq', [(i, i ^ bit) for i in range(4)])  18.8 us
    ppermute x4, starting transfers between devices, send(): return lax.ppermute(value, ('dp', 'seq'), route(turn))  11.1 us
  transfers between devices with their start and end apart: 56, of which 20 were waited for; matrix products, arithmetic and copies ran while one was open for 10% of the time, Pallas kernels for 28%

profile of v1, /device:TPU:0, one launch (start us, length us, event | category | flops | bytes accessed | tf_op | source)
XLA Modules:
  0.0 496.6 jit_solution(653007516174224847)
XLA Ops:
  19.7 22.2 %collective-permute-done.2.second = bf16[384,768]{1,0:T(8,128)(2,1)S(1)} collective-permute-done((bf16[384,768]{1,0:T(8,128)(2,1)}, bf16[384,768]{1,0:T(8,128)(2,1)S(1)}, u32[]{:S(2)}, u32[]{:S(2)}) %collective-permute-start.2) | collective-permute-done | bytes 589856 | tf_op jit(solution)/shard_map/ppermute | solution.py:512
  42.7 8.4 %shard_map.340 = (bf16[768,768]{1,0:T(8,128)(2,1)}, bf16[2,768,768]{2,1,0:T(8,128)(2,1)}, bf16[2,256,768]{2,1,0:T(8,128)(2,1)}, bf16[768,768]{1,0:T(8,128)(2,1)}) custom-call(s32[4]{0:T(128)} %pad_add_fusion.2.place, bf16[384,768]{1,0:T(8,128)(2,1)} %copy-done.11, bf16[384,768]{1,0:T(8,128)(2,1)} %copy-done.12, f32[1,768]{1,0:T(1,128)} %reshape.197.gain, ...), custom_call_target="tpu_custom_call" | custom-call | flops 2717908992 | bytes 11287552 | tf_op jit(solution)/shard_map/pallas_call | solution.py:61
  51.6 19.6 %collective-permute-done.4.refs_2_ = bf16[2,256,768]{2,1,0:T(8,128)(2,1)S(1)} collective-permute-done((bf16[2,256,768]{2,1,0:T(8,128)(2,1)}, bf16[2,256,768]{2,1,0:T(8,128)(2,1)S(1)}, u32[]{:S(2)}, u32[]{:S(2)}) %collective-permute-start.4) | collective-permute-done | bytes 786464 | tf_op jit(solution)/shard_map/ppermute | solution.py:500
  92.1 21.1 %shard_map.342 = (bf16[256,768]{1,0:T(8,128)(2,1)}, f32[6,8,256]{2,1,0:T(8,128)}) custom-call(s32[11]{0:T(128)} %concatenate.72.place, bf16[768,768]{1,0:T(8,128)(2,1)} %get-tuple-element.86.query, bf16[2,768,768]{2,1,0:T(8,128)(2,1)} %get-tuple-element.87.refs_0_, bf16[2,768,768]{2,1,0:T(8,128)(2,1)} %copy-done, bf16[2,256,768]{2,1,0:T(8,128)(2,1)} %copy-done.5, ...), custom_call_target="tpu_custom_call" | custom-call | flops 805306368 | bytes 7913472 | tf_op jit(solution)/shard_map/pallas_call | solution.py:61
  113.2 9.0 %shard_map.341 = (bf16[512,768]{1,0:T(8,128)(2,1)}, f32[6,8,512]{2,1,0:T(8,128)}) custom-call(s32[7]{0:T(128)} %pad_add_fusion.1.place, bf16[768,768]{1,0:T(8,128)(2,1)} %get-tuple-element.86.query, bf16[2,768,768]{2,1,0:T(8,128)(2,1)} %get-tuple-element.87.refs_0_, bf16[2,768,768]{2,1,0:T(8,128)(2,1)} %copy-done), custom_call_target="tpu_custom_call" | custom-call | flops 1610612736 | bytes 6782976 | tf_op jit(solution)/shard_map/pallas_call | solution.py:61
  122.2 19.8 %shard_map.344 = (f32[768,768]{1,0:T(8,128)}, f32[768,768]{1,0:T(8,128)}, f32[768,768]{1,0:T(8,128)}, bf16[768,768]{1,0:T(8,128)(2,1)}, bf16[768,768]{1,0:T(8,12...) custom-call(s32[3]{0:T(128)} %get-tuple-element.174.tiles, ...), custom_call_target="tpu_custom_call" | custom-call | flops 11777605632 | bytes 28382208 | tf_op jit(solution)/shard_map/pallas_call | solution.py:61
  142.7 25.1 %shard_map.345 = (bf16[2,2,768,768]{3,2,1,0:T(8,128)(2,1)}, f32[2,8,768]{2,1,0:T(8,128)}, bf16[384,768]{1,0:T(8,128)(2,1)}, bf16[384,768]{1,0:T(8,128)(2,1)}, f3...) custom-call(s32[3]{0:T(128)} %get-tuple-element.173.tiles, ...), custom_call_target="tpu_custom_call" | custom-call | flops 12683575296 | bytes 31942656 | tf_op jit(solution)/shard_map/pallas_call | solution.py:61
  167.7 22.0 %shard_map.348 = (bf16[256,768]{1,0:T(8,128)(2,1)}, bf16[2,256,768]{2,1,0:T(8,128)(2,1)}, bf16[2,256,768]{2,1,0:T(8,128)(2,1)}, bf16[2,256,768]{2,1,0:T(8,128)(2,1)}, bf16[2,256,768]{2,1,0:T(8,128)(2,1)}) custom-call(s32[11]{0:T(128)} %concatenate.72.place, bf16[768,768]{1,0:T(8,128)(2,1)} %get-tuple-element.86.query, ...), custom_call_target="tpu_custom_call" | custom-call | flops 2013265920 | bytes 12894208 | tf_op jit(solution)/shard_map/pallas_call | solution.py:61
  190.3 13.2 %shard_map.347 = (bf16[512,768]{1,0:T(8,128)(2,1)}, bf16[2,512,768]{2,1,0:T(8,128)(2,1)}, bf16[2,512,768]{2,1,0:T(8,128)(2,1)}) custom-call(s32[7]{0:T(128)} %pad_add_fusion.1.place, bf16[768,768]{1,0:T(8,128)(2,1)} %get-tuple-element.86.query, bf16[512,768]{1,0:T(8,128)(2,1)} %get-tuple-element.101.grad, bf16[512,768]{1,0:T(8,128)(2,1)} %get-tuple-element.88.own.mixed, ...), custom_call_target="tpu_custom_call" | custom-call | flops 4026531840 | bytes 12550144 | tf_op jit(solution)/shard_map/pallas_call | solution.py:61
  210.6 13.4 %collective-permute-done.13.mixed_sent = bf16[2,256,768]{2,1,0:T(8,128)(2,1)} collective-permute-done((bf16[2,256,768]{2,1,0:T(8,128)(2,1)S(1)}, bf16[2,256,768]{2,1,0:T(8,128)(2,1)}, u32[]{:S(2)}, u32[]{:S(2)}) %collective-permute-start.13) | collective-permute-done | bytes 786464 | tf_op jit(solution)/shard_map/ppermute | solution.py:500
  224.0 8.7 %shard_map.349 = (bf16[3,384,768]{2,1,0:T(8,128)(2,1)}, bf16[3,384,768]{2,1,0:T(8,128)(2,1)}, bf16[2,768,768]{2,1,0:T(8,128)(2,1)}, f32[8,768]{1,0:T(8,128)}) custom-call(s32[1]{0:T(128)} %bitcast.2.core, bf16[768,768]{1,0:T(8,128)(2,1)} %get-tuple-element.107.normed, bf16[512,768]{1,0:T(8,128)(2,1)} %get-tuple-element.103.query_own, ...), custom_call_target="tpu_custom_call" | custom-call | flops 2717908992 | bytes 13000704 | tf_op jit(solution)/shard_map/pallas_call | solution.py:61
  237.5 12.3 %collective-permute-start.40 = (bf16[768,768]{1,0:T(8,128)(2,1)}, bf16[768,768]{1,0:T(8,128)(2,1)}, u32[]{:S(2)}, u32[]{:S(2)}) collective-permute-start(bf16[768,768]{1,0:T(8,128)(2,1)} %get-tuple-element.159), channel_id=1, source_target_pairs={{0,8},{4,12},{8,0},{12,4},{16,24},{20,28},{24,16},{28,20},{1,9},{5... | collective-permute-start | bytes 3538952 | tf_op jit(solution)/shard_map/ppermute | solution.py:497
  253.1 23.6 %collective-permute-done.40 = bf16[768,768]{1,0:T(8,128)(2,1)} collective-permute-done((bf16[768,768]{1,0:T(8,128)(2,1)}, bf16[768,768]{1,0:T(8,128)(2,1)}, u32[]{:S(2)}, u32[]{:S(2)}) %collective-permute-start.40) | collective-permute-done | bytes 1179680 | tf_op jit(solution)/shard_map/ppermute | solution.py:497
  300.8 8.0 %collective-permute-done.22 = bf16[384,768]{1,0:T(8,128)(2,1)S(1)} collective-permute-done((bf16[384,768]{1,0:T(8,128)(2,1)S(1)}, bf16[384,768]{1,0:T(8,128)(2,1)S(1)}, u32[]{:S(2)}, u32[]{:S(2)}) %collective-permute-start.22) | collective-permute-done | bytes 589856 | tf_op jit(solution)/shard_map/ppermute | solution.py:497
  317.8 8.2 %collective-permute-done.45 = bf16[192,768]{1,0:T(8,128)(2,1)S(1)} collective-permute-done((bf16[192,768]{1,0:T(8,128)(2,1)S(1)}, bf16[192,768]{1,0:T(8,128)(2,1)S(1)}, u32[]{:S(2)}, u32[]{:S(2)}) %collective-permute-start.45) | collective-permute-done | bytes 294944 | tf_op jit(solution)/shard_map/ppermute | solution.py:500
  329.8 14.2 %collective-permute-done.46 = bf16[192,768]{1,0:T(8,128)(2,1)S(1)} collective-permute-done((bf16[192,768]{1,0:T(8,128)(2,1)S(1)}, bf16[192,768]{1,0:T(8,128)(2,1)S(1)}, u32[]{:S(2)}, u32[]{:S(2)}) %collective-permute-start.46) | collective-permute-done | bytes 294944 | tf_op jit(solution)/shard_map/ppermute | solution.py:500
  347.3 9.0 %shard_map.350 = (bf16[384,768]{1,0:T(8,128)(2,1)}, bf16[384,768]{1,0:T(8,128)(2,1)}, f32[8,768]{1,0:T(8,128)}) custom-call(s32[1]{0:T(128)} %bitcast.2.core, bf16[512,768]{1,0:T(8,128)(2,1)} %get-tuple-element.103.query_own, bf16[256,768]{1,0:T(8,128)(2,1)} %get-tuple-element.106.query_mixed, bf16[2,768,768]{2,1,0:T(8,128)(2,1)} %get-tuple-element.114.both, ...), custom_call_target="tpu_custom_call" | custom-call | flops 2717908992 | bytes 11824128 | tf_op jit(solution)/shard_map/pallas_call | solution.py:61
  377.9 12.1 %collective-permute-done.19 = f32[14,768]{1,0:T(8,128)S(1)} collective-permute-done((f32[14,768]{1,0:T(8,128)S(1)}, f32[14,768]{1,0:T(8,128)S(1)}, u32[]{:S(2)}, u32[]{:S(2)}) %collective-permute-start.19) | collective-permute-done | bytes 43040 | tf_op jit(solution)/shard_map/ppermute | solution.py:500
  390.1 6.7 %collective-permute-done.31 = bf16[192,768]{1,0:T(8,128)(2,1)S(1)} collective-permute-done((bf16[192,768]{1,0:T(8,128)(2,1)S(1)}, bf16[192,768]{1,0:T(8,128)(2,1)S(1)}, u32[]{:S(2)}, u32[]{:S(2)}) %collective-permute-start.31) | collective-permute-done | bytes 294944 | tf_op jit(solution)/shard_map/ppermute | solution.py:497
  414.6 6.0 %collective-permute-done.15.second = bf16[384,768]{1,0:T(8,128)(2,1)S(1)} collective-permute-done((bf16[384,768]{1,0:T(8,128)(2,1)S(1)}, bf16[384,768]{1,0:T(8,128)(2,1)S(1)}, u32[]{:S(2)}, u32[]{:S(2)}) %collective-permute-start.15) | collective-permute-done | bytes 589856 | tf_op jit(solution)/shard_map/ppermute | solution.py:515
  422.3 12.0 %collective-permute-start.37 = (bf16[384,768]{1,0:T(8,128)(2,1)S(1)}, bf16[384,768]{1,0:T(8,128)(2,1)S(1)}, u32[]{:S(2)}, u32[]{:S(2)}) collective-permute-start(bf16[384,768]{1,0:T(8,128)(2,1)S(1)} %maximum_select_fusion.3.refs_0_), channel_id=1, source_target_pairs={{0,4},{4,0},{8,12},{12,8},{16,20},{20,16},{24,28},{28,24},{1,5},{5... | collective-permute-start | bytes 1769480 | tf_op jit(solution)/shard_map/ppermute | solution.py:497
  434.3 17.2 %collective-permute-done.36.refs_1_ = bf16[384,768]{1,0:T(8,128)(2,1)S(1)} collective-permute-done((bf16[384,768]{1,0:T(8,128)(2,1)S(1)}, bf16[384,768]{1,0:T(8,128)(2,1)S(1)}, u32[]{:S(2)}, u32[]{:S(2)}) %collective-permute-start.36) | collective-permute-done | bytes 589856 | tf_op jit(solution)/shard_map/ppermute | solution.py:497
  482.5 6.9 %shard_map.355 = f32[3072,768]{1,0:T(8,128)} custom-call(s32[2]{0:T(128)} %get-tuple-element.175.order, bf16[768,768]{1,0:T(8,128)(2,1)} %copy-done.2, bf16[768,768]{1,0:T(8,128)(2,1)} %collective-permute-done.53.refs_1_, bf16[768,768]{1,0:T(8,128)(2,1)} %collective-permute-done.54.refs_2_, bf16[768,768]{1,0:T(8,128)(2,1)} %collective-permute-done.55.refs_3_), custom_call_target="tpu_custom_call" | custom-call | bytes 14155776 | tf_op jit(solution)/shard_map/pallas_call | solution.py:61
  489.5 6.9 %shard_map.354 = f32[768,3072]{1,0:T(8,128)} custom-call(s32[2]{0:T(128)} %get-tuple-element.176.order, bf16[768,768]{1,0:T(8,128)(2,1)} %copy-done.3, bf16[768,768]{1,0:T(8,128)(2,1)} %collective-permute-done.49.refs_1_, bf16[768,768]{1,0:T(8,128)(2,1)} %collective-permute-done.50.refs_2_, bf16[768,768]{1,0:T(8,128)(2,1)} %collective-permute-done.51.refs_3_), custom_call_target="tpu_custom_call" | custom-call | bytes 14155776 | tf_op jit(solution)/shard_map/pallas_call | solution.py:61
  (268 shorter events, 164.2 us)
Async XLA Ops:
  10.2 31.7 %collective-permute-start.2 = (bf16[384,768]{1,0:T(8,128)(2,1)}, bf16[384,768]{1,0:T(8,128)(2,1)S(1)}, u32[]{:S(2)}, u32[]{:S(2)}) collective-permute-start(bf16[384,768]{1,0:T(8,128)(2,1)} %get-tuple-element.85), channel_id=1, source_target_pairs={{0,1},{1,5},{2,0},{3,4},{4,3},{5,7},{6,2},{7,6},{8,9},{9,13},{10,8... | collective-permute-start | bytes 1769480 | tf_op jit(solution)/shard_map/ppermute | solution.py:512
  51.1 39.6 %collective-permute-start.3 = (bf16[2,768,768]{2,1,0:T(8,128)(2,1)}, bf16[2,768,768]{2,1,0:T(8,128)(2,1)S(1)}, u32[]{:S(2)}, u32[]{:S(2)}) collective-permute-start(bf16[2,768,768]{2,1,0:T(8,128)(2,1)} %get-tuple-element.87.refs_0_), channel_id=1, source_target_pairs={{0,4},{4,0},{8,12},{12,8},{16,20},{20,16},{24,28},{28,24},{1,5},{5... | collective-permute-start | bytes 7077896 | tf_op jit(solution)/shard_map/ppermute | solution.py:497
  51.2 32.5 %collective-permute-start = (s32[3]{0:T(128)S(1)}, s32[3]{0:T(128)S(1)}, u32[]{:S(2)}, u32[]{:S(2)}) collective-permute-start(s32[3]{0:T(128)S(1)} %copy-done.35), channel_id=1, source_target_pairs={{0,4},{4,0},{8,12},{12,8},{16,20},{20,16},{24,28},{28,24},{1,5},{5... | collective-permute-start | bytes 44 | tf_op jit(solution)/shard_map/ppermute | solution.py:497
  77.6 44.6 %collective-permute-start.6 = (bf16[384,768]{1,0:T(8,128)(2,1)}, bf16[384,768]{1,0:T(8,128)(2,1)}, u32[]{:S(2)}, u32[]{:S(2)}) collective-permute-start(bf16[384,768]{1,0:T(8,128)(2,1)} %get-tuple-element.92), channel_id=1, source_target_pairs={{0,0},{1,4},{2,1},{3,5},{4,2},{5,6},{6,3},{7,7},{8,8},{9,12},{10,9... | collective-permute-start | bytes 1769480 | tf_op jit(solution)/shard_map/ppermute | solution.py:512
  83.5 38.7 %collective-permute-start.7 = (bf16[384,768]{1,0:T(8,128)(2,1)}, bf16[384,768]{1,0:T(8,128)(2,1)}, u32[]{:S(2)}, u32[]{:S(2)}) collective-permute-start(bf16[384,768]{1,0:T(8,128)(2,1)} %get-tuple-element.93), channel_id=1, source_target_pairs={{0,1},{1,5},{2,0},{3,4},{4,3},{5,7},{6,2},{7,6},{8,9},{9,13},{10,8... | collective-permute-start | bytes 1769480 | tf_op jit(solution)/shard_map/ppermute | solution.py:512
  142.0 90.7 %collective-permute-start.39 = (bf16[2,2,768,768]{3,2,1,0:T(8,128)(2,1)}, bf16[2,2,768,768]{3,2,1,0:T(8,128)(2,1)}, u32[]{:S(2)}, u32[]{:S(2)}) collective-permute-start(bf16[2,2,768,768]{3,2,1,0:T(8,128)(2,1)} %get-tuple-element.132), channel_id=1, source_target_pairs={{0,4},{4,0},{8,12},{12,8},{16,20},{20,16},{24,28},{28,24},{1,5},{5... | collective-permute-start | bytes 14155784 | tf_op jit(solution)/shard_map/ppermute | solution.py:497
  232.7 49.2 %collective-permute-start.21 = (bf16[3,384,768]{2,1,0:T(8,128)(2,1)}, bf16[3,384,768]{2,1,0:T(8,128)(2,1)}, u32[]{:S(2)}, u32[]{:S(2)}) collective-permute-start(bf16[3,384,768]{2,1,0:T(8,128)(2,1)} %get-tuple-element.124), channel_id=1, source_target_pairs={{0,4},{4,0},{8,12},{12,8},{16,20},{20,16},{24,28},{28,24},{1,5},{5... | collective-permute-start | bytes 5308424 | tf_op jit(solution)/shard_map/ppermute | solution.py:497
  237.5 39.2 %collective-permute-start.40 = (bf16[768,768]{1,0:T(8,128)(2,1)}, bf16[768,768]{1,0:T(8,128)(2,1)}, u32[]{:S(2)}, u32[]{:S(2)}) collective-permute-start(bf16[768,768]{1,0:T(8,128)(2,1)} %get-tuple-element.159), channel_id=1, source_target_pairs={{0,8},{4,12},{8,0},{12,4},{16,24},{20,28},{24,16},{28,20},{1,9},{5... | collective-permute-start | bytes 3538952 | tf_op jit(solution)/shard_map/ppermute | solution.py:497
  251.8 28.4 %collective-permute-start.42 = (bf16[768,768]{1,0:T(8,128)(2,1)}, bf16[768,768]{1,0:T(8,128)(2,1)}, u32[]{:S(2)}, u32[]{:S(2)}) collective-permute-start(bf16[768,768]{1,0:T(8,128)(2,1)} %get-tuple-element.153), channel_id=1, source_target_pairs={{0,16},{4,20},{8,24},{12,28},{16,0},{20,4},{24,8},{28,12},{1,17},{... | collective-permute-start | bytes 3538952 | tf_op jit(solution)/shard_map/ppermute | solution.py:497
  252.9 33.7 %collective-permute-start.24 = (bf16[384,768]{1,0:T(8,128)(2,1)}, bf16[384,768]{1,0:T(8,128)(2,1)S(1)}, u32[]{:S(2)}, u32[]{:S(2)}) collective-permute-start(bf16[384,768]{1,0:T(8,128)(2,1)} %get-tuple-element.126), channel_id=1, source_target_pairs={{0,4},{4,0},{8,12},{12,8},{16,20},{20,16},{24,28},{28,24},{1,5},{5... | collective-permute-start | bytes 1769480 | tf_op jit(solution)/shard_map/ppermute | solution.py:497
  283.6 25.2 %collective-permute-start.22 = (bf16[384,768]{1,0:T(8,128)(2,1)S(1)}, bf16[384,768]{1,0:T(8,128)(2,1)S(1)}, u32[]{:S(2)}, u32[]{:S(2)}) collective-permute-start(bf16[384,768]{1,0:T(8,128)(2,1)S(1)} %get-tuple-element.163), channel_id=1, source_target_pairs={{0,8},{4,12},{8,0},{12,4},{16,24},{20,28},{24,16},{28,20},{1,9},{5... | collective-permute-start | bytes 1769480 | tf_op jit(solution)/shard_map/ppermute | solution.py:497
  344.2 32.7 %collective-permute-start.47 = (bf16[384,768]{1,0:T(8,128)(2,1)S(1)}, bf16[384,768]{1,0:T(8,128)(2,1)S(1)}, u32[]{:S(2)}, u32[]{:S(2)}) collective-permute-start(bf16[384,768]{1,0:T(8,128)(2,1)S(1)} %maximum_select_fusion.4), channel_id=1, source_target_pairs={{0,1},{1,0},{2,3},{3,2},{4,5},{5,4},{6,7},{7,6},{8,9},{9,8},{10,11... | collective-permute-start | bytes 1769480 | tf_op jit(solution)/shard_map/ppermute | solution.py:500
  368.9 35.3 %collective-permute-start.8 = (bf16[384,768]{1,0:T(8,128)(2,1)}, bf16[384,768]{1,0:T(8,128)(2,1)}, u32[]{:S(2)}, u32[]{:S(2)}) collective-permute-start(bf16[384,768]{1,0:T(8,128)(2,1)} %get-tuple-element.99), channel_id=1, source_target_pairs={{0,0},{4,1},{1,2},{5,3},{2,4},{6,5},{3,6},{7,7},{8,8},{12,9},{9,10... | collective-permute-start | bytes 1769480 | tf_op jit(solution)/shard_map/ppermute | solution.py:515
  374.8 30.1 %collective-permute-start.9 = (bf16[384,768]{1,0:T(8,128)(2,1)}, bf16[384,768]{1,0:T(8,128)(2,1)}, u32[]{:S(2)}, u32[]{:S(2)}) collective-permute-start(bf16[384,768]{1,0:T(8,128)(2,1)} %get-tuple-element.100), channel_id=1, source_target_pairs={{1,0},{5,1},{0,2},{4,3},{3,4},{7,5},{2,6},{6,7},{9,8},{13,9},{8,10... | collective-permute-start | bytes 1769480 | tf_op jit(solution)/shard_map/ppermute | solution.py:515
  377.1 30.7 %collective-permute-start.48 = (bf16[384,768]{1,0:T(8,128)(2,1)S(1)}, bf16[384,768]{1,0:T(8,128)(2,1)}, u32[]{:S(2)}, u32[]{:S(2)}) collective-permute-start(bf16[384,768]{1,0:T(8,128)(2,1)S(1)} %get-tuple-element.165), channel_id=1, source_target_pairs={{0,8},{4,12},{8,0},{12,4},{16,24},{20,28},{24,16},{28,20},{1,9},{5... | collective-permute-start | bytes 1769480 | tf_op jit(solution)/shard_map/ppermute | solution.py:497
  407.8 44.3 %collective-permute-start.53 = (bf16[768,768]{1,0:T(8,128)(2,1)S(1)}, bf16[768,768]{1,0:T(8,128)(2,1)}, u32[]{:S(2)}, u32[]{:S(2)}) collective-permute-start(bf16[768,768]{1,0:T(8,128)(2,1)S(1)} %maximum_select_fusion.1.refs_0_), channel_id=1, source_target_pairs={{0,8},{4,12},{8,0},{12,4},{16,24},{20,28},{24,16},{28,20},{1,9},{5... | collective-permute-start | bytes 3538952 | tf_op jit(solution)/shard_map/ppermute | solution.py:497
  411.1 41.4 %collective-permute-start.49 = (bf16[768,768]{1,0:T(8,128)(2,1)S(1)}, bf16[768,768]{1,0:T(8,128)(2,1)}, u32[]{:S(2)}, u32[]{:S(2)}) collective-permute-start(bf16[768,768]{1,0:T(8,128)(2,1)S(1)} %maximum_select_fusion.refs_0_), channel_id=1, source_target_pairs={{0,16},{4,20},{8,24},{12,28},{16,0},{20,4},{24,8},{28,12},{1,17},{... | collective-permute-start | bytes 3538952 | tf_op jit(solution)/shard_map/ppermute | solution.py:497
  412.8 38.7 %collective-permute-start.36 = (bf16[384,768]{1,0:T(8,128)(2,1)S(1)}, bf16[384,768]{1,0:T(8,128)(2,1)S(1)}, u32[]{:S(2)}, u32[]{:S(2)}) collective-permute-start(bf16[384,768]{1,0:T(8,128)(2,1)S(1)} %maximum_select_fusion.3.refs_0_), channel_id=1, source_target_pairs={{0,16},{4,20},{8,24},{12,28},{16,0},{20,4},{24,8},{28,12},{1,17},{... | collective-permute-start | bytes 1769480 | tf_op jit(solution)/shard_map/ppermute | solution.py:497
  420.6 30.9 %collective-permute-start.32 = (bf16[384,768]{1,0:T(8,128)(2,1)S(1)}, bf16[384,768]{1,0:T(8,128)(2,1)}, u32[]{:S(2)}, u32[]{:S(2)}) collective-permute-start(bf16[384,768]{1,0:T(8,128)(2,1)S(1)} %maximum_select_fusion.2.refs_0_), channel_id=1, source_target_pairs={{0,8},{4,12},{8,0},{12,4},{16,24},{20,28},{24,16},{28,20},{1,9},{5... | collective-permute-start | bytes 1769480 | tf_op jit(solution)/shard_map/ppermute | solution.py:497
  422.3 29.8 %collective-permute-start.37 = (bf16[384,768]{1,0:T(8,128)(2,1)S(1)}, bf16[384,768]{1,0:T(8,128)(2,1)S(1)}, u32[]{:S(2)}, u32[]{:S(2)}) collective-permute-start(bf16[384,768]{1,0:T(8,128)(2,1)S(1)} %maximum_select_fusion.3.refs_0_), channel_id=1, source_target_pairs={{0,4},{4,0},{8,12},{12,8},{16,20},{20,16},{24,28},{28,24},{1,5},{5... | collective-permute-start | bytes 1769480 | tf_op jit(solution)/shard_map/ppermute | solution.py:497
  451.5 31.0 %collective-permute-start.54 = (bf16[768,768]{1,0:T(8,128)(2,1)S(1)}, bf16[768,768]{1,0:T(8,128)(2,1)}, u32[]{:S(2)}, u32[]{:S(2)}) collective-permute-start(bf16[768,768]{1,0:T(8,128)(2,1)S(1)} %maximum_select_fusion.1.refs_0_), channel_id=1, source_target_pairs={{0,4},{4,0},{8,12},{12,8},{16,20},{20,16},{24,28},{28,24},{1,5},{5... | collective-permute-start | bytes 3538952 | tf_op jit(solution)/shard_map/ppermute | solution.py:497
  452.0 30.5 %collective-permute-start.55 = (bf16[768,768]{1,0:T(8,128)(2,1)}, bf16[768,768]{1,0:T(8,128)(2,1)}, u32[]{:S(2)}, u32[]{:S(2)}) collective-permute-start(bf16[768,768]{1,0:T(8,128)(2,1)} %collective-permute-done.53.refs_1_), channel_id=1, source_target_pairs={{0,4},{4,0},{8,12},{12,8},{16,20},{20,16},{24,28},{28,24},{1,5},{5... | collective-permute-start | bytes 3538952 | tf_op jit(solution)/shard_map/ppermute | solution.py:497
  452.1 37.4 %collective-permute-start.50 = (bf16[768,768]{1,0:T(8,128)(2,1)S(1)}, bf16[768,768]{1,0:T(8,128)(2,1)}, u32[]{:S(2)}, u32[]{:S(2)}) collective-permute-start(bf16[768,768]{1,0:T(8,128)(2,1)S(1)} %maximum_select_fusion.refs_0_), channel_id=1, source_target_pairs={{0,4},{4,0},{8,12},{12,8},{16,20},{20,16},{24,28},{28,24},{1,5},{5... | collective-permute-start | bytes 3538952 | tf_op jit(solution)/shard_map/ppermute | solution.py:497
  452.9 36.5 %collective-permute-start.51 = (bf16[768,768]{1,0:T(8,128)(2,1)}, bf16[768,768]{1,0:T(8,128)(2,1)}, u32[]{:S(2)}, u32[]{:S(2)}) collective-permute-start(bf16[768,768]{1,0:T(8,128)(2,1)} %collective-permute-done.49.refs_1_), channel_id=1, source_target_pairs={{0,4},{4,0},{8,12},{12,8},{16,20},{20,16},{24,28},{28,24},{1,5},{5... | collective-permute-start | bytes 3538952 | tf_op jit(solution)/shard_map/ppermute | solution.py:497
  (70 other events, 1102.2 us)

commit v2 on v1

v2 whole, which is shorter than its diff:
```python
import functools

import jax
import jax.numpy as jnp
from jax import lax
from jax.experimental import pallas as pl
from jax.experimental.pallas import tpu as pltpu
from jax.sharding import PartitionSpec as P

HEAD = 64
CLASSES = 70
PAIR = 2 * HEAD
BLOCK = 256

epsilon = 1e-05
low = jnp.bfloat16
full = jnp.float32


def matmul(left, right):
    return lax.dot_general(
        left, right, (((1,), (0,)), ((), ())), preferred_element_type=full
    )


def matmul_left(left, right):
    return lax.dot_general(
        left, right, (((0,), (0,)), ((), ())), preferred_element_type=full
    )


def matmul_right(left, right):
    return lax.dot_general(
        left, right, (((1,), (1,)), ((), ())), preferred_element_type=full
    )


def whiten(value):
    centre = value - jnp.mean(value, axis=-1, keepdims=True)
    scale = lax.rsqrt(jnp.mean(centre * centre, axis=-1, keepdims=True) + epsilon)
    return centre * scale, scale


def whiten_back(grad, hat, scale):
    mean = jnp.mean(grad, axis=-1, keepdims=True)
    along = jnp.mean(grad * hat, axis=-1, keepdims=True)
    return scale * (grad - mean - hat * along)


def rotate(value, cosine, sine):
    lane = lax.broadcasted_iota(jnp.int32, value.shape, 1)
    ahead = pltpu.roll(value, PAIR - HEAD // 2, 1)
    behind = pltpu.roll(value, HEAD // 2, 1)
    swapped = jnp.where(lane % HEAD < HEAD // 2, ahead, behind)
    return value * cosine + swapped * sine


def call(kernel, grid, scalars, inputs, outputs, scratch=(), flops=0, special=0, room=60, aliases=None):
    moved = sum(array.size * array.dtype.itemsize for array, _ in inputs)
    moved += sum(shape.size * shape.dtype.itemsize for shape, _ in outputs)
    return pl.pallas_call(
        kernel,
        grid_spec=pltpu.PrefetchScalarGridSpec(
            num_scalar_prefetch=1,
            grid=grid,
            in_specs=[spec for _, spec in inputs],
            out_specs=[spec for _, spec in outputs],
            scratch_shapes=list(scratch),
        ),
        out_shape=[shape for shape, _ in outputs],
        input_output_aliases=aliases or {},
        compiler_params=pltpu.CompilerParams(
            dimension_semantics=("arbitrary",) * len(grid), vmem_limit_bytes=room << 20
        ),
        cost_estimate=pl.CostEstimate(
            flops=1, transcendentals=0, bytes_accessed=1
        ),
    )(scalars, *[array for array, _ in inputs])


def whole(array):
    rank = len(array.shape)
    return (array, pl.BlockSpec(array.shape, lambda *_: (0,) * rank))


def fresh(shape, kind):
    return jax.ShapeDtypeStruct(shape, kind)


def pack_kernel(order, blocks, first, second, sems):
    half = blocks.shape[1]
    copies = []
    for number, target in enumerate((first, second)):
        for place in range(target.shape[0] // half):
            at = 4 * number + place
            copies.append(
                pltpu.make_async_copy(
                    blocks.at[order[at]], target.at[pl.ds(place * half, half)], sems.at[at]
                )
            )
    for copy in copies:
        copy.start()
    for copy in copies:
        copy.wait()


def in_place(array):
    return (array, pl.BlockSpec(memory_space=pl.ANY))


def pack(array, order, parts):
    seqs, span, width = array.shape
    half = span // 2
    message = fresh((parts * half, width), array.dtype)
    return call(
        pack_kernel,
        (1,),
        order,
        [in_place(array.reshape(2 * seqs, half, width))],
        [whole(message), whole(message)],
        [pltpu.SemaphoreType.DMA((8,))],
        room=12,
    )


def unpack_kernel(order, first, second, out, sems):
    half = out.shape[1]
    number = out.shape[0]

    def copy(source, index):
        at = pl.ds(pl.multiple_of(order[number + index] * half, half), half)
        return pltpu.make_async_copy(source.at[at], out.at[index], sems.at[index])

    for index in range(number):

        @pl.when(order[index] == 0)
        def _(index=index):
            copy(first, index).start()

        @pl.when(order[index] != 0)
        def _(index=index):
            copy(second, index).start()

    for index in range(number):
        copy(first, index).wait()


def unpack(first, second, order, seqs):
    rows, width = first.shape
    half = rows // seqs
    blocks = call(
        unpack_kernel,
        (1,),
        order,
        [in_place(first), in_place(second)],
        [whole(fresh((2 * seqs, half, width), first.dtype))],
        [pltpu.SemaphoreType.DMA((2 * seqs,))],
        room=12,
    )[0]
    return blocks.reshape(seqs, 2 * half, width)


def join(first, second, span):
    half = span // 2
    return jnp.concatenate(
        [first[:span], second[:span], first[span : span + half], second[span : span + half]],
        axis=0,
    )


def turn_heads(raw, cos, sin):
    columns = range(0, raw.shape[1], PAIR)
    return [rotate(raw[:, at : at + PAIR], cos, sin).astype(low) for at in columns]


def project_kernel(
    place, first, second, gain, shift, w_query, w_key, w_value, b_query, b_key, b_value,
    cosine, sine, query, both, normed,
):
    span = first.shape[0] // 2
    half = span // 2
    for slot, message in enumerate((first, second)):
        rows = [
            slice(slot * span, (slot + 1) * span),
            slice(2 * span + slot * half, 2 * span + (slot + 1) * half),
            slice(3 * span + slot * half, 3 * span + (slot + 1) * half),
        ]
        parts = [slice(0, span), slice(span, span + half), slice(span + half, 2 * span)]
        hat, _ = whiten(message[...].astype(full))
        item = (hat * gain[...] + shift[...]).astype(low)
        starts = [(place[slot], span), (place[2 + slot], half), (place[4 + slot], half)]
        at = [pl.ds(pl.multiple_of(start, half), size) for start, size in starts]
        cos = jnp.concatenate([cosine[index, :] for index in at], axis=0)
        sin = jnp.concatenate([sine[index, :] for index in at], axis=0)
        for row, part in zip(rows, parts):
            normed[row, :] = item[part]
        raw = (matmul(item, w_key[...]) + b_key[...]).astype(low).astype(full)
        for index, turned in enumerate(turn_heads(raw, cos, sin)):
            spot = slice(index * PAIR, (index + 1) * PAIR)
            for row, part in zip(rows, parts):
                both[0, row, spot] = turned[part]
        raw = (matmul(item, w_value[...]) + b_value[...]).astype(low)
        for row, part in zip(rows, parts):
            both[1, row, :] = raw[part]
        near = span + half
        raw = (matmul(item[:near], w_query[...]) + b_query[...]).astype(low).astype(full)
        for index, turned in enumerate(turn_heads(raw, cos[:near], sin[:near])):
            spot = slice(index * PAIR, (index + 1) * PAIR)
            turned = turned * low(HEAD**-0.5)
            for row, part in zip(rows[:2], parts[:2]):
                query[row, spot] = turned[part]


def load_pieces(place, pieces, keys, values):
    for index, piece in enumerate(pieces):
        rows = piece.shape[1] // 2
        for slot in range(2):
            at = pl.ds(pl.multiple_of(place[1 + 2 * index + slot], rows), rows)
            keys[at, :] = piece[0, slot * rows : (slot + 1) * rows, :]
            values[at, :] = piece[1, slot * rows : (slot + 1) * rows, :]


def head_masks(value):
    lane = lax.broadcasted_iota(jnp.int32, value.shape, 1)
    wide = value.astype(full)
    return (
        jnp.where(lane < HEAD, wide, 0.0).astype(low),
        jnp.where(lane < HEAD, 0.0, wide).astype(low),
    )


def by_blocks(length, most, visit):
    number = pl.cdiv(length, BLOCK)
    for blocks in range(1, most + 1):

        @pl.when(number == blocks)
        def _(blocks=blocks):
            visit(blocks, length - (blocks - 1) * BLOCK)


def attend_kernel(count, place, query, *refs):
    pieces = refs[:count]
    out, logsum, keys, values = refs[count:]
    load_pieces(place, pieces, keys, values)
    pairs = [slice(at, at + PAIR) for at in range(0, query.shape[1], PAIR)]

    def visit(blocks, left):
        for pair, columns in enumerate(pairs):
            masked = head_masks(query[:, columns])
            value = values[: blocks * BLOCK, columns].T
            mixed = []
            for head in range(2):
                spot = slice(head * HEAD, (head + 1) * HEAD)
                scores = []
                for block in range(blocks):
                    key = keys[block * BLOCK : (block + 1) * BLOCK, columns]
                    item = matmul_right(key, masked[head])
                    if block == blocks - 1:
                        index = lax.broadcasted_iota(jnp.int32, item.shape, 0)
                        item = jnp.where(index < left, item, -1e30)
                    scores.append(item)
                peaks = [jnp.max(item, axis=0, keepdims=True) for item in scores]
                peak = functools.reduce(jnp.maximum, peaks)
                weights = [jnp.exp(item - peak) for item in scores]
                total = sum(jnp.sum(item, axis=0, keepdims=True) for item in weights)
                product = sum(
                    matmul(value[spot, block * BLOCK : (block + 1) * BLOCK], item.astype(low))
                    for block, item in enumerate(weights)
                )
                mixed.append(product / total)
                logsum[pair, head : head + 1, :] = peak + jnp.log(total)
            out[:, columns] = jnp.concatenate(mixed, axis=0).T.astype(low)

    by_blocks(place[0], keys.shape[0] // BLOCK, visit)


def attend_back_kernel(count, place, query, grad, mixed, logsum, cosine, sine, *refs):
    pieces = refs[:count]
    grad_query, *grad_pieces = refs[count : 1 + 2 * count]
    keys, values, grad_keys, grad_values = refs[1 + 2 * count :]
    load_pieces(place, pieces, keys, values)
    rows = query.shape[0]
    step = rows // 2
    pairs = [slice(at, at + PAIR) for at in range(0, query.shape[1], PAIR)]

    def visit(blocks, left):
        for pair, columns in enumerate(pairs):
            grad_low = grad[:, columns]
            masked = head_masks(query[:, columns])
            masked_grad = head_masks(grad_low)
            inner = (grad_low.astype(full) * mixed[:, columns].astype(full)).T
            delta = [
                jnp.sum(inner[head * HEAD : (head + 1) * HEAD, :], axis=0, keepdims=True)
                for head in range(2)
            ]
            turned = [0.0, 0.0]
            for block in range(blocks):
                at = slice(block * BLOCK, (block + 1) * BLOCK)
                key = keys[at, columns]
                value = values[at, columns]
                flat = key.T
                grad_key = 0.0
                grad_value = 0.0
                for head in range(2):
                    scores = matmul_right(key, masked[head])
                    weights = jnp.exp(scores - logsum[pair, head : head + 1, :])
                    if block == blocks - 1:
                        index = lax.broadcasted_iota(jnp.int32, scores.shape, 0)
                        weights = jnp.where(index < left, weights, 0.0)
                    grad_weights = matmul_right(value, masked_grad[head])
                    grad_scores = (weights * (grad_weights - delta[head])).astype(low)
                    grad_value += matmul(weights.astype(low), masked_grad[head])
                    grad_key += matmul(grad_scores, masked[head])
                    turned[head] += matmul(flat[head * HEAD : (head + 1) * HEAD, :], grad_scores)
                grad_keys[at, columns] = rotate(
                    grad_key, cosine[at, :], -sine[at, :]
                ).astype(low)
                grad_values[at, columns] = grad_value.astype(low)
            back = jnp.concatenate(turned, axis=0).T * HEAD**-0.5
            for slot in range(2):
                at = pl.ds(pl.multiple_of(place[1 + 2 * count + slot], step), step)
                part = slice(slot * step, (slot + 1) * step)
                grad_query[part, columns] = rotate(
                    back[part], cosine[at, :], -sine[at, :]
                ).astype(low)
        for block in range(blocks, keys.shape[0] // BLOCK):
            at = slice(block * BLOCK, (block + 1) * BLOCK)
            grad_keys[at, :] = jnp.zeros_like(grad_keys[at, :])
            grad_values[at, :] = jnp.zeros_like(grad_values[at, :])

    by_blocks(place[0], keys.shape[0] // BLOCK, visit)
    for index, piece in enumerate(grad_pieces):
        rows = piece.shape[1] // 2
        for slot in range(2):
            at = pl.ds(pl.multiple_of(place[1 + 2 * index + slot], rows), rows)
            piece[0, slot * rows : (slot + 1) * rows, :] = grad_keys[at, :]
            piece[1, slot * rows : (slot + 1) * rows, :] = grad_values[at, :]


def put_messages(to_first, to_second, value):
    span = 2 * to_first.shape[0] // 3
    half = span // 2
    to_first[:span, :] = value[:span]
    to_second[:span, :] = value[span : 2 * span]
    to_first[span:, :] = value[2 * span : 2 * span + half]
    to_second[span:, :] = value[2 * span + half :]


def forward_kernel(
    order, own, mixed, first, second, w_out, b_out, gain, shift, w_up, b_up, w_down, b_down,
    middle, normed, hidden, slope, to_first, to_second, result,
):
    span = first.shape[0] // 2
    count = middle.shape[0]

    @pl.when(pl.program_id(0) == 0)
    def _():
        attended = jnp.concatenate([own[...], mixed[...]], axis=0)
        value = join(first[...], second[...], span).astype(full)
        value = value + matmul(attended, w_out[...]) + b_out[...]
        middle[...] = value
        result[...] = value + b_down[...]
        hat, _ = whiten(value)
        normed[...] = (hat * gain[...] + shift[...]).astype(low)

    for row in range(0, count, span):
        spot = slice(row, row + span)
        hidden_in = matmul(normed[spot, :], w_up[...]) + b_up[...]
        share = 0.5 * (1.0 + lax.erf(hidden_in * 0.5**0.5))
        item = (hidden_in * share).astype(low)
        hidden[spot, :] = item
        slope[spot, :] = (
            share + hidden_in * jnp.exp(-0.5 * hidden_in * hidden_in) * 0.3989422804014327
        )
        result[spot, :] += matmul(item, w_down[...])

    @pl.when(pl.program_id(0) == pl.num_programs(0) - 1)
    def _():
        put_messages(to_first, to_second, result[...].astype(low))


def backward_tile(hidden, slope, cot, normed, w_up, w_down, grad_normed, grad_hidden, target):
    count = cot.shape[0]
    step = min(count, 256)
    total = jnp.zeros((1, w_up.shape[1]), full)
    target[0] = matmul_left(hidden[...], cot[...]).astype(low)
    for row in range(0, count, step):
        spot = slice(row, row + step)
        item = (matmul_right(cot[spot, :], w_down[...]) * slope[spot, :]).astype(low)
        grad_hidden[spot, :] = item
        total += jnp.sum(item.astype(full), axis=0, keepdims=True)
        grad_normed[spot, :] += matmul_right(item, w_up[...])
    target[1] = matmul_left(normed[: cot.shape[0], :], grad_hidden[...]).astype(low)
    return total


def backward_first_kernel(
    tiles, hidden, slope, cot_first, cot_second, normed, w_up, w_down,
    sent, grad_b_up, grad_normed, cot, grad_hidden,
):
    @pl.when(pl.program_id(0) == 0)
    def _():
        span = 2 * cot_first.shape[0] // 3
        cot[...] = join(cot_first[...], cot_second[...], span)
        grad_normed[...] = jnp.zeros_like(grad_normed)

    grad_b_up[0:1, :] = backward_tile(
        hidden, slope, cot, normed, w_up, w_down, grad_normed, grad_hidden, sent
    )


def backward_last_kernel(
    tiles, hidden, slope, cot, normed, w_up, w_down, grad_normed_in, own, mixed, middle, w_out,
    gain, kept, grad_b_up, grad_middle, grad_own, grad_mixed, out_kept, out_sent, rows_out,
    grad_normed, grad_hidden, grad_out,
):
    @pl.when(pl.program_id(0) == 0)
    def _():
        grad_normed[...] = grad_normed_in[...]

    grad_b_up[0:1, :] = backward_tile(
        hidden, slope, cot, normed, w_up, w_down, grad_normed, grad_hidden, kept
    )

    @pl.when(pl.program_id(0) == pl.num_programs(0) - 1)
    def _():
        hat, scale = whiten(middle[...])
        grad = grad_normed[...]
        cot_full = cot[...].astype(full)
        rows_out[0:1, :] = jnp.sum(cot_full, axis=0, keepdims=True)
        rows_out[2:3, :] = jnp.sum(grad * hat, axis=0, keepdims=True)
        rows_out[3:4, :] = jnp.sum(grad, axis=0, keepdims=True)
        total = cot_full + whiten_back(grad * gain[...], hat, scale)
        rows_out[1:2, :] = jnp.sum(total, axis=0, keepdims=True)
        rows_out[4:8, :] = jnp.zeros_like(rows_out[4:8, :])
        grad_middle[...] = total
        branch = total.astype(low)
        back = matmul_right(branch, w_out[...]).astype(low)
        grad_own[...] = back[: own.shape[0]]
        grad_mixed[...] = back[own.shape[0] :]
        attended = jnp.concatenate([own[...], mixed[...]], axis=0)
        grad_out[...] = matmul_left(attended, branch).astype(low)
        keep_core_half(tiles[2], grad_out, out_kept, out_sent)


def keep_core_half(core, source, kept, sent):
    size = source.shape[0] // 2
    mine = source[pl.ds(pl.multiple_of(core * size, size), size), :]
    theirs = source[pl.ds(pl.multiple_of((1 - core) * size, size), size), :]
    columns = kept.shape[-1]
    for index in range(kept.shape[0]):
        spot = slice(index * columns, (index + 1) * columns)
        kept[index] = mine[:, spot]
        sent[index] = theirs[:, spot]


def halve_kernel(order, kept, received, keep_left, give_left, keep_right, give_right):
    for index, (keep, give) in enumerate(((keep_left, give_left), (keep_right, give_right))):
        for target, half in ((keep, order[1 + index]), (give, 1 - order[1 + index])):
            total = kept[index, half].astype(full) + received[index, half].astype(full)
            target[0] = total.astype(low)


def quarter_kernel(order, kept, received, out_kept, out_received, *targets):
    rows = targets[0].shape[1]
    for index in range(2):
        for target, half in (
            (targets[2 * index], order[1 + index]),
            (targets[2 * index + 1], 1 - order[1 + index]),
        ):
            at = pl.ds(pl.multiple_of((2 * index + half) * rows, rows), rows)
            for lead in range(3):
                total = kept[lead, at, :].astype(full) + received[lead, at, :].astype(full)
                target[lead] = total.astype(low)
            total = out_kept[0, at, :].astype(full) + out_received[0, at, :].astype(full)
            target[3] = total.astype(low)


def stage_kernel(joined, order, *refs):
    count = len(refs) // 5 if not joined else (len(refs) - 3) // 2
    pairs = refs[: 2 * count]
    if joined:
        outs, totals = refs[-3:-1], refs[-1:]
        at = 0
        for index in range(count):
            rows = pairs[2 * index].shape[1]
            totals[0][:, at : at + rows, :] = (
                pairs[2 * index][...].astype(full) + pairs[2 * index + 1][...].astype(full)
            )
            at += rows
    else:
        outs, totals = refs[2 * count : 4 * count], refs[4 * count :]
        for index in range(count):
            totals[index][...] = (
                pairs[2 * index][...].astype(full) + pairs[2 * index + 1][...].astype(full)
            )
    for index, total in enumerate(totals):
        rows = total.shape[1] // 2
        for target, half in ((outs[2 * index], order[index]), (outs[2 * index + 1], 1 - order[index])):
            at = pl.ds(pl.multiple_of(half * rows, rows), rows)
            target[...] = total[:, at, :].astype(low)


def grad_far_kernel(order, kept, received, w_key, w_value, both, grad_far):
    for index in range(2):
        both[index] = (kept[index].astype(full) + received[index].astype(full)).astype(low)
    grad = matmul_right(both[0], w_key[...]) + matmul_right(both[1], w_value[...])
    half = grad.shape[0] // 2
    grad_far[:half, :] = grad[half:].astype(low)
    grad_far[half:, :] = grad[:half].astype(low)


def weight_kernel(
    core, normed, query_own, query_mixed, own_kept, own_received, mixed_kept,
    mixed_received, far, kept, sent, both, rows_out, grad_weight,
):
    item = jnp.concatenate([query_own[...], query_mixed[...]], axis=0)
    count = item.shape[0]
    rows_out[0:1, :] = jnp.sum(item.astype(full), axis=0, keepdims=True)
    grad_weight[...] = matmul_left(normed[:count, :], item).astype(low)
    keep_core_half(core[0], grad_weight, kept.at[0:1], sent.at[0:1])
    for index in range(2):
        own = own_kept[index].astype(full) + own_received[index].astype(full)
        mixed = mixed_kept[index].astype(full) + mixed_received[index].astype(full)
        item = jnp.concatenate([own.astype(low), mixed.astype(low), far[index]], axis=0)
        both[index] = item[:count]
        rows_out[1 + index : 2 + index, :] = jnp.sum(item.astype(full), axis=0, keepdims=True)
        grad_weight[...] = matmul_left(normed[...], item).astype(low)
        keep_core_half(
            core[0], grad_weight, kept.at[1 + index : 2 + index], sent.at[1 + index : 2 + index]
        )
    rows_out[3:8, :] = jnp.zeros_like(rows_out[3:8, :])


def input_kernel(
    core, query_own, query_mixed, both, far, w_query, w_key, w_value, first,
    second, gain, grad_middle, to_first, to_second, rows_out,
):
    span = first.shape[0] // 2
    grad_query = jnp.concatenate([query_own[...], query_mixed[...]], axis=0)
    grad = matmul_right(grad_query, w_query[...])
    for index, weight in enumerate((w_key, w_value)):
        grad = grad + matmul_right(both[index], weight[...])
    grad = jnp.concatenate(
        [grad[: 2 * span], grad[2 * span :] + far[...].astype(full)], axis=0
    )
    hat, scale = whiten(join(first[...], second[...], span).astype(full))
    rows_out[0:1, :] = jnp.sum(grad * hat, axis=0, keepdims=True)
    rows_out[1:2, :] = jnp.sum(grad, axis=0, keepdims=True)
    rows_out[2:8, :] = jnp.zeros_like(rows_out[2:8, :])
    done = (grad_middle[...] + whiten_back(grad * gain[...], hat, scale)).astype(low)
    put_messages(to_first, to_second, done)


def expand_kernel(place, order, *refs):
    sources = refs[:4]
    out = refs[-1]
    choice = 2 * ((pl.program_id(0) // 2) ^ order[0]) + ((pl.program_id(0) % 2) ^ order[place])
    for number, source in enumerate(sources):

        @pl.when(choice == number)
        def _(source=source):
            out[...] = source[0].astype(full)


def expand_mixed_kernel(order, *refs):
    sources, outs = refs[:8], refs[8:]
    index = pl.program_id(0)
    side = (index // 2) % 2
    bit = jnp.where(side == 0, order[1], order[2])
    choice = 4 * side + 2 * ((index // 4) ^ order[0]) + ((index % 2) ^ bit)
    for number, source in enumerate(sources):

        @pl.when(choice == number)
        def _(source=source):
            for place, out in enumerate(outs):
                out[...] = source[place].astype(full)


def after(value, *others):
    return lax.optimization_barrier((value, *others))[0]


def on_device(
    inputs, cotangent, lengths, predicted, norm1_gain, norm1_shift, w_query, b_query, w_key,
    b_key, w_value, b_value, w_out, b_out, norm2_gain, norm2_shift, w_up, b_up, w_down, b_down,
):
    seqs, span, width = inputs.shape
    half = span // 2
    tokens = seqs * span
    hidden_width = w_up.shape[1]
    groups = lax.axis_size("dp")
    assert seqs == 3 and lax.axis_size("seq") == 4 and hidden_width == 4 * width
    bits = [1 << place for place in range(1, groups.bit_length() - 1)]
    group = lax.axis_index("dp")
    depth = lax.axis_index("seq")
    core = group & 1
    side = depth & 1
    pair = depth >> 1
    count = 4 * span
    pairs = width // PAIR
    square = (width, width)

    def flip(value, bit):
        return lax.ppermute(value, "dp", [(i, i ^ bit) for i in range(groups)])

    def flip_depth(value, bit):
        return lax.ppermute(value, "seq", [(i, i ^ bit) for i in range(4)])

    def route(turn):
        moves = []
        for at in range(groups):
            for z in range(4):
                to = (at & ~1) | (z & 1)
                to_z = 2 * (at & 1) + (turn ^ (z >> 1))
                moves.append((at * 4 + z, to * 4 + to_z))
        return moves

    def send(value, turn):
        return lax.ppermute(value, ("dp", "seq"), route(turn))

    def send_back(value, turn):
        return lax.ppermute(value, ("dp", "seq"), [(b, a) for a, b in route(turn)])

    def ranks(sizes):
        longest = jnp.argmax(sizes).astype(jnp.int32)
        return (
            jnp.where(longest == 0, 1, 0),
            jnp.where(longest == 2, 1, 2),
            longest,
        )

    low_own, high_own, mixed_at = ranks(lengths)
    near = jnp.where(pair == 0, low_own, high_own)
    other = jnp.where(pair == 0, high_own, low_own)
    index = jnp.arange(8)
    turn = index // 4
    spot = index % 4
    chosen = jnp.where(turn == 0, near, other)
    order = jnp.where(
        spot < 2, 2 * chosen + spot, 2 * mixed_at + (turn ^ pair ^ (spot // 3))
    )
    first, second = pack(inputs, order, 4)
    cot_first, cot_second = pack(after(cotangent, first), order, 3)
    first, second = send(first, 0), send(second, 1)
    index = jnp.arange(2 * seqs)
    seq_at = index // 2
    part = index % 2
    from_turn = jnp.where(seq_at == mixed_at, part, (seq_at == high_own).astype(jnp.int32)) ^ pair
    from_row = jnp.where(seq_at == mixed_at, 2, part)
    order_back = jnp.concatenate([from_turn, from_row])

    sibling_lengths = flip(lengths, 1)
    sizes = jnp.where(core == pair, lengths, sibling_lengths)
    low_here, high_here, mixed_here = ranks(sizes)
    own_length = sizes[jnp.where(side == 0, low_here, high_here)]
    mixed_length = sizes[mixed_here]

    def starts(at_side, at_core):
        slots = jnp.arange(2)
        quarter = 2 * (slots ^ at_side) + at_core
        return quarter * span, quarter * span + at_side * half

    own_at, mixed_start = starts(side, core)
    own_sibling, mixed_sibling = starts(side, 1 - core)
    far_start = own_at + (1 - side) * half
    far_sibling = own_sibling + (1 - side) * half
    own_place = jnp.concatenate([own_length[None], own_at, own_sibling, own_at])
    mixed_place = jnp.concatenate(
        [mixed_length[None], mixed_start, mixed_sibling, far_start, far_sibling, mixed_start]
    )
    project_place = jnp.concatenate([own_at, mixed_start, far_start])

    frequency = 10000.0 ** (-jnp.arange(HEAD // 2, dtype=full) / (HEAD // 2))
    angle = jnp.arange(count, dtype=full)[:, None] * frequency[None, :]
    cosine = jnp.tile(jnp.cos(angle), (1, 4))
    sine = jnp.sin(angle)
    sine = jnp.tile(jnp.concatenate([-sine, sine], axis=1), (1, 2))

    def row(vector):
        return vector.reshape(1, -1)

    gain1, shift1 = row(norm1_gain), row(norm1_shift)
    gain2, shift2 = row(norm2_gain), row(norm2_shift)

    def wholes(*items):
        return [whole(item) for item in items]

    extent = tokens + span
    project_place = after(project_place, cot_first, own_place, mixed_place, cosine, sine)
    query, both, normed = call(
        project_kernel,
        (1,),
        project_place,
        wholes(
            first, second, gain1, shift1, w_query, w_key, w_value, row(b_query), row(b_key),
            row(b_value), cosine, sine,
        ),
        wholes(
            fresh((tokens, width), low), fresh((2, extent, width), low), fresh((extent, width), low)
        ),
    )
    both_sibling = flip(both, 1)
    cot_first, cot_second, _ = lax.optimization_barrier((cot_first, cot_second, first))
    cot_first, cot_second = send(cot_first, 0), send(cot_second, 1)

    def columns(array, rows, at, size=PAIR, base=0):
        if len(array.shape) == 2:
            return (array, pl.BlockSpec((rows, size), lambda h, _: (at, base + h)))
        return (array, pl.BlockSpec((2, rows, size), lambda h, _: (0, at, base + h)))

    def own_pieces(*given):
        return [columns(both, 2 * span, 0, *given), columns(both_sibling, 2 * span, 0, *given)]

    def mixed_pieces(*given):
        return [
            columns(both, span, 2, *given),
            columns(both_sibling, span, 2, *given),
            columns(both, span, 3, *given),
            columns(both_sibling, span, 3, *given),
        ]

    def attend(place, rows, at, pieces):
        size = 2 * PAIR
        pieces = pieces(size)
        return call(
            functools.partial(attend_kernel, len(pieces)),
            (width // size,),
            place,
            [columns(query, rows, at, size), *pieces],
            [
                columns(fresh((rows, width), low), rows, 0, size),
                (
                    fresh((pairs, 8, rows), full),
                    pl.BlockSpec((2, 8, rows), lambda h, _: (h, 0, 0)),
                ),
            ],
            [pltpu.VMEM((count, size), low), pltpu.VMEM((count, size), low)],
                )

    own, own_logsum = attend(own_place, 2 * span, 0, own_pieces)
    mixed, mixed_logsum = attend(after(mixed_place, own), span, 2, mixed_pieces)

    def wide(array):
        return (array, pl.BlockSpec(square, lambda j, tiles: (0, tiles[j])))

    def tall(array):
        return (array, pl.BlockSpec(square, lambda j, tiles: (tiles[j], 0)))

    middle, normed2, hidden, slope, result_first, result_second = call(
        forward_kernel,
        (4,),
        jnp.arange(4),
        wholes(own, mixed, first, second, w_out, row(b_out), gain2, shift2)
        + [
            wide(w_up),
            (row(b_up), pl.BlockSpec((1, width), lambda j, tiles: (0, tiles[j]))),
            tall(w_down),
            whole(row(b_down)),
        ],
        wholes(fresh((tokens, width), full), fresh((tokens, width), low))
        + [wide(fresh((tokens, hidden_width), low)), wide(fresh((tokens, hidden_width), full))]
        + wholes(fresh((tokens // 2, width), low), fresh((tokens // 2, width), low)),
        [pltpu.VMEM((tokens, width), full)],
    )
    result = [send_back(result_first, 0), send_back(result_second, 1)]

    rows_fresh = fresh((8, width), full)
    grad_scratch = [pltpu.VMEM((tokens, width), low)]

    def tile_outs():
        return [
            (
                fresh((2, 2, width, width), low),
                pl.BlockSpec((2, None, width, width), lambda j, _: (0, j, 0, 0)),
            ),
            (fresh((2, 8, width), full), pl.BlockSpec((None, 8, width), lambda j, _: (j, 0, 0))),
        ]

    tiles_sent, b_up_sent, grad_normed2, cot = call(
        backward_first_kernel,
        (2,),
        jnp.stack([2 * (1 - core), 2 * (1 - core) + 1]),
        [wide(hidden), wide(slope)]
        + wholes(cot_first, cot_second, normed2)
        + [wide(w_up), tall(w_down)],
        tile_outs() + wholes(fresh((tokens, width), full), fresh((tokens, width), low)),
        grad_scratch,
    )
    tiles_received = flip(tiles_sent, 1)
    (
        tiles_kept, b_up_kept, grad_middle, grad_own, grad_mixed, out_kept, out_sent, rows_middle,
    ) = call(
        backward_last_kernel,
        (2,),
        jnp.stack([2 * core, 2 * core + 1, core]),
        [wide(hidden), wide(slope)]
        + wholes(cot, normed2)
        + [wide(w_up), tall(w_down)]
        + wholes(grad_normed2, own, mixed, middle, w_out, gain2),
        tile_outs()
        + wholes(
            fresh((tokens, width), full), fresh((2 * span, width), low), fresh((span, width), low),
            fresh((1, width // 2, width), low), fresh((1, width // 2, width), low), rows_fresh,
        ),
        [pltpu.VMEM((tokens, width), full), *grad_scratch, pltpu.VMEM(square, low)],
    )
    out_received = flip(out_sent, 1)

    def bit_of(bit):
        return (group & bit) // bit

    def split(addends, at):
        rows = addends[0].shape[1] // 2

        def part(which):
            items = [
                lax.dynamic_slice_in_dim(item, which * rows, rows, 1).astype(full)
                for item in addends
            ]
            return sum(items[1:], items[0]).astype(low)

        return part(at), part(1 - at)

    def added(addends):
        return (addends[0].astype(full) + addends[1].astype(full)).astype(low)

    def ordered(at, mine, theirs):
        return jnp.where(
            at == 0,
            jnp.concatenate([mine, theirs], axis=1),
            jnp.concatenate([theirs, mine], axis=1),
        )

    def stage(values, at, joined=False):
        lead, _, columns_in = values[0][0].shape
        sizes = [item[0].shape[1] for item in values]
        sizes = [sum(sizes)] if joined else sizes
        if any(size % 16 for size in sizes):
            if joined:
                values = [[jnp.concatenate([added(item) for item in values], axis=1)]]
            return [split(item, place) for item, place in zip(values, at)]
        parts = call(
            functools.partial(stage_kernel, joined),
            (1,),
            jnp.stack(at),
            wholes(*[part for item in values for part in item]),
            wholes(
                *[fresh((lead, size // 2, columns_in), low) for size in sizes for _ in range(2)]
            ),
            [pltpu.VMEM((lead, size, columns_in), full) for size in sizes],
            room=32,
        )
        return [tuple(parts[2 * place : 2 * place + 2]) for place in range(len(sizes))]

    def chain(parts, orders):
        for step in range(len(bits)):
            if step > 0:
                parts = stage(values, [bit_of(order[step]) for order in orders])
            values = yield [
                [keep, flip(give, order[step])] for (keep, give), order in zip(parts, orders)
            ]
        sizes = [item[0].shape[1] for item in values]
        ((keep, give),) = stage(values, [side], joined=True)
        values = yield [[keep, flip_depth(give, 1)]]
        ((keep, give),) = stage(values, [pair])
        (value,) = yield [[keep, flip_depth(give, 2)]]
        total = added(value)
        (value,) = yield [[total, flip_depth(total, 2)]]
        joined = ordered(pair, *value)
        (value,) = yield [[joined, flip_depth(joined, 1)]]
        joined = ordered(side, *value)
        ends = [sum(sizes[: place + 1]) for place in range(len(sizes))]
        values = [joined[:, end - size : end] for end, size in zip(ends, sizes)]
        for step in range(len(bits) - 1, 0, -1):
            values = yield [
                [item, flip(item, order[step])] for item, order in zip(values, orders)
            ]
            values = [
                ordered(bit_of(order[step]), *item) for item, order in zip(values, orders)
            ]
        values = yield [[item, flip(item, order[0])] for item, order in zip(values, orders)]
        values = yield [item + [flip(part, 1) for part in item] for item in values]
        yield values

    class Chain:
        def __init__(self, left, right):
            self.steps = chain([left, right], [bits, reverse])
            self.state = next(self.steps)
            self.left = 2 * len(bits) + 5

        def here(self):
            return [item[0] for item in self.state]

    def advance(chains, *gates):
        chains = [item for item in chains if item.left > 0]
        states = lax.optimization_barrier(([item.state for item in chains], gates))[0]
        for item, state in zip(chains, states):
            item.state = item.steps.send(state)
            item.left -= 1

    reverse = bits[::-1]
    orders = jnp.stack([core, bit_of(bits[0]), bit_of(bits[-1])])

    part = fresh((1, width, width), low)
    parts = call(
        halve_kernel,
        (1,),
        orders,
        wholes(tiles_kept, tiles_received),
        wholes(part, part, part, part),
        room=40,
    )
    tile_sum = Chain(tuple(parts[:2]), tuple(parts[2:]))
    result = unpack(after(result[0], grad_middle), result[1], order_back, seqs)

    def attend_back(place, rows, at, pieces, grad, out, logsum, size, base, steps):
        given = pieces(size, base)
        group_pairs = size // PAIR
        return call(
            functools.partial(attend_back_kernel, len(given)),
            (steps,),
            place,
            [
                columns(query, rows, at, size, base),
                columns(grad, rows, 0, size, base),
                columns(out, rows, 0, size, base),
                (logsum, pl.BlockSpec((group_pairs, 8, rows), lambda h, _: (base + h, 0, 0))),
                whole(cosine),
                whole(sine),
                *given,
            ],
            [columns(fresh((rows, size * steps), low), rows, 0, size)]
            + [columns(fresh((2, rows, size * steps), low), rows, 0, size) for _ in given],
            [pltpu.VMEM((count, size), low)] * 4,
                )

    query_mixed, mixed_here_grad, mixed_sibling_grad, far_grad, far_sibling_grad = attend_back(
        after(mixed_place, *tile_sum.here(), result), span, 2, mixed_pieces, grad_mixed, mixed, mixed_logsum,
        2 * PAIR, 0, pairs // 2,
    )
    far_received = flip(far_sibling_grad, 1)
    mixed_received = flip(mixed_sibling_grad, 1)
    advance([tile_sum], query_mixed)
    far_both, grad_far = call(
        grad_far_kernel,
        (1,),
        after(core[None], *tile_sum.here()),
        wholes(far_grad, far_received, w_key, w_value),
        wholes(fresh((2, span, width), low), fresh((span, width), low)),
    )
    grad_far = flip_depth(grad_far, 1)

    query_own, own_kept, own_sent = attend_back(
        after(own_place, far_both), 2 * span, 0, own_pieces, grad_own, own, own_logsum, 2 * PAIR, 0,
        pairs // 2,
    )
    own_received = flip(own_sent, 1)
    advance([tile_sum], query_own)
    weight_kept, weight_sent, both_grad, rows_weight = call(
        weight_kernel,
        (1,),
        after(core[None], *tile_sum.here()),
        wholes(
            normed, query_own, query_mixed, own_kept, own_received, mixed_here_grad,
            mixed_received, far_both,
        ),
        wholes(
            fresh((3, width // 2, width), low), fresh((3, width // 2, width), low),
            fresh((2, tokens, width), low), rows_fresh,
        ),
        [pltpu.VMEM(square, low)],
    )
    weight_received = flip(weight_sent, 1)
    advance([tile_sum], rows_weight)
    back_first, back_second, rows_input = call(
        input_kernel,
        (1,),
        after(core[None], *tile_sum.here()),
        wholes(
            query_own, query_mixed, both_grad, grad_far, w_query, w_key, w_value, first, second,
            gain1, grad_middle,
        ),
        wholes(fresh((tokens // 2, width), low), fresh((tokens // 2, width), low), rows_fresh),
    )

    live = (depth * span + jnp.arange(span))[None, :] < lengths[:, None]
    counts = jnp.sum(
        jnp.where(live[:, :, None] & (predicted[:, :, None] == jnp.arange(CLASSES)), 1.0, 0.0),
        axis=(0, 1),
    )
    counts = jnp.zeros((1, width), full).at[0, :CLASSES].set(counts)
    b_up_kept, b_up_sent = b_up_kept[:, 0], b_up_sent[:, 0]
    rows_up = jnp.where(
        core == 0,
        jnp.concatenate([b_up_kept, b_up_sent]),
        jnp.concatenate([b_up_sent, b_up_kept]),
    )
    small = jnp.concatenate(
        [rows_middle[:4], rows_up, rows_weight[:3], rows_input[:2], counts], axis=0
    )

    class Small:
        def __init__(self):
            self.moves = [(flip, bit) for bit in (1, *bits)] + [(flip_depth, 1), (flip_depth, 2)]
            self.steps = self
            move, bit = self.moves.pop(0)
            self.state = [[small, move(small, bit)]]
            self.left = len(bits) + 3

        def send(self, state):
            total = state[0][0] + state[0][1]
            if not self.moves:
                return [[total]]
            move, bit = self.moves.pop(0)
            return [[total, move(total, bit)]]
    back = [send_back(back_first, 0), send_back(back_second, 1)]
    weight_kept, weight_received, out_kept, out_received, _ = lax.optimization_barrier(
        (weight_kept, weight_received, out_kept, out_received, rows_input)
    )
    part = fresh((4, width // 8, width), low)
    parts = call(
        quarter_kernel,
        (1,),
        orders,
        wholes(weight_kept, weight_received, out_kept, out_received),
        wholes(part, part, part, part),
        room=32,
    )
    weight_sum = Chain(tuple(parts[:2]), tuple(parts[2:]))
    small_sum = Small()
    for _ in range(3):
        advance([weight_sum, small_sum, tile_sum])
    grad_inputs = unpack(after(back[0], *weight_sum.here()), back[1], order_back, seqs)
    advance([weight_sum, small_sum, tile_sum], grad_inputs)
    while tile_sum.left > 0:
        advance([weight_sum, small_sum, tile_sum])
    left, right = tile_sum.state
    gate = weight_sum.here()

    def expand(sources, place, shape, target):
        return call(
            functools.partial(expand_kernel, place),
            (4,),
            after(orders, *gate),
            wholes(*sources),
            [(fresh(shape, full), pl.BlockSpec(square, target))],
            room=32,
        )[0]

    grad_w_down = expand(left, 1, (hidden_width, width), lambda i, _: (i, 0))
    grad_w_up = expand(right, 2, (width, hidden_width), lambda i, _: (0, i))
    advance([weight_sum, small_sum], grad_w_down)
    advance([weight_sum, small_sum], grad_w_up)
    gates = []
    while weight_sum.left > 0 or small_sum.left > 0:
        advance([weight_sum, small_sum], *gates)
        gates = []
    left, right = weight_sum.state
    grad_w_query, grad_w_key, grad_w_value, grad_w_out = call(
        expand_mixed_kernel,
        (8,),
        orders,
        wholes(*left, *right),
        [(fresh(square, full), pl.BlockSpec((width // 8, width), lambda i, _: (i, 0)))] * 4,
        room=32,
    )
    small = small_sum.state[0][0]

    return (
        result,
        grad_inputs,
        small[11],
        small[12],
        grad_w_query,
        small[8],
        grad_w_key,
        small[9],
        grad_w_value,
        small[10],
        grad_w_out,
        small[1],
        small[2],
        small[3],
        grad_w_up,
        small[4:8].reshape(-1),
        grad_w_down,
        small[0],
        small[13, :CLASSES].astype(jnp.int32),
    )


def solution(mesh):
    tokens = P("dp", "seq", None)
    return jax.shard_map(
        on_device,
        mesh=mesh,
        in_specs=(tokens, tokens, P("dp"), P("dp", "seq")) + (P(),) * 16,
        out_specs=(tokens, tokens) + (P(),) * 17,
        check_vma=False,
    )
```

time: 503 us -> 459 us (0.913)
  waiting for transfers between devices: 174 us -> 150 us
  other arithmetic: 29.7 us -> 14.2 us
  starting transfers between devices: 81 us -> 68.4 us
  local copies, waits for them, and re-layouts: 27.1 us -> 35.6 us
    ppermute x36 -> x35, waiting for transfers between devices: 71.3 us -> 54.5 us  [flip(): return lax.ppermute(value, 'dp', [(i, i ^ bit) for i in range(groups)])]
    unnamed x76 -> x100, local copies, waits for them, and re-layouts: 4.51 us -> 16.7 us
    convert_element_type x10 -> x0, other arithmetic: 8.66 us -> none  [part(): return sum(items[1:], items[0]).astype(low)]
    slice x4 -> x2, local copies, waits for them, and re-layouts: 8.41 us -> 0.12 us  [chain(): values = [joined[:, end - size:end] for end, size in zip(ends, sizes)]]
    ppermute x36 -> x35, starting transfers between devices: 42.7 us -> 36.7 us  [flip(): return lax.ppermute(value, 'dp', [(i, i ^ bit) for i in range(groups)])]
    ppermute x4, waiting for transfers between devices: 5.96 us -> 0.01 us  [send_back(): return lax.ppermute(value, ('dp', 'seq'), [(b, a) for a, b in route(turn)])]
    ppermute x12 -> x11, starting transfers between devices: 18.8 us -> 13.8 us  [flip_depth(): return lax.ppermute(value, 'seq', [(i, i ^ bit) for i in range(4)])]
    ppermute x12 -> x11, waiting for transfers between devices: 74.4 us -> 76.3 us  [flip_depth(): return lax.ppermute(value, 'seq', [(i, i ^ bit) for i in range(4)])]
  transfers between devices with their start and end apart: 56 -> 54, of which waited for: 20 -> 22; matrix products, arithmetic and copies ran while one was open for 10% -> 7% of each run, Pallas kernels for 28% -> 26%
where the time goes in v2:
time: 459 us; the launch traced here: 453 us
  Pallas kernels  177 us (39%)
  waiting for transfers between devices  150 us (33%)
  starting transfers between devices  68.4 us (15%)
  local copies, waits for them, and re-layouts  35.6 us (8%)
  other arithmetic  14.2 us (3%)
  between operations  7.04 us (2%)
    pallas_call x26, Pallas kernels, call(): pl.pallas_call(kernel, grid_spec=pltpu.PrefetchScalarGridSpec(num_scalar_...  177 us
    ppermute x11, waiting for transfers between devices, flip_depth(): return lax.ppermute(value, 'seq', [(i, i ^ bit) for i in range(4)])  76.3 us
    ppermute x35, waiting for transfers between devices, flip(): return lax.ppermute(value, 'dp', [(i, i ^ bit) for i in range(groups)])  54.5 us
    ppermute x35, starting transfers between devices, flip(): return lax.ppermute(value, 'dp', [(i, i ^ bit) for i in range(groups)])  36.7 us
    ppermute x4, waiting for transfers between devices, send(): return lax.ppermute(value, ('dp', 'seq'), route(turn))  19.6 us
    unnamed x100, local copies, waits for them, and re-layouts  16.7 us
    ppermute x11, starting transfers between devices, flip_depth(): return lax.ppermute(value, 'seq', [(i, i ^ bit) for i in range(4)])  13.8 us
  transfers between devices with their start and end apart: 54, of which 22 were waited for; matrix products, arithmetic and copies ran while one was open for 7% of the time, Pallas kernels for 26%

profile of v2, /device:TPU:0, one launch (start us, length us, event | category | flops | bytes accessed | tf_op | source)
XLA Modules:
  0.0 452.6 jit_solution(6028184232987617948)
XLA Ops:
  30.3 19.6 %collective-permute-done.2.second = bf16[512,768]{1,0:T(8,128)(2,1)} collective-permute-done((bf16[512,768]{1,0:T(8,128)(2,1)S(1)}, bf16[512,768]{1,0:T(8,128)(2,1)}, u32[]{:S(2)}, u32[]{:S(2)}) %collective-permute-start.2) | collective-permute-done | bytes 786464 | tf_op jit(solution)/shard_map/ppermute | solution.py:620
  49.9 10.1 %shard_map.341 = (bf16[768,768]{1,0:T(8,128)(2,1)}, bf16[2,1024,768]{2,1,0:T(8,128)(2,1)}, bf16[1024,768]{1,0:T(8,128)(2,1)}) custom-call(s32[6]{0:T(128)} %pad_add_fusion.2.place, bf16[512,768]{1,0:T(8,128)(2,1)} %collective-permute-done.1.first, bf16[512,768]{1,0:T(8,128)(2,1)} %collective-permute-done.2.second, f32[1,768]{1,0:T(1,128)} %reshape.399.gain, ...), custom_call_target="tpu_custom_call" | custom-call | flops 1 | bytes 1 | tf_op jit(solution)/shard_map/pallas_call | solution.py:61
  67.3 7.9 %shard_map.342 = (bf16[512,768]{1,0:T(8,128)(2,1)}, f32[6,8,512]{2,1,0:T(8,128)}) custom-call(s32[7]{0:T(128)} %pad_add_fusion.1.place, bf16[768,768]{1,0:T(8,128)(2,1)} %get-tuple-element.205.query, bf16[2,1024,768]{2,1,0:T(8,128)(2,1)} %get-tuple-element.206.refs_0_.refs_2_, bf16[2,1024,768]{2,1,0:T(8,128)(2,1)} %collective-permute-done.3.refs_1_.refs_3_), custom_call_target="tpu_custom_call" | custom-call | flops 1 | bytes 1 | tf_op jit(solution)/shard_map/pallas_call | solution.py:61
  75.2 10.7 %shard_map.343 = (bf16[256,768]{1,0:T(8,128)(2,1)}, f32[6,8,256]{2,1,0:T(8,128)}) custom-call(s32[11]{0:T(128)} %concatenate.141.place, bf16[768,768]{1,0:T(8,128)(2,1)} %get-tuple-element.205.query, bf16[2,1024,768]{2,1,0:T(8,128)(2,1)} %get-tuple-element.206.refs_0_.refs_2_, bf16[2,1024,768]{2,1,0:T(8,128)(2,1)} %collective-permute-done.3.refs_1_.refs_3_, ...), custom_call_target="tpu_custom_call" | custom-call | flops 1 | bytes 1 | tf_op jit(solution)/shard_map/pallas_call | solution.py:61
  86.4 19.3 %shard_map.344 = (f32[768,768]{1,0:T(8,128)}, bf16[768,768]{1,0:T(8,128)(2,1)}, bf16[768,3072]{1,0:T(8,128)(2,1)}, f32[768,3072]{1,0:T(8,128)}, bf16[384,768]{1,0:T(8,128)(2,1)}, /*index=5*/bf16[384,768]{1,0:T(8,128)(2,1)}) custom-call(s32[4]{0:T(128)} %iota.71.order, bf16[512,768]{1,0:T(8,128)(2,1)} %get-tuple-element.207.own.mixed, ...), custom_call_target="tpu_custom_call" | custom-call | flops 1 | bytes 1 | tf_op jit(solution)/shard_map/pallas_call | solution.py:61
  106.8 15.7 %shard_map.345 = (bf16[2,2,768,768]{3,2,1,0:T(8,128)(2,1)}, f32[2,8,768]{2,1,0:T(8,128)}, f32[768,768]{1,0:T(8,128)}, bf16[768,768]{1,0:T(8,128)(2,1)}) custom-call(s32[2]{0:T(128)} %pad_add_fusion.4.tiles, bf16[768,3072]{1,0:T(8,128)(2,1)} %get-tuple-element.211.hidden, f32[768,3072]{1,0:T(8,128)} %get-tuple-element.212.slope, bf16[384,768]{1,0:T(8,128)(2,1)} %copy-done.30, ...), custom_call_target="tpu_custom_call" | custom-call | flops 1 | bytes 1 | tf_op jit(solution)/shard_map/pallas_call | solution.py:61
  128.2 22.2 %shard_map.346 = (bf16[2,2,768,768]{3,2,1,0:T(8,128)(2,1)}, f32[2,8,768]{2,1,0:T(8,128)}, f32[768,768]{1,0:T(8,128)}, bf16[512,768]{1,0:T(8,128)(2,1)}, bf16[256...) custom-call(s32[3]{0:T(128)} %pad_add_fusion.3.tiles, ...), custom_call_target="tpu_custom_call" | custom-call | flops 1 | bytes 1 | tf_op jit(solution)/shard_map/pallas_call | solution.py:61
  158.0 6.3 %collective-permute-start.9 = (bf16[1,768,768]{2,1,0:T(8,128)(2,1)}, bf16[1,768,768]{2,1,0:T(8,128)(2,1)S(1)}, u32[]{:S(2)}, u32[]{:S(2)}) collective-permute-start(bf16[1,768,768]{2,1,0:T(8,128)(2,1)} %get-tuple-element.226), channel_id=1, source_target_pairs={{0,8},{4,12},{8,0},{12,4},{16,24},{20,28},{24,16},{28,20},{1,9},{5... | collective-permute-start | bytes 3538952 | tf_op jit(solution)/shard_map/ppermute | solution.py:605
  168.5 16.5 %shard_map.349 = (bf16[256,768]{1,0:T(8,128)(2,1)}, bf16[2,256,768]{2,1,0:T(8,128)(2,1)}, bf16[2,256,768]{2,1,0:T(8,128)(2,1)}, bf16[2,256,768]{2,1,0:T(8,128)(2,1)}, bf16[2,256,768]{2,1,0:T(8,128)(2,1)}) custom-call(s32[11]{0:T(128)} %concatenate.141.place, bf16[768,768]{1,0:T(8,128)(2,1)} %get-tuple-element.205.query, ...), custom_call_target="tpu_custom_call" | custom-call | flops 1 | bytes 1 | tf_op jit(solution)/shard_map/pallas_call | solution.py:61
  200.5 11.0 %shard_map.352 = (bf16[512,768]{1,0:T(8,128)(2,1)}, bf16[2,512,768]{2,1,0:T(8,128)(2,1)}, bf16[2,512,768]{2,1,0:T(8,128)(2,1)}) custom-call(s32[7]{0:T(128)} %pad_add_fusion.1.place, bf16[768,768]{1,0:T(8,128)(2,1)} %get-tuple-element.205.query, bf16[512,768]{1,0:T(8,128)(2,1)} %get-tuple-element.246.grad, bf16[512,768]{1,0:T(8,128)(2,1)} %get-tuple-element.207.own.mixed, ...), custom_call_target="tpu_custom_call" | custom-call | flops 1 | bytes 1 | tf_op jit(solution)/shard_map/pallas_call | solution.py:61
  212.4 8.5 %collective-permute-start.12 = (bf16[1,384,768]{2,1,0:T(8,128)(2,1)S(1)}, bf16[1,384,768]{2,1,0:T(8,128)(2,1)S(1)}, u32[]{:S(2)}, u32[]{:S(2)}) collective-permute-start(bf16[1,384,768]{2,1,0:T(8,128)(2,1)S(1)} %copy-done.24), channel_id=1, source_target_pairs={{0,8},{4,12},{8,0},{12,4},{16,24},{20,28},{24,16},{28,20},{1,9},{5... | collective-permute-start | bytes 1769480 | tf_op jit(solution)/shard_map/ppermute | solution.py:605
  220.9 6.5 %collective-permute-done.11.refs_1_ = bf16[1,384,768]{2,1,0:T(8,128)(2,1)S(1)} collective-permute-done((bf16[1,384,768]{2,1,0:T(8,128)(2,1)S(1)}, bf16[1,384,768]{2,1,0:T(8,128)(2,1)S(1)}, u32[]{:S(2)}, u32[]{:S(2)}) %collective-permute-start.11) | collective-permute-done | bytes 589856 | tf_op jit(solution)/shard_map/ppermute | solution.py:605
  227.4 7.1 %collective-permute-done.12.refs_3_ = bf16[1,384,768]{2,1,0:T(8,128)(2,1)S(1)} collective-permute-done((bf16[1,384,768]{2,1,0:T(8,128)(2,1)S(1)}, bf16[1,384,768]{2,1,0:T(8,128)(2,1)S(1)}, u32[]{:S(2)}, u32[]{:S(2)}) %collective-permute-start.12) | collective-permute-done | bytes 589856 | tf_op jit(solution)/shard_map/ppermute | solution.py:605
  237.0 9.7 %shard_map.354 = (bf16[3,384,768]{2,1,0:T(8,128)(2,1)}, bf16[3,384,768]{2,1,0:T(8,128)(2,1)}, bf16[2,768,768]{2,1,0:T(8,128)(2,1)}, f32[8,768]{1,0:T(8,128)}) custom-call(s32[1]{0:T(128)} %bitcast.7.order.core, bf16[1024,768]{1,0:T(8,128)(2,1)} %get-tuple-element.256.normed, bf16[512,768]{1,0:T(8,128)(2,1)} %get-tuple-element.248.query_own, ...), custom_call_target="tpu_custom_call" | custom-call | flops 1 | bytes 1 | tf_op jit(solution)/shard_map/pallas_call | solution.py:61
  256.5 10.3 %collective-permute-done.14.refs_1_ = bf16[1,384,768]{2,1,0:T(8,128)(2,1)S(1)} collective-permute-done((bf16[1,384,768]{2,1,0:T(8,128)(2,1)}, bf16[1,384,768]{2,1,0:T(8,128)(2,1)S(1)}, u32[]{:S(2)}, u32[]{:S(2)}) %collective-permute-start.14) | collective-permute-done | bytes 589856 | tf_op jit(solution)/shard_map/ppermute | solution.py:608
  275.4 9.4 %shard_map.356 = (bf16[384,768]{1,0:T(8,128)(2,1)}, bf16[384,768]{1,0:T(8,128)(2,1)}, f32[8,768]{1,0:T(8,128)}) custom-call(s32[1]{0:T(128)} %bitcast.7.order.core, bf16[512,768]{1,0:T(8,128)(2,1)} %get-tuple-element.248.query_own, bf16[256,768]{1,0:T(8,128)(2,1)} %get-tuple-element.232.query_mixed, bf16[2,768,768]{2,1,0:T(8,128)(2,1)} %get-tuple-element.266.both, ...), custom_call_target="tpu_custom_call" | custom-call | flops 1 | bytes 1 | tf_op jit(solution)/shard_map/pallas_call | solution.py:61
  298.5 11.1 %collective-permute-done.24 = bf16[1,192,768]{2,1,0:T(8,128)(2,1)S(1)} collective-permute-done((bf16[1,192,768]{2,1,0:T(8,128)(2,1)}, bf16[1,192,768]{2,1,0:T(8,128)(2,1)S(1)}, u32[]{:S(2)}, u32[]{:S(2)}) %collective-permute-start.24) | collective-permute-done | bytes 294944 | tf_op jit(solution)/shard_map/ppermute | solution.py:608
  316.2 6.5 %collective-permute-done.27 = f32[14,768]{1,0:T(8,128)S(1)} collective-permute-done((f32[14,768]{1,0:T(8,128)S(1)}, f32[14,768]{1,0:T(8,128)S(1)}, u32[]{:S(2)}, u32[]{:S(2)}) %collective-permute-start.27) | collective-permute-done | bytes 43040 | tf_op jit(solution)/shard_map/ppermute | solution.py:605
  336.6 20.0 %collective-permute-done.29.refs_1_ = bf16[4,48,768]{2,1,0:T(8,128)(2,1)S(1)} collective-permute-done((bf16[4,48,768]{2,1,0:T(8,128)(2,1)S(1)}, bf16[4,48,768]{2,1,0:T(8,128)(2,1)S(1)}, u32[]{:S(2)}, u32[]{:S(2)}) %collective-permute-start.29) | collective-permute-done | bytes 294944 | tf_op jit(solution)/shard_map/ppermute | solution.py:608
  384.1 6.2 %collective-permute-done.38 = f32[14,768]{1,0:T(8,128)S(1)} collective-permute-done((f32[14,768]{1,0:T(8,128)S(1)}, f32[14,768]{1,0:T(8,128)S(1)}, u32[]{:S(2)}, u32[]{:S(2)}) %collective-permute-start.38) | collective-permute-done | bytes 43040 | tf_op jit(solution)/shard_map/ppermute | solution.py:608
  390.3 14.2 %collective-permute-done.39.refs_1_ = bf16[1,768,768]{2,1,0:T(8,128)(2,1)S(1)} collective-permute-done((bf16[1,768,768]{2,1,0:T(8,128)(2,1)S(1)}, bf16[1,768,768]{2,1,0:T(8,128)(2,1)S(1)}, u32[]{:S(2)}, u32[]{:S(2)}) %collective-permute-start.39) | collective-permute-done | bytes 1179680 | tf_op jit(solution)/shard_map/ppermute | solution.py:605
  407.4 8.9 %collective-permute-done.41 = bf16[4,48,768]{2,1,0:T(8,128)(2,1)S(1)} collective-permute-done((bf16[4,48,768]{2,1,0:T(8,128)(2,1)S(1)}, bf16[4,48,768]{2,1,0:T(8,128)(2,1)S(1)}, u32[]{:S(2)}, u32[]{:S(2)}) %collective-permute-start.41) | collective-permute-done | bytes 294944 | tf_op jit(solution)/shard_map/ppermute | solution.py:608
  432.0 7.5 %collective-permute-done.48.refs_1_ = bf16[4,96,768]{2,1,0:T(8,128)(2,1)S(1)} collective-permute-done((bf16[4,96,768]{2,1,0:T(8,128)(2,1)S(1)}, bf16[4,96,768]{2,1,0:T(8,128)(2,1)S(1)}, u32[]{:S(2)}, u32[]{:S(2)}) %collective-permute-start.48) | collective-permute-done | bytes 589856 | tf_op jit(solution)/shard_map/ppermute | solution.py:605
  445.7 6.6 %shard_map.364 = (f32[768,768]{1,0:T(8,128)}, f32[768,768]{1,0:T(8,128)}, f32[768,768]{1,0:T(8,128)}, f32[768,768]{1,0:T(8,128)}) custom-call(s32[3]{0:T(128)S(1)} %copy-done.15, bf16[4,96,768]{2,1,0:T(8,128)(2,1)S(1)} %maximum_select_fusion.5.refs_0_, bf16[4,96,768]{2,1,0:T(8,128)(2,1)S(1)} %collective-permute-done.48.refs_1_, ...), custom_call_target="tpu_custom_call" | custom-call | flops 1 | bytes 1 | tf_op jit(solution)/shard_map/pallas_call | solution.py:61
  (280 shorter events, 173.9 us)
Async XLA Ops:
  0.7 22.5 %collective-permute-start = (s32[3]{0:T(128)}, s32[3]{0:T(128)S(1)}, u32[]{:S(2)}, u32[]{:S(2)}) collective-permute-start(s32[3]{0:T(128)} %param.24), channel_id=1, source_target_pairs={{0,4},{4,0},{8,12},{12,8},{16,20},{20,16},{24,28},{28,24},{1,5},{5... | collective-permute-start | bytes 44 | tf_op jit(solution)/shard_map/ppermute | solution.py:605
  8.5 21.8 %collective-permute-start.1 = (bf16[512,768]{1,0:T(8,128)(2,1)S(1)}, bf16[512,768]{1,0:T(8,128)(2,1)}, u32[]{:S(2)}, u32[]{:S(2)}) collective-permute-start(bf16[512,768]{1,0:T(8,128)(2,1)S(1)} %get-tuple-element.200), channel_id=1, source_target_pairs={{0,0},{1,4},{2,1},{3,5},{4,2},{5,6},{6,3},{7,7},{8,8},{9,12},{10,9... | collective-permute-start | bytes 2359304 | tf_op jit(solution)/shard_map/ppermute | solution.py:620
  10.2 39.7 %collective-permute-start.2 = (bf16[512,768]{1,0:T(8,128)(2,1)S(1)}, bf16[512,768]{1,0:T(8,128)(2,1)}, u32[]{:S(2)}, u32[]{:S(2)}) collective-permute-start(bf16[512,768]{1,0:T(8,128)(2,1)S(1)} %get-tuple-element.204), channel_id=1, source_target_pairs={{0,1},{1,5},{2,0},{3,4},{4,3},{5,7},{6,2},{7,6},{8,9},{9,13},{10,8... | collective-permute-start | bytes 2359304 | tf_op jit(solution)/shard_map/ppermute | solution.py:620
  60.0 45.7 %collective-permute-start.5 = (bf16[384,768]{1,0:T(8,128)(2,1)S(1)}, bf16[384,768]{1,0:T(8,128)(2,1)S(1)}, u32[]{:S(2)}, u32[]{:S(2)}) collective-permute-start(bf16[384,768]{1,0:T(8,128)(2,1)S(1)} %copy-done.21), channel_id=1, source_target_pairs={{0,0},{1,4},{2,1},{3,5},{4,2},{5,6},{6,3},{7,7},{8,8},{9,12},{10,9... | collective-permute-start | bytes 1769480 | tf_op jit(solution)/shard_map/ppermute | solution.py:620
  60.7 45.0 %collective-permute-start.6 = (bf16[384,768]{1,0:T(8,128)(2,1)S(1)}, bf16[384,768]{1,0:T(8,128)(2,1)S(1)}, u32[]{:S(2)}, u32[]{:S(2)}) collective-permute-start(bf16[384,768]{1,0:T(8,128)(2,1)S(1)} %get-tuple-element.215), channel_id=1, source_target_pairs={{0,1},{1,5},{2,0},{3,4},{4,3},{5,7},{6,2},{7,6},{8,9},{9,13},{10,8... | collective-permute-start | bytes 1769480 | tf_op jit(solution)/shard_map/ppermute | solution.py:620
  122.5 27.9 %collective-permute-start.8 = (bf16[2,2,768,768]{3,2,1,0:T(8,128)(2,1)}, bf16[2,2,768,768]{3,2,1,0:T(8,128)(2,1)}, u32[]{:S(2)}, u32[]{:S(2)}) collective-permute-start(bf16[2,2,768,768]{3,2,1,0:T(8,128)(2,1)} %get-tuple-element.224), channel_id=1, source_target_pairs={{0,4},{4,0},{8,12},{12,8},{16,20},{20,16},{24,28},{28,24},{1,5},{5... | collective-permute-start | bytes 14155784 | tf_op jit(solution)/shard_map/ppermute | solution.py:605
  122.6 42.4 %collective-permute-start.4 = (bf16[384,768]{1,0:T(8,128)(2,1)}, bf16[384,768]{1,0:T(8,128)(2,1)S(1)}, u32[]{:S(2)}, u32[]{:S(2)}) collective-permute-start(bf16[384,768]{1,0:T(8,128)(2,1)} %get-tuple-element.210), channel_id=1, source_target_pairs={{0,0},{4,1},{1,2},{5,3},{2,4},{6,5},{3,6},{7,7},{8,8},{12,9},{9,10... | collective-permute-start | bytes 1769480 | tf_op jit(solution)/shard_map/ppermute | solution.py:623
  124.3 40.7 %collective-permute-start.7 = (bf16[384,768]{1,0:T(8,128)(2,1)}, bf16[384,768]{1,0:T(8,128)(2,1)}, u32[]{:S(2)}, u32[]{:S(2)}) collective-permute-start(bf16[384,768]{1,0:T(8,128)(2,1)} %get-tuple-element.222), channel_id=1, source_target_pairs={{1,0},{5,1},{0,2},{4,3},{3,4},{7,5},{2,6},{6,7},{9,8},{13,9},{8,10... | collective-permute-start | bytes 1769480 | tf_op jit(solution)/shard_map/ppermute | solution.py:623
  158.0 32.0 %collective-permute-start.9 = (bf16[1,768,768]{2,1,0:T(8,128)(2,1)}, bf16[1,768,768]{2,1,0:T(8,128)(2,1)S(1)}, u32[]{:S(2)}, u32[]{:S(2)}) collective-permute-start(bf16[1,768,768]{2,1,0:T(8,128)(2,1)} %get-tuple-element.226), channel_id=1, source_target_pairs={{0,8},{4,12},{8,0},{12,4},{16,24},{20,28},{24,16},{28,20},{1,9},{5... | collective-permute-start | bytes 3538952 | tf_op jit(solution)/shard_map/ppermute | solution.py:605
  164.3 27.3 %collective-permute-start.10 = (bf16[1,768,768]{2,1,0:T(8,128)(2,1)}, bf16[1,768,768]{2,1,0:T(8,128)(2,1)}, u32[]{:S(2)}, u32[]{:S(2)}) collective-permute-start(bf16[1,768,768]{2,1,0:T(8,128)(2,1)} %get-tuple-element.228), channel_id=1, source_target_pairs={{0,16},{4,20},{8,24},{12,28},{16,0},{20,4},{24,8},{28,12},{1,17},{... | collective-permute-start | bytes 3538952 | tf_op jit(solution)/shard_map/ppermute | solution.py:605
  211.5 23.5 %collective-permute-start.15 = (bf16[2,512,768]{2,1,0:T(8,128)(2,1)}, bf16[2,512,768]{2,1,0:T(8,128)(2,1)S(1)}, u32[]{:S(2)}, u32[]{:S(2)}) collective-permute-start(bf16[2,512,768]{2,1,0:T(8,128)(2,1)} %get-tuple-element.258), channel_id=1, source_target_pairs={{0,4},{4,0},{8,12},{12,8},{16,20},{20,16},{24,28},{28,24},{1,5},{5... | collective-permute-start | bytes 4718600 | tf_op jit(solution)/shard_map/ppermute | solution.py:605
  211.6 23.4 %collective-permute-start.16 = (bf16[2,256,768]{2,1,0:T(8,128)(2,1)}, bf16[2,256,768]{2,1,0:T(8,128)(2,1)S(1)}, u32[]{:S(2)}, u32[]{:S(2)}) collective-permute-start(bf16[2,256,768]{2,1,0:T(8,128)(2,1)} %get-tuple-element.260), channel_id=1, source_target_pairs={{0,4},{4,0},{8,12},{12,8},{16,20},{20,16},{24,28},{28,24},{1,5},{5... | collective-permute-start | bytes 2359304 | tf_op jit(solution)/shard_map/ppermute | solution.py:605
  212.4 22.1 %collective-permute-start.12 = (bf16[1,384,768]{2,1,0:T(8,128)(2,1)S(1)}, bf16[1,384,768]{2,1,0:T(8,128)(2,1)S(1)}, u32[]{:S(2)}, u32[]{:S(2)}) collective-permute-start(bf16[1,384,768]{2,1,0:T(8,128)(2,1)S(1)} %copy-done.24), channel_id=1, source_target_pairs={{0,8},{4,12},{8,0},{12,4},{16,24},{20,28},{24,16},{28,20},{1,9},{5... | collective-permute-start | bytes 1769480 | tf_op jit(solution)/shard_map/ppermute | solution.py:605
  246.8 38.1 %collective-permute-start.19 = (bf16[3,384,768]{2,1,0:T(8,128)(2,1)}, bf16[3,384,768]{2,1,0:T(8,128)(2,1)S(1)}, u32[]{:S(2)}, u32[]{:S(2)}) collective-permute-start(bf16[3,384,768]{2,1,0:T(8,128)(2,1)} %get-tuple-element.270), channel_id=1, source_target_pairs={{0,4},{4,0},{8,12},{12,8},{16,20},{20,16},{24,28},{28,24},{1,5},{5... | collective-permute-start | bytes 5308424 | tf_op jit(solution)/shard_map/ppermute | solution.py:605
  246.9 38.0 %collective-permute-start.20 = (bf16[1,384,768]{2,1,0:T(8,128)(2,1)}, bf16[1,384,768]{2,1,0:T(8,128)(2,1)}, u32[]{:S(2)}, u32[]{:S(2)}) collective-permute-start(bf16[1,384,768]{2,1,0:T(8,128)(2,1)} %get-tuple-element.272), channel_id=1, source_target_pairs={{0,4},{4,0},{8,12},{12,8},{16,20},{20,16},{24,28},{28,24},{1,5},{5... | collective-permute-start | bytes 1769480 | tf_op jit(solution)/shard_map/ppermute | solution.py:605
  247.3 19.4 %collective-permute-start.14 = (bf16[1,384,768]{2,1,0:T(8,128)(2,1)}, bf16[1,384,768]{2,1,0:T(8,128)(2,1)S(1)}, u32[]{:S(2)}, u32[]{:S(2)}) collective-permute-start(bf16[1,384,768]{2,1,0:T(8,128)(2,1)} %copy-done.22), channel_id=1, source_target_pairs={{0,1},{1,0},{2,3},{3,2},{4,5},{5,4},{6,7},{7,6},{8,9},{9,8},{10,11... | collective-permute-start | bytes 1769480 | tf_op jit(solution)/shard_map/ppermute | solution.py:608
  252.4 22.2 %collective-permute-start.17 = (bf16[256,768]{1,0:T(8,128)(2,1)}, bf16[256,768]{1,0:T(8,128)(2,1)S(1)}, u32[]{:S(2)}, u32[]{:S(2)}) collective-permute-start(bf16[256,768]{1,0:T(8,128)(2,1)} %get-tuple-element.267), channel_id=1, source_target_pairs={{0,1},{1,0},{2,3},{3,2},{4,5},{5,4},{6,7},{7,6},{8,9},{9,8},{10,11... | collective-permute-start | bytes 1179656 | tf_op jit(solution)/shard_map/ppermute | solution.py:608
  290.2 19.5 %collective-permute-start.21 = (bf16[4,96,768]{2,1,0:T(8,128)(2,1)}, bf16[4,96,768]{2,1,0:T(8,128)(2,1)S(1)}, u32[]{:S(2)}, u32[]{:S(2)}) collective-permute-start(bf16[4,96,768]{2,1,0:T(8,128)(2,1)} %get-tuple-element.279), channel_id=1, source_target_pairs={{0,8},{4,12},{8,0},{12,4},{16,24},{20,28},{24,16},{28,20},{1,9},{5... | collective-permute-start | bytes 1769480 | tf_op jit(solution)/shard_map/ppermute | solution.py:605
  328.6 28.0 %collective-permute-start.31 = (bf16[1,384,768]{2,1,0:T(8,128)(2,1)S(1)}, bf16[1,384,768]{2,1,0:T(8,128)(2,1)S(1)}, u32[]{:S(2)}, u32[]{:S(2)}) collective-permute-start(bf16[1,384,768]{2,1,0:T(8,128)(2,1)S(1)} %maximum_select_fusion.3), channel_id=1, source_target_pairs={{0,1},{1,0},{2,3},{3,2},{4,5},{5,4},{6,7},{7,6},{8,9},{9,8},{10,11... | collective-permute-start | bytes 1769480 | tf_op jit(solution)/shard_map/ppermute | solution.py:608
  328.9 27.6 %collective-permute-start.29 = (bf16[4,48,768]{2,1,0:T(8,128)(2,1)S(1)}, bf16[4,48,768]{2,1,0:T(8,128)(2,1)S(1)}, u32[]{:S(2)}, u32[]{:S(2)}) collective-permute-start(bf16[4,48,768]{2,1,0:T(8,128)(2,1)S(1)} %get-tuple-element.303), channel_id=1, source_target_pairs={{0,1},{1,0},{2,3},{3,2},{4,5},{5,4},{6,7},{7,6},{8,9},{9,8},{10,11... | collective-permute-start | bytes 884744 | tf_op jit(solution)/shard_map/ppermute | solution.py:608
  332.6 28.9 %collective-permute-start.18 = (bf16[384,768]{1,0:T(8,128)(2,1)S(1)}, bf16[384,768]{1,0:T(8,128)(2,1)S(1)}, u32[]{:S(2)}, u32[]{:S(2)}) collective-permute-start(bf16[384,768]{1,0:T(8,128)(2,1)S(1)} %copy-done.49), channel_id=1, source_target_pairs={{0,0},{4,1},{1,2},{5,3},{2,4},{6,5},{3,6},{7,7},{8,8},{12,9},{9,10... | collective-permute-start | bytes 1769480 | tf_op jit(solution)/shard_map/ppermute | solution.py:623
  333.3 30.8 %collective-permute-start.32 = (bf16[384,768]{1,0:T(8,128)(2,1)}, bf16[384,768]{1,0:T(8,128)(2,1)S(1)}, u32[]{:S(2)}, u32[]{:S(2)}) collective-permute-start(bf16[384,768]{1,0:T(8,128)(2,1)} %get-tuple-element.312), channel_id=1, source_target_pairs={{1,0},{5,1},{0,2},{4,3},{3,4},{7,5},{2,6},{6,7},{9,8},{13,9},{8,10... | collective-permute-start | bytes 1769480 | tf_op jit(solution)/shard_map/ppermute | solution.py:623
  377.0 27.5 %collective-permute-start.39 = (bf16[1,768,768]{2,1,0:T(8,128)(2,1)S(1)}, bf16[1,768,768]{2,1,0:T(8,128)(2,1)S(1)}, u32[]{:S(2)}, u32[]{:S(2)}) collective-permute-start(bf16[1,768,768]{2,1,0:T(8,128)(2,1)S(1)} %maximum_select_fusion.1.refs_0_), channel_id=1, source_target_pairs={{0,8},{4,12},{8,0},{12,4},{16,24},{20,28},{24,16},{28,20},{1,9},{5... | collective-permute-start | bytes 3538952 | tf_op jit(solution)/shard_map/ppermute | solution.py:605
  378.5 27.7 %collective-permute-start.40 = (bf16[1,768,768]{2,1,0:T(8,128)(2,1)S(1)}, bf16[1,768,768]{2,1,0:T(8,128)(2,1)S(1)}, u32[]{:S(2)}, u32[]{:S(2)}) collective-permute-start(bf16[1,768,768]{2,1,0:T(8,128)(2,1)S(1)} %maximum_select_fusion.2.refs_0_), channel_id=1, source_target_pairs={{0,16},{4,20},{8,24},{12,28},{16,0},{20,4},{24,8},{28,12},{1,17},{... | collective-permute-start | bytes 3538952 | tf_op jit(solution)/shard_map/ppermute | solution.py:605
  (80 other events, 803.6 us)

commit v3 on v2

--- a/solution.py
+++ b/solution.py
@@ -55,9 +55,7 @@
     return value * cosine + swapped * sine
 
 
-def call(kernel, grid, scalars, inputs, outputs, scratch=(), flops=0, special=0, room=60, aliases=None):
-    moved = sum(array.size * array.dtype.itemsize for array, _ in inputs)
-    moved += sum(shape.size * shape.dtype.itemsize for shape, _ in outputs)
+def call(kernel, grid, scalars, inputs, outputs, scratch=(), cost=20, room=60, aliases=None):
     return pl.pallas_call(
         kernel,
         grid_spec=pltpu.PrefetchScalarGridSpec(
@@ -73,7 +71,7 @@
             dimension_semantics=("arbitrary",) * len(grid), vmem_limit_bytes=room << 20
         ),
         cost_estimate=pl.CostEstimate(
-            flops=1, transcendentals=0, bytes_accessed=1
+            flops=int(cost * 1e9), transcendentals=0, bytes_accessed=int(cost * 2e6)
         ),
     )(scalars, *[array for array, _ in inputs])
 
@@ -87,15 +85,27 @@
     return jax.ShapeDtypeStruct(shape, kind)
 
 
-def pack_kernel(order, blocks, first, second, sems):
+def ranks(sizes):
+    one, two, three = sizes[0], sizes[1], sizes[2]
+    longest = jnp.where((one >= two) & (one >= three), 0, jnp.where(two >= three, 1, 2))
+    return jnp.where(longest == 0, 1, 0), jnp.where(longest == 2, 1, 2), longest
+
+
+def pack_kernel(sizes, blocks, first, second, sems):
     half = blocks.shape[1]
+    pair = lax.axis_index("seq") // 2
+    low_own, high_own, longest = ranks(sizes)
     copies = []
     for number, target in enumerate((first, second)):
+        side = pair if number == 0 else 1 - pair
+        own = jnp.where(side == 0, low_own, high_own)
+        spots = [2 * own, 2 * own + 1, 2 * longest + side, 2 * longest + 1 - side]
         for place in range(target.shape[0] // half):
-            at = 4 * number + place
             copies.append(
                 pltpu.make_async_copy(
-                    blocks.at[order[at]], target.at[pl.ds(place * half, half)], sems.at[at]
+                    blocks.at[spots[place]],
+                    target.at[pl.ds(place * half, half)],
+                    sems.at[4 * number + place],
                 )
             )
     for copy in copies:
@@ -108,14 +118,14 @@
     return (array, pl.BlockSpec(memory_space=pl.ANY))
 
 
-def pack(array, order, parts):
+def pack(array, sizes, parts):
     seqs, span, width = array.shape
     half = span // 2
     message = fresh((parts * half, width), array.dtype)
     return call(
         pack_kernel,
         (1,),
-        order,
+        sizes,
         [in_place(array.reshape(2 * seqs, half, width))],
         [whole(message), whole(message)],
         [pltpu.SemaphoreType.DMA((8,))],
@@ -346,85 +356,73 @@
     to_second[span:, :] = value[2 * span + half :]
 
 
-def forward_kernel(
-    order, own, mixed, first, second, w_out, b_out, gain, shift, w_up, b_up, w_down, b_down,
-    middle, normed, hidden, slope, to_first, to_second, result,
+def hidden_tile(normed, cot, w_up, b_up, w_down, result, grad_normed, hidden, grad_hidden):
+    count = normed.shape[0]
+    step = min(count, 256)
+    total = jnp.zeros((1, w_up.shape[1]), full)
+    for row in range(0, count, step):
+        spot = slice(row, row + step)
+        hidden_in = matmul(normed[spot, :], w_up[...]) + b_up[...]
+        back = matmul_right(cot[spot, :], w_down[...])
+        share = 0.5 * (1.0 + lax.erf(hidden_in * 0.5**0.5))
+        item = (hidden_in * share).astype(low)
+        slope = share + hidden_in * jnp.exp(-0.5 * hidden_in * hidden_in) * 0.3989422804014327
+        grad_item = (back * slope).astype(low)
+        hidden[spot, :] = item
+        grad_hidden[spot, :] = grad_item
+        total += jnp.sum(grad_item.astype(full), axis=0, keepdims=True)
+        result[spot, :] += matmul(item, w_down[...])
+        grad_normed[spot, :] += matmul_right(grad_item, w_up[...])
+    return total
+
+
+def first_tiles_kernel(
+    tiles, own, mixed, first, second, cot_first, cot_second, w_out, b_out, gain, shift,
+    w_up, b_up, w_down, middle, result, grad_normed, normed, cot, sent, grad_b_up,
+    hidden, grad_hidden,
 ):
     span = first.shape[0] // 2
-    count = middle.shape[0]
 
     @pl.when(pl.program_id(0) == 0)
     def _():
+        cot[...] = join(cot_first[...], cot_second[...], span)
         attended = jnp.concatenate([own[...], mixed[...]], axis=0)
         value = join(first[...], second[...], span).astype(full)
         value = value + matmul(attended, w_out[...]) + b_out[...]
         middle[...] = value
-        result[...] = value + b_down[...]
         hat, _ = whiten(value)
         normed[...] = (hat * gain[...] + shift[...]).astype(low)
-
-    for row in range(0, count, span):
-        spot = slice(row, row + span)
-        hidden_in = matmul(normed[spot, :], w_up[...]) + b_up[...]
-        share = 0.5 * (1.0 + lax.erf(hidden_in * 0.5**0.5))
-        item = (hidden_in * share).astype(low)
-        hidden[spot, :] = item
-        slope[spot, :] = (
-            share + hidden_in * jnp.exp(-0.5 * hidden_in * hidden_in) * 0.3989422804014327
-        )
-        result[spot, :] += matmul(item, w_down[...])
-
-    @pl.when(pl.program_id(0) == pl.num_programs(0) - 1)
-    def _():
-        put_messages(to_first, to_second, result[...].astype(low))
-
-
-def backward_tile(hidden, slope, cot, normed, w_up, w_down, grad_normed, grad_hidden, target):
-    count = cot.shape[0]
-    step = min(count, 256)
-    total = jnp.zeros((1, w_up.shape[1]), full)
-    target[0] = matmul_left(hidden[...], cot[...]).astype(low)
-    for row in range(0, count, step):
-        spot = slice(row, row + step)
-        item = (matmul_right(cot[spot, :], w_down[...]) * slope[spot, :]).astype(low)
-        grad_hidden[spot, :] = item
-        total += jnp.sum(item.astype(full), axis=0, keepdims=True)
-        grad_normed[spot, :] += matmul_right(item, w_up[...])
-    target[1] = matmul_left(normed[: cot.shape[0], :], grad_hidden[...]).astype(low)
-    return total
-
-
-def backward_first_kernel(
-    tiles, hidden, slope, cot_first, cot_second, normed, w_up, w_down,
-    sent, grad_b_up, grad_normed, cot, grad_hidden,
+        result[...] = jnp.zeros_like(result)
+        grad_normed[...] = jnp.zeros_like(grad_normed)
+
+    grad_b_up[0:1, :] = hidden_tile(
+        normed, cot, w_up, b_up, w_down, result, grad_normed, hidden, grad_hidden
+    )
+    sent[0, ...] = matmul_left(hidden[...], cot[...]).astype(low)
+    sent[1, ...] = matmul_left(normed[...], grad_hidden[...]).astype(low)
+
+
+def last_tiles_kernel(
+    tiles, own, mixed, middle, result_in, grad_normed_in, normed, cot, w_out, gain, w_up, b_up,
+    w_down, b_down, kept, grad_b_up, to_first, to_second, grad_middle, grad_own, grad_mixed,
+    out_kept, out_sent, rows_out, result, grad_normed, hidden, grad_hidden, grad_out,
 ):
     @pl.when(pl.program_id(0) == 0)
     def _():
-        span = 2 * cot_first.shape[0] // 3
-        cot[...] = join(cot_first[...], cot_second[...], span)
-        grad_normed[...] = jnp.zeros_like(grad_normed)
-
-    grad_b_up[0:1, :] = backward_tile(
-        hidden, slope, cot, normed, w_up, w_down, grad_normed, grad_hidden, sent
-    )
-
-
-def backward_last_kernel(
-    tiles, hidden, slope, cot, normed, w_up, w_down, grad_normed_in, own, mixed, middle, w_out,
-    gain, kept, grad_b_up, grad_middle, grad_own, grad_mixed, out_kept, out_sent, rows_out,
-    grad_normed, grad_hidden, grad_out,
-):
-    @pl.when(pl.program_id(0) == 0)
-    def _():
+        result[...] = result_in[...]
         grad_normed[...] = grad_normed_in[...]
 
-    grad_b_up[0:1, :] = backward_tile(
-        hidden, slope, cot, normed, w_up, w_down, grad_normed, grad_hidden, kept
-    )
+    grad_b_up[0:1, :] = hidden_tile(
+        normed, cot, w_up, b_up, w_down, result, grad_normed, hidden, grad_hidden
+    )
+    kept[0, ...] = matmul_left(hidden[...], cot[...]).astype(low)
+    kept[1, ...] = matmul_left(normed[...], grad_hidden[...]).astype(low)
 
     @pl.when(pl.program_id(0) == pl.num_programs(0) - 1)
     def _():
-        hat, scale = whiten(middle[...])
+        value = middle[...]
+        put_messages(to_first, to_second, (value + result[...] + b_down[...]).astype(low))
+        hat, scale = whiten(value)
         grad = grad_normed[...]
         cot_full = cot[...].astype(full)
         rows_out[0:1, :] = jnp.sum(cot_full, axis=0, keepdims=True)
@@ -601,6 +599,9 @@
     pairs = width // PAIR
     square = (width, width)
 
+    def bit_of(bit):
+        return (group & bit) // bit
+
     def flip(value, bit):
         return lax.ppermute(value, "dp", [(i, i ^ bit) for i in range(groups)])
 
@@ -622,27 +623,10 @@
     def send_back(value, turn):
         return lax.ppermute(value, ("dp", "seq"), [(b, a) for a, b in route(turn)])
 
-    def ranks(sizes):
-        longest = jnp.argmax(sizes).astype(jnp.int32)
-        return (
-            jnp.where(longest == 0, 1, 0),
-            jnp.where(longest == 2, 1, 2),
-            longest,
-        )
-
+    first, second = pack(inputs, lengths, 4)
+    cot_first, cot_second = pack(after(cotangent, first), lengths, 3)
+    first, second = send(first, 0), send(second, 1)
     low_own, high_own, mixed_at = ranks(lengths)
-    near = jnp.where(pair == 0, low_own, high_own)
-    other = jnp.where(pair == 0, high_own, low_own)
-    index = jnp.arange(8)
-    turn = index // 4
-    spot = index % 4
-    chosen = jnp.where(turn == 0, near, other)
-    order = jnp.where(
-        spot < 2, 2 * chosen + spot, 2 * mixed_at + (turn ^ pair ^ (spot // 3))
-    )
-    first, second = pack(inputs, order, 4)
-    cot_first, cot_second = pack(after(cotangent, first), order, 3)
-    first, second = send(first, 0), send(second, 1)
     index = jnp.arange(2 * seqs)
     seq_at = index // 2
     part = index % 2
@@ -687,14 +671,36 @@
         return [whole(item) for item in items]
 
     extent = tokens + span
-    project_place = after(project_place, cot_first, own_place, mixed_place, cosine, sine)
+    bias_rows = [row(item) for item in (b_query, b_key, b_value, b_out, b_up, b_down)]
+    tiles_first = jnp.stack([2 * (1 - core), 2 * (1 - core) + 1])
+    tiles_last = jnp.stack([2 * core, 2 * core + 1, core])
+    orders = jnp.stack([core, bit_of(bits[0]), bit_of(bits[-1])])
+    core_only = core[None]
+    sides = [jnp.stack([bit_of(near), bit_of(far)]) for near, far in zip(bits, bits[::-1])]
+    sides += [side[None], pair[None]]
+    live = (depth * span + jnp.arange(span))[None, :] < lengths[:, None]
+    counts = jnp.sum(
+        jnp.where(live[:, :, None] & (predicted[:, :, None] == jnp.arange(CLASSES)), 1.0, 0.0),
+        axis=(0, 1),
+    )
+    counts = jnp.pad(counts[None], ((0, 0), (0, width - CLASSES)))
+    early = (
+        own_place, mixed_place, cosine, sine, bias_rows, gain1, shift1, gain2, shift2, tiles_first,
+        tiles_last, orders, core_only, sides, counts, order_back,
+    )
+    project_place, early, _ = lax.optimization_barrier((project_place, early, cot_first))
+    (
+        own_place, mixed_place, cosine, sine, bias_rows, gain1, shift1, gain2, shift2, tiles_first,
+        tiles_last, orders, core_only, sides, counts, order_back,
+    ) = early
+    b_query, b_key, b_value, b_out, b_up, b_down = bias_rows
     query, both, normed = call(
         project_kernel,
         (1,),
         project_place,
         wholes(
-            first, second, gain1, shift1, w_query, w_key, w_value, row(b_query), row(b_key),
-            row(b_value), cosine, sine,
+            first, second, gain1, shift1, w_query, w_key, w_value, b_query, b_key, b_value,
+            cosine, sine,
         ),
         wholes(
             fresh((tokens, width), low), fresh((2, extent, width), low), fresh((extent, width), low)
@@ -747,26 +753,14 @@
     def tall(array):
         return (array, pl.BlockSpec(square, lambda j, tiles: (tiles[j], 0)))
 
-    middle, normed2, hidden, slope, result_first, result_second = call(
-        forward_kernel,
-        (4,),
-        jnp.arange(4),
-        wholes(own, mixed, first, second, w_out, row(b_out), gain2, shift2)
-        + [
+    rows_fresh = fresh((8, width), full)
+
+    def tiles_in():
+        return [
             wide(w_up),
-            (row(b_up), pl.BlockSpec((1, width), lambda j, tiles: (0, tiles[j]))),
+            (b_up, pl.BlockSpec((1, width), lambda j, tiles: (0, tiles[j]))),
             tall(w_down),
-            whole(row(b_down)),
-        ],
-        wholes(fresh((tokens, width), full), fresh((tokens, width), low))
-        + [wide(fresh((tokens, hidden_width), low)), wide(fresh((tokens, hidden_width), full))]
-        + wholes(fresh((tokens // 2, width), low), fresh((tokens // 2, width), low)),
-        [pltpu.VMEM((tokens, width), full)],
-    )
-    result = [send_back(result_first, 0), send_back(result_second, 1)]
-
-    rows_fresh = fresh((8, width), full)
-    grad_scratch = [pltpu.VMEM((tokens, width), low)]
+        ]
 
     def tile_outs():
         return [
@@ -777,38 +771,43 @@
             (fresh((2, 8, width), full), pl.BlockSpec((None, 8, width), lambda j, _: (j, 0, 0))),
         ]
 
-    tiles_sent, b_up_sent, grad_normed2, cot = call(
-        backward_first_kernel,
+    tokens_full = fresh((tokens, width), full)
+    tokens_low = fresh((tokens, width), low)
+    tile_scratch = [pltpu.VMEM((tokens, width), low), pltpu.VMEM((tokens, width), low)]
+    middle, result, grad_normed2, normed2, cot, tiles_sent, b_up_sent = call(
+        first_tiles_kernel,
         (2,),
-        jnp.stack([2 * (1 - core), 2 * (1 - core) + 1]),
-        [wide(hidden), wide(slope)]
-        + wholes(cot_first, cot_second, normed2)
-        + [wide(w_up), tall(w_down)],
-        tile_outs() + wholes(fresh((tokens, width), full), fresh((tokens, width), low)),
-        grad_scratch,
+        tiles_first,
+        wholes(
+            own, mixed, first, second, cot_first, cot_second, w_out, b_out, gain2, shift2
+        )
+        + tiles_in(),
+        wholes(tokens_full, tokens_full, tokens_full, tokens_low, tokens_low) + tile_outs(),
+        tile_scratch,
     )
     tiles_received = flip(tiles_sent, 1)
     (
-        tiles_kept, b_up_kept, grad_middle, grad_own, grad_mixed, out_kept, out_sent, rows_middle,
+        tiles_kept, b_up_kept, result_first, result_second, grad_middle, grad_own, grad_mixed,
+        out_kept, out_sent, rows_middle,
     ) = call(
-        backward_last_kernel,
+        last_tiles_kernel,
         (2,),
-        jnp.stack([2 * core, 2 * core + 1, core]),
-        [wide(hidden), wide(slope)]
-        + wholes(cot, normed2)
-        + [wide(w_up), tall(w_down)]
-        + wholes(grad_normed2, own, mixed, middle, w_out, gain2),
+        tiles_last,
+        wholes(own, mixed, middle, result, grad_normed2, normed2, cot, w_out, gain2)
+        + tiles_in()
+        + wholes(b_down),
         tile_outs()
         + wholes(
-            fresh((tokens, width), full), fresh((2 * span, width), low), fresh((span, width), low),
+            fresh((tokens // 2, width), low), fresh((tokens // 2, width), low), tokens_full,
+            fresh((2 * span, width), low), fresh((span, width), low),
             fresh((1, width // 2, width), low), fresh((1, width // 2, width), low), rows_fresh,
         ),
-        [pltpu.VMEM((tokens, width), full), *grad_scratch, pltpu.VMEM(square, low)],
-    )
+        [pltpu.VMEM((tokens, width), full), pltpu.VMEM((tokens, width), full)]
+        + tile_scratch
+        + [pltpu.VMEM(square, low)],
+    )
+    result = [send_back(result_first, 0), send_back(result_second, 1)]
     out_received = flip(out_sent, 1)
-
-    def bit_of(bit):
-        return (group & bit) // bit
 
     def split(addends, at):
         rows = addends[0].shape[1] // 2
@@ -832,7 +831,7 @@
             jnp.concatenate([theirs, mine], axis=1),
         )
 
-    def stage(values, at, joined=False):
+    def stage(values, at, number, joined=False):
         lead, _, columns_in = values[0][0].shape
         sizes = [item[0].shape[1] for item in values]
         sizes = [sum(sizes)] if joined else sizes
@@ -843,7 +842,7 @@
         parts = call(
             functools.partial(stage_kernel, joined),
             (1,),
-            jnp.stack(at),
+            sides[number],
             wholes(*[part for item in values for part in item]),
             wholes(
                 *[fresh((lead, size // 2, columns_in), low) for size in sizes for _ in range(2)]
@@ -856,14 +855,14 @@
     def chain(parts, orders):
         for step in range(len(bits)):
             if step > 0:
-                parts = stage(values, [bit_of(order[step]) for order in orders])
+                parts = stage(values, [bit_of(order[step]) for order in orders], step)
             values = yield [
                 [keep, flip(give, order[step])] for (keep, give), order in zip(parts, orders)
             ]
         sizes = [item[0].shape[1] for item in values]
-        ((keep, give),) = stage(values, [side], joined=True)
+        ((keep, give),) = stage(values, [side], -2, joined=True)
         values = yield [[keep, flip_depth(give, 1)]]
-        ((keep, give),) = stage(values, [pair])
+        ((keep, give),) = stage(values, [pair], -1)
         (value,) = yield [[keep, flip_depth(give, 2)]]
         total = added(value)
         (value,) = yield [[total, flip_depth(total, 2)]]
@@ -879,8 +878,10 @@
             values = [
                 ordered(bit_of(order[step]), *item) for item, order in zip(values, orders)
             ]
-        values = yield [[item, flip(item, order[0])] for item, order in zip(values, orders)]
-        values = yield [item + [flip(part, 1) for part in item] for item in values]
+        values = yield [
+            [item, flip(item, order[0]), flip(item, 1)] for item, order in zip(values, orders)
+        ]
+        values = yield [[*item, flip(item[1], 1)] for item in values]
         yield values
 
     class Chain:
@@ -900,7 +901,6 @@
             item.left -= 1
 
     reverse = bits[::-1]
-    orders = jnp.stack([core, bit_of(bits[0]), bit_of(bits[-1])])
 
     part = fresh((1, width, width), low)
     parts = call(
@@ -912,7 +912,6 @@
         room=40,
     )
     tile_sum = Chain(tuple(parts[:2]), tuple(parts[2:]))
-    result = unpack(after(result[0], grad_middle), result[1], order_back, seqs)
 
     def attend_back(place, rows, at, pieces, grad, out, logsum, size, base, steps):
         given = pieces(size, base)
@@ -936,16 +935,17 @@
                 )
 
     query_mixed, mixed_here_grad, mixed_sibling_grad, far_grad, far_sibling_grad = attend_back(
-        after(mixed_place, *tile_sum.here(), result), span, 2, mixed_pieces, grad_mixed, mixed, mixed_logsum,
+        after(mixed_place, *tile_sum.here()), span, 2, mixed_pieces, grad_mixed, mixed, mixed_logsum,
         2 * PAIR, 0, pairs // 2,
     )
     far_received = flip(far_sibling_grad, 1)
     mixed_received = flip(mixed_sibling_grad, 1)
+    result = unpack(after(result[0], query_mixed), result[1], order_back, seqs)
     advance([tile_sum], query_mixed)
     far_both, grad_far = call(
         grad_far_kernel,
         (1,),
-        after(core[None], *tile_sum.here()),
+        after(core_only, result, *tile_sum.here()),
         wholes(far_grad, far_received, w_key, w_value),
         wholes(fresh((2, span, width), low), fresh((span, width), low)),
     )
@@ -960,7 +960,7 @@
     weight_kept, weight_sent, both_grad, rows_weight = call(
         weight_kernel,
         (1,),
-        after(core[None], *tile_sum.here()),
+        after(core_only, grad_far, *tile_sum.here()),
         wholes(
             normed, query_own, query_mixed, own_kept, own_received, mixed_here_grad,
             mixed_received, far_both,
@@ -973,50 +973,8 @@
     )
     weight_received = flip(weight_sent, 1)
     advance([tile_sum], rows_weight)
-    back_first, back_second, rows_input = call(
-        input_kernel,
-        (1,),
-        after(core[None], *tile_sum.here()),
-        wholes(
-            query_own, query_mixed, both_grad, grad_far, w_query, w_key, w_value, first, second,
-            gain1, grad_middle,
-        ),
-        wholes(fresh((tokens // 2, width), low), fresh((tokens // 2, width), low), rows_fresh),
-    )
-
-    live = (depth * span + jnp.arange(span))[None, :] < lengths[:, None]
-    counts = jnp.sum(
-        jnp.where(live[:, :, None] & (predicted[:, :, None] == jnp.arange(CLASSES)), 1.0, 0.0),
-        axis=(0, 1),
-    )
-    counts = jnp.zeros((1, width), full).at[0, :CLASSES].set(counts)
-    b_up_kept, b_up_sent = b_up_kept[:, 0], b_up_sent[:, 0]
-    rows_up = jnp.where(
-        core == 0,
-        jnp.concatenate([b_up_kept, b_up_sent]),
-        jnp.concatenate([b_up_sent, b_up_kept]),
-    )
-    small = jnp.concatenate(
-        [rows_middle[:4], rows_up, rows_weight[:3], rows_input[:2], counts], axis=0
-    )
-
-    class Small:
-        def __init__(self):
-            self.moves = [(flip, bit) for bit in (1, *bits)] + [(flip_depth, 1), (flip_depth, 2)]
-            self.steps = self
-            move, bit = self.moves.pop(0)
-            self.state = [[small, move(small, bit)]]
-            self.left = len(bits) + 3
-
-        def send(self, state):
-            total = state[0][0] + state[0][1]
-            if not self.moves:
-                return [[total]]
-            move, bit = self.moves.pop(0)
-            return [[total, move(total, bit)]]
-    back = [send_back(back_first, 0), send_back(back_second, 1)]
     weight_kept, weight_received, out_kept, out_received, _ = lax.optimization_barrier(
-        (weight_kept, weight_received, out_kept, out_received, rows_input)
+        (weight_kept, weight_received, out_kept, out_received, tile_sum.here())
     )
     part = fresh((4, width // 8, width), low)
     parts = call(
@@ -1028,11 +986,51 @@
         room=32,
     )
     weight_sum = Chain(tuple(parts[:2]), tuple(parts[2:]))
+    back_first, back_second, rows_input = call(
+        input_kernel,
+        (1,),
+        after(core_only, *tile_sum.here(), *weight_sum.here()),
+        wholes(
+            query_own, query_mixed, both_grad, grad_far, w_query, w_key, w_value, first, second,
+            gain1, grad_middle,
+        ),
+        wholes(fresh((tokens // 2, width), low), fresh((tokens // 2, width), low), rows_fresh),
+    )
+
+    b_up_kept, b_up_sent, _ = lax.optimization_barrier((b_up_kept, b_up_sent, rows_input))
+    b_up_kept, b_up_sent = b_up_kept[:, 0], b_up_sent[:, 0]
+    rows_up = jnp.where(
+        core == 0,
+        jnp.concatenate([b_up_kept, b_up_sent]),
+        jnp.concatenate([b_up_sent, b_up_kept]),
+    )
+    small = jnp.concatenate(
+        [rows_middle[:4], rows_up, rows_weight[:3], rows_input[:2], counts], axis=0
+    )
+
+    class Small:
+        def __init__(self):
+            self.moves = [(flip, bit) for bit in (1, *bits)] + [(flip_depth, 1), (flip_depth, 2)]
+            self.steps = self
+            move, bit = self.moves.pop(0)
+            self.state = [[small, move(small, bit)]]
+            self.left = len(bits) + 3
+
+        def send(self, state):
+            total = state[0][0] + state[0][1]
+            if not self.moves:
+                return [[total]]
+            move, bit = self.moves.pop(0)
+            return [[total, move(total, bit)]]
+    advance([tile_sum, weight_sum], rows_input)
     small_sum = Small()
-    for _ in range(3):
+    while tile_sum.left > 2:
         advance([weight_sum, small_sum, tile_sum])
-    grad_inputs = unpack(after(back[0], *weight_sum.here()), back[1], order_back, seqs)
-    advance([weight_sum, small_sum, tile_sum], grad_inputs)
+    advance([weight_sum, small_sum])
+    back_first, back_second, _ = lax.optimization_barrier(
+        (back_first, back_second, weight_sum.here())
+    )
+    back = [send_back(back_first, 0), send_back(back_second, 1)]
     while tile_sum.left > 0:
         advance([weight_sum, small_sum, tile_sum])
     left, right = tile_sum.state
@@ -1050,12 +1048,11 @@
 
     grad_w_down = expand(left, 1, (hidden_width, width), lambda i, _: (i, 0))
     grad_w_up = expand(right, 2, (width, hidden_width), lambda i, _: (0, i))
-    advance([weight_sum, small_sum], grad_w_down)
-    advance([weight_sum, small_sum], grad_w_up)
-    gates = []
+    gates = [grad_w_down, grad_w_up]
     while weight_sum.left > 0 or small_sum.left > 0:
         advance([weight_sum, small_sum], *gates)
         gates = []
+    grad_inputs = unpack(back[0], back[1], order_back, seqs)
     left, right = weight_sum.state
     grad_w_query, grad_w_key, grad_w_value, grad_w_out = call(
         expand_mixed_kernel,

time: 459 us -> 386 us (0.84)
  waiting for transfers between devices: 150 us -> 111 us
  Pallas kernels: 177 us -> 161 us
  starting transfers between devices: 68.4 us -> 54.5 us
    ppermute x11, waiting for transfers between devices: 76.3 us -> 49.9 us  [flip_depth(): return lax.ppermute(value, 'seq', [(i, i ^ bit) for i in range(4)])]
    pallas_call x26 -> x25, Pallas kernels: 177 us -> 161 us  [call(): pl.pallas_call(kernel, grid_spec=pltpu.PrefetchScalarGridSpec(num_scalar_...]
    ppermute x35, starting transfers between devices: 36.7 us -> 26.2 us  [flip(): return lax.ppermute(value, 'dp', [(i, i ^ bit) for i in range(groups)])]
    ppermute x35, waiting for transfers between devices: 54.5 us -> 45.6 us  [flip(): return lax.ppermute(value, 'dp', [(i, i ^ bit) for i in range(groups)])]
    unnamed x100 -> x78, local copies, waits for them, and re-layouts: 16.7 us -> 13.1 us
  transfers between devices with their start and end apart: 54 -> 54, of which waited for: 22 -> 21; matrix products, arithmetic and copies ran while one was open for 7% -> 7% of each run, Pallas kernels for 26% -> 33%
where the time goes in v3:
time: 386 us; the launch traced here: 379 us
  Pallas kernels  161 us (42%)
  waiting for transfers between devices  111 us (29%)
  starting transfers between devices  54.5 us (14%)
  local copies, waits for them, and re-layouts  32 us (8%)
  other arithmetic  10.3 us (3%)
  between operations  9.61 us (2%)
    pallas_call x25, Pallas kernels, call(): pl.pallas_call(kernel, grid_spec=pltpu.PrefetchScalarGridSpec(num_scalar_...  161 us
    ppermute x11, waiting for transfers between devices, flip_depth(): return lax.ppermute(value, 'seq', [(i, i ^ bit) for i in range(4)])  49.9 us
    ppermute x35, waiting for transfers between devices, flip(): return lax.ppermute(value, 'dp', [(i, i ^ bit) for i in range(groups)])  45.6 us
    ppermute x35, starting transfers between devices, flip(): return lax.ppermute(value, 'dp', [(i, i ^ bit) for i in range(groups)])  26.2 us
    ppermute x4, waiting for transfers between devices, send(): return lax.ppermute(value, ('dp', 'seq'), route(turn))  15.8 us
    unnamed x78, local copies, waits for them, and re-layouts  13.1 us
    ppermute x11, starting transfers between devices, flip_depth(): return lax.ppermute(value, 'seq', [(i, i ^ bit) for i in range(4)])  12.7 us
    ppermute x4, starting transfers between devices, send(): return lax.ppermute(value, ('dp', 'seq'), route(turn))  8.87 us
  transfers between devices with their start and end apart: 54, of which 21 were waited for; matrix products, arithmetic and copies ran while one was open for 7% of the time, Pallas kernels for 33%

profile of v3, /device:TPU:0, one launch (start us, length us, event | category | flops | bytes accessed | tf_op | source)
XLA Modules:
  0.0 378.8 jit_solution(13238848813770842981)
XLA Ops:
  36.3 10.8 %collective-permute-done.2.second = bf16[512,768]{1,0:T(8,128)(2,1)} collective-permute-done((bf16[512,768]{1,0:T(8,128)(2,1)S(1)}, bf16[512,768]{1,0:T(8,128)(2,1)}, u32[]{:S(2)}, u32[]{:S(2)}) %collective-permute-start.2) | collective-permute-done | bytes 786464 | tf_op jit(solution)/shard_map/ppermute | solution.py:621
  47.1 10.1 %shard_map.341 = (bf16[768,768]{1,0:T(8,128)(2,1)}, bf16[2,1024,768]{2,1,0:T(8,128)(2,1)}, bf16[1024,768]{1,0:T(8,128)(2,1)}) custom-call(s32[6]{0:T(128)} %pad_add_fusion.place, bf16[512,768]{1,0:T(8,128)(2,1)} %collective-permute-done.1.first, bf16[512,768]{1,0:T(8,128)(2,1)} %collective-permute-done.2.second, f32[1,768]{1,0:T(1,128)} %reshape.383.gain, ...), custom_call_target="tpu_custom_call" | custom-call | flops 20000000000 | bytes 40000000 | tf_op jit(solution)/shard_map/pallas_call | solution.py:59
  63.2 7.8 %shard_map.342 = (bf16[512,768]{1,0:T(8,128)(2,1)}, f32[6,8,512]{2,1,0:T(8,128)}) custom-call(s32[7]{0:T(128)} %pad_add_fusion.1.place, bf16[768,768]{1,0:T(8,128)(2,1)} %get-tuple-element.228.query, bf16[2,1024,768]{2,1,0:T(8,128)(2,1)} %get-tuple-element.229.refs_0_.refs_2_, bf16[2,1024,768]{2,1,0:T(8,128)(2,1)} %collective-permute-done.3.refs_1_.refs_3_), custom_call_target="tpu_custom_call" | custom-call | flops 20000000000 | bytes 40000000 | tf_op jit(solution)/shard_map/pallas_call | solution.py:59
  71.0 10.5 %shard_map.343 = (bf16[256,768]{1,0:T(8,128)(2,1)}, f32[6,8,256]{2,1,0:T(8,128)}) custom-call(s32[11]{0:T(128)} %concatenate.138.place, bf16[768,768]{1,0:T(8,128)(2,1)} %get-tuple-element.228.query, bf16[2,1024,768]{2,1,0:T(8,128)(2,1)} %get-tuple-element.229.refs_0_.refs_2_, bf16[2,1024,768]{2,1,0:T(8,128)(2,1)} %collective-permute-done.3.refs_1_.refs_3_, ...), custom_call_target="tpu_custom_call" | custom-call | flops 20000000000 | bytes 40000000 | tf_op jit(solution)/shard_map/pallas_call | solution.py:59
  81.5 5.0 %collective-permute-done.5.cot_second = bf16[384,768]{1,0:T(8,128)(2,1)S(1)} collective-permute-done((bf16[384,768]{1,0:T(8,128)(2,1)S(1)}, bf16[384,768]{1,0:T(8,128)(2,1)S(1)}, u32[]{:S(2)}, u32[]{:S(2)}) %collective-permute-start.5) | collective-permute-done | bytes 589856 | tf_op jit(solution)/shard_map/ppermute | solution.py:621
  87.4 20.3 %shard_map.344 = (f32[768,768]{1,0:T(8,128)}, f32[768,768]{1,0:T(8,128)}, f32[768,768]{1,0:T(8,128)}, bf16[768,768]{1,0:T(8,128)(2,1)}, bf16[768,768]{1,0:T(8,12...) custom-call(s32[2]{0:T(128)} %get-tuple-element.234.tiles, ...), custom_call_target="tpu_custom_call" | custom-call | flops 20000000000 | bytes 40000000 | tf_op jit(solution)/shard_map/pallas_call | solution.py:59
  107.8 25.1 %shard_map.345 = (bf16[2,2,768,768]{3,2,1,0:T(8,128)(2,1)}, f32[2,8,768]{2,1,0:T(8,128)}, bf16[384,768]{1,0:T(8,128)(2,1)}, bf16[384,768]{1,0:T(8,128)(2,1)}, f3...) custom-call(s32[3]{0:T(128)} %get-tuple-element.217.tiles, ...), custom_call_target="tpu_custom_call" | custom-call | flops 20000000000 | bytes 40000000 | tf_op jit(solution)/shard_map/pallas_call | solution.py:59
  132.9 5.9 %collective-permute-start.6 = (bf16[384,768]{1,0:T(8,128)(2,1)}, bf16[384,768]{1,0:T(8,128)(2,1)}, u32[]{:S(2)}, u32[]{:S(2)}) collective-permute-start(bf16[384,768]{1,0:T(8,128)(2,1)} %get-tuple-element.248), channel_id=1, source_target_pairs={{0,0},{4,1},{1,2},{5,3},{2,4},{6,5},{3,6},{7,7},{8,8},{12,9},{9,10... | collective-permute-start | bytes 1769480 | tf_op jit(solution)/shard_map/ppermute | solution.py:624
  142.5 4.9 %shard_map.346 = (bf16[1,768,768]{2,1,0:T(8,128)(2,1)S(1)}, bf16[1,768,768]{2,1,0:T(8,128)(2,1)S(1)}, bf16[1,768,768]{2,1,0:T(8,128)(2,1)S(1)}, bf16[1,768,768]{2,1,0:T(8,128)(2,1)}) custom-call(s32[3]{0:T(128)S(1)} %get-tuple-element.380.order, bf16[2,2,768,768]{3,2,1,0:T(8,128)(2,1)S(1)} %copy-done.8, bf16[2,2,768,768]{3,2,1,0:T(8,128)(2,1)} %collective-permute-done.7.received), custom_call_target="tpu_custom_call" | custom-call | flops 20000000000 | bytes 40000000 | tf_op jit(solution)/shard_map/pallas_call | solution.py:59
  152.4 16.5 %shard_map.347 = (bf16[256,768]{1,0:T(8,128)(2,1)}, bf16[2,256,768]{2,1,0:T(8,128)(2,1)}, bf16[2,256,768]{2,1,0:T(8,128)(2,1)}, bf16[2,256,768]{2,1,0:T(8,128)(2,1)}, bf16[2,256,768]{2,1,0:T(8,128)(2,1)}) custom-call(s32[11]{0:T(128)} %concatenate.138.place, bf16[768,768]{1,0:T(8,128)(2,1)} %get-tuple-element.228.query, ...), custom_call_target="tpu_custom_call" | custom-call | flops 20000000000 | bytes 40000000 | tf_op jit(solution)/shard_map/pallas_call | solution.py:59
  172.5 5.5 %collective-permute-done.10.refs_3_ = bf16[1,768,768]{2,1,0:T(8,128)(2,1)S(1)} collective-permute-done((bf16[1,768,768]{2,1,0:T(8,128)(2,1)}, bf16[1,768,768]{2,1,0:T(8,128)(2,1)S(1)}, u32[]{:S(2)}, u32[]{:S(2)}) %collective-permute-start.10) | collective-permute-done | bytes 1179680 | tf_op jit(solution)/shard_map/ppermute | solution.py:606
  189.9 11.0 %shard_map.351 = (bf16[512,768]{1,0:T(8,128)(2,1)}, bf16[2,512,768]{2,1,0:T(8,128)(2,1)}, bf16[2,512,768]{2,1,0:T(8,128)(2,1)}) custom-call(s32[7]{0:T(128)} %pad_add_fusion.1.place, bf16[768,768]{1,0:T(8,128)(2,1)} %get-tuple-element.228.query, bf16[512,768]{1,0:T(8,128)(2,1)} %get-tuple-element.279.grad, bf16[512,768]{1,0:T(8,128)(2,1)} %get-tuple-element.230.own.mixed, ...), custom_call_target="tpu_custom_call" | custom-call | flops 20000000000 | bytes 40000000 | tf_op jit(solution)/shard_map/pallas_call | solution.py:59
  204.7 9.7 %shard_map.353 = (bf16[3,384,768]{2,1,0:T(8,128)(2,1)}, bf16[3,384,768]{2,1,0:T(8,128)(2,1)}, bf16[2,768,768]{2,1,0:T(8,128)(2,1)}, f32[8,768]{1,0:T(8,128)}) custom-call(s32[1]{0:T(128)} %bitcast.8.order.core, bf16[1024,768]{1,0:T(8,128)(2,1)} %get-tuple-element.290.normed, bf16[512,768]{1,0:T(8,128)(2,1)} %get-tuple-element.281.query_own, ...), custom_call_target="tpu_custom_call" | custom-call | flops 20000000000 | bytes 40000000 | tf_op jit(solution)/shard_map/pallas_call | solution.py:59
  225.4 4.7 %collective-permute-start.21 = (bf16[4,96,768]{2,1,0:T(8,128)(2,1)S(1)}, bf16[4,96,768]{2,1,0:T(8,128)(2,1)S(1)}, u32[]{:S(2)}, u32[]{:S(2)}) collective-permute-start(bf16[4,96,768]{2,1,0:T(8,128)(2,1)S(1)} %get-tuple-element.315), channel_id=1, source_target_pairs={{0,8},{4,12},{8,0},{12,4},{16,24},{20,28},{24,16},{28,20},{1,9},{5... | collective-permute-start | bytes 1769480 | tf_op jit(solution)/shard_map/ppermute | solution.py:606
  233.4 9.3 %shard_map.356 = (bf16[384,768]{1,0:T(8,128)(2,1)}, bf16[384,768]{1,0:T(8,128)(2,1)}, f32[8,768]{1,0:T(8,128)}) custom-call(s32[1]{0:T(128)} %bitcast.8.order.core, bf16[512,768]{1,0:T(8,128)(2,1)} %get-tuple-element.281.query_own, bf16[256,768]{1,0:T(8,128)(2,1)} %get-tuple-element.257.query_mixed, bf16[2,768,768]{2,1,0:T(8,128)(2,1)} %get-tuple-element.310.both, ...), custom_call_target="tpu_custom_call" | custom-call | flops 20000000000 | bytes 40000000 | tf_op jit(solution)/shard_map/pallas_call | solution.py:59
  256.5 5.8 %collective-permute-done.26 = bf16[1,192,768]{2,1,0:T(8,128)(2,1)} collective-permute-done((bf16[1,192,768]{2,1,0:T(8,128)(2,1)}, bf16[1,192,768]{2,1,0:T(8,128)(2,1)}, u32[]{:S(2)}, u32[]{:S(2)}) %collective-permute-start.26) | collective-permute-done | bytes 294944 | tf_op jit(solution)/shard_map/ppermute | solution.py:609
  270.2 15.1 %collective-permute-done.27.refs_1_ = bf16[4,48,768]{2,1,0:T(8,128)(2,1)S(1)} collective-permute-done((bf16[4,48,768]{2,1,0:T(8,128)(2,1)S(1)}, bf16[4,48,768]{2,1,0:T(8,128)(2,1)S(1)}, u32[]{:S(2)}, u32[]{:S(2)}) %collective-permute-start.27) | collective-permute-done | bytes 294944 | tf_op jit(solution)/shard_map/ppermute | solution.py:609
  288.9 12.5 %collective-permute-done.31 = f32[14,768]{1,0:T(8,128)S(1)} collective-permute-done((f32[14,768]{1,0:T(8,128)S(1)}, f32[14,768]{1,0:T(8,128)S(1)}, u32[]{:S(2)}, u32[]{:S(2)}) %collective-permute-start.31) | collective-permute-done | bytes 43040 | tf_op jit(solution)/shard_map/ppermute | solution.py:606
  308.9 9.2 %collective-permute-done.34 = bf16[4,24,768]{2,1,0:T(8,128)(2,1)S(1)} collective-permute-done((bf16[4,24,768]{2,1,0:T(8,128)(2,1)S(1)}, bf16[4,24,768]{2,1,0:T(8,128)(2,1)S(1)}, u32[]{:S(2)}, u32[]{:S(2)}) %collective-permute-start.34) | collective-permute-done | bytes 147488 | tf_op jit(solution)/shard_map/ppermute | solution.py:609
  318.3 4.9 %collective-permute-done.39 = f32[14,768]{1,0:T(8,128)S(1)} collective-permute-done((f32[14,768]{1,0:T(8,128)S(1)}, f32[14,768]{1,0:T(8,128)S(1)}, u32[]{:S(2)}, u32[]{:S(2)}) %collective-permute-start.39) | collective-permute-done | bytes 43040 | tf_op jit(solution)/shard_map/ppermute | solution.py:609
  323.1 7.7 %collective-permute-done.38 = bf16[4,48,768]{2,1,0:T(8,128)(2,1)S(1)} collective-permute-done((bf16[4,48,768]{2,1,0:T(8,128)(2,1)S(1)}, bf16[4,48,768]{2,1,0:T(8,128)(2,1)S(1)}, u32[]{:S(2)}, u32[]{:S(2)}) %collective-permute-start.38) | collective-permute-done | bytes 294944 | tf_op jit(solution)/shard_map/ppermute | solution.py:609
  335.4 6.6 %collective-permute-done.44 = bf16[4,48,768]{2,1,0:T(8,128)(2,1)S(1)} collective-permute-done((bf16[4,48,768]{2,1,0:T(8,128)(2,1)S(1)}, bf16[4,48,768]{2,1,0:T(8,128)(2,1)S(1)}, u32[]{:S(2)}, u32[]{:S(2)}) %collective-permute-start.44) | collective-permute-done | bytes 294944 | tf_op jit(solution)/shard_map/ppermute | solution.py:606
  349.4 9.2 %collective-permute-done.50.refs_5_ = bf16[4,96,768]{2,1,0:T(8,128)(2,1)S(1)} collective-permute-done((bf16[4,96,768]{2,1,0:T(8,128)(2,1)S(1)}, bf16[4,96,768]{2,1,0:T(8,128)(2,1)S(1)}, u32[]{:S(2)}, u32[]{:S(2)}) %collective-permute-start.50) | collective-permute-done | bytes 589856 | tf_op jit(solution)/shard_map/ppermute | solution.py:606
  371.8 6.5 %shard_map.363 = (f32[768,768]{1,0:T(8,128)}, f32[768,768]{1,0:T(8,128)}, f32[768,768]{1,0:T(8,128)}, f32[768,768]{1,0:T(8,128)}) custom-call(s32[3]{0:T(128)S(1)} %copy-done.3, bf16[4,96,768]{2,1,0:T(8,128)(2,1)S(1)} %maximum_select_fusion.5.refs_0_, bf16[4,96,768]{2,1,0:T(8,128)(2,1)S(1)} %collective-permute-done.48.refs_1_, ...), custom_call_target="tpu_custom_call" | custom-call | flops 20000000000 | bytes 40000000 | tf_op jit(solution)/shard_map/pallas_call | solution.py:59
  (251 shorter events, 134.4 us)
Async XLA Ops:
  0.7 25.9 %collective-permute-start = (s32[3]{0:T(128)}, s32[3]{0:T(128)}, u32[]{:S(2)}, u32[]{:S(2)}) collective-permute-start(s32[3]{0:T(128)} %sizes.3), channel_id=1, source_target_pairs={{0,4},{4,0},{8,12},{12,8},{16,20},{20,16},{24,28},{28,24},{1,5},{5... | collective-permute-start | bytes 44 | tf_op jit(solution)/shard_map/ppermute | solution.py:606
  5.8 30.5 %collective-permute-start.1 = (bf16[512,768]{1,0:T(8,128)(2,1)S(1)}, bf16[512,768]{1,0:T(8,128)(2,1)}, u32[]{:S(2)}, u32[]{:S(2)}) collective-permute-start(bf16[512,768]{1,0:T(8,128)(2,1)S(1)} %get-tuple-element.213), channel_id=1, source_target_pairs={{0,0},{1,4},{2,1},{3,5},{4,2},{5,6},{6,3},{7,7},{8,8},{9,12},{10,9... | collective-permute-start | bytes 2359304 | tf_op jit(solution)/shard_map/ppermute | solution.py:621
  7.3 39.7 %collective-permute-start.2 = (bf16[512,768]{1,0:T(8,128)(2,1)S(1)}, bf16[512,768]{1,0:T(8,128)(2,1)}, u32[]{:S(2)}, u32[]{:S(2)}) collective-permute-start(bf16[512,768]{1,0:T(8,128)(2,1)S(1)} %get-tuple-element.220), channel_id=1, source_target_pairs={{0,1},{1,5},{2,0},{3,4},{4,3},{5,7},{6,2},{7,6},{8,9},{9,13},{10,8... | collective-permute-start | bytes 2359304 | tf_op jit(solution)/shard_map/ppermute | solution.py:621
  57.2 24.3 %collective-permute-start.4 = (bf16[384,768]{1,0:T(8,128)(2,1)S(1)}, bf16[384,768]{1,0:T(8,128)(2,1)S(1)}, u32[]{:S(2)}, u32[]{:S(2)}) collective-permute-start(bf16[384,768]{1,0:T(8,128)(2,1)S(1)} %copy-done.7), channel_id=1, source_target_pairs={{0,0},{1,4},{2,1},{3,5},{4,2},{5,6},{6,3},{7,7},{8,8},{9,12},{10,9... | collective-permute-start | bytes 1769480 | tf_op jit(solution)/shard_map/ppermute | solution.py:621
  57.9 28.6 %collective-permute-start.5 = (bf16[384,768]{1,0:T(8,128)(2,1)S(1)}, bf16[384,768]{1,0:T(8,128)(2,1)S(1)}, u32[]{:S(2)}, u32[]{:S(2)}) collective-permute-start(bf16[384,768]{1,0:T(8,128)(2,1)S(1)} %get-tuple-element.237), channel_id=1, source_target_pairs={{0,1},{1,5},{2,0},{3,4},{4,3},{5,7},{6,2},{7,6},{8,9},{9,13},{10,8... | collective-permute-start | bytes 1769480 | tf_op jit(solution)/shard_map/ppermute | solution.py:621
  107.7 32.5 %collective-permute-start.7 = (bf16[2,2,768,768]{3,2,1,0:T(8,128)(2,1)}, bf16[2,2,768,768]{3,2,1,0:T(8,128)(2,1)}, u32[]{:S(2)}, u32[]{:S(2)}) collective-permute-start(bf16[2,2,768,768]{3,2,1,0:T(8,128)(2,1)} %get-tuple-element.251), channel_id=1, source_target_pairs={{0,4},{4,0},{8,12},{12,8},{16,20},{20,16},{24,28},{28,24},{1,5},{5... | collective-permute-start | bytes 14155784 | tf_op jit(solution)/shard_map/ppermute | solution.py:606
  132.9 36.1 %collective-permute-start.6 = (bf16[384,768]{1,0:T(8,128)(2,1)}, bf16[384,768]{1,0:T(8,128)(2,1)}, u32[]{:S(2)}, u32[]{:S(2)}) collective-permute-start(bf16[384,768]{1,0:T(8,128)(2,1)} %get-tuple-element.248), channel_id=1, source_target_pairs={{0,0},{4,1},{1,2},{5,3},{2,4},{6,5},{3,6},{7,7},{8,8},{12,9},{9,10... | collective-permute-start | bytes 1769480 | tf_op jit(solution)/shard_map/ppermute | solution.py:624
  138.8 30.2 %collective-permute-start.8 = (bf16[384,768]{1,0:T(8,128)(2,1)}, bf16[384,768]{1,0:T(8,128)(2,1)}, u32[]{:S(2)}, u32[]{:S(2)}) collective-permute-start(bf16[384,768]{1,0:T(8,128)(2,1)} %get-tuple-element.259), channel_id=1, source_target_pairs={{1,0},{5,1},{0,2},{4,3},{3,4},{7,5},{2,6},{6,7},{9,8},{13,9},{8,10... | collective-permute-start | bytes 1769480 | tf_op jit(solution)/shard_map/ppermute | solution.py:624
  138.8 83.6 %collective-permute-start.19 = (bf16[1,384,768]{2,1,0:T(8,128)(2,1)}, bf16[1,384,768]{2,1,0:T(8,128)(2,1)}, u32[]{:S(2)}, u32[]{:S(2)}) collective-permute-start(bf16[1,384,768]{2,1,0:T(8,128)(2,1)} %get-tuple-element.302), channel_id=1, source_target_pairs={{0,4},{4,0},{8,12},{12,8},{16,20},{20,16},{24,28},{28,24},{1,5},{5... | collective-permute-start | bytes 1769480 | tf_op jit(solution)/shard_map/ppermute | solution.py:606
  149.4 28.6 %collective-permute-start.10 = (bf16[1,768,768]{2,1,0:T(8,128)(2,1)}, bf16[1,768,768]{2,1,0:T(8,128)(2,1)S(1)}, u32[]{:S(2)}, u32[]{:S(2)}) collective-permute-start(bf16[1,768,768]{2,1,0:T(8,128)(2,1)} %get-tuple-element.265), channel_id=1, source_target_pairs={{0,16},{4,20},{8,24},{12,28},{16,0},{20,4},{24,8},{28,12},{1,17},{... | collective-permute-start | bytes 3538952 | tf_op jit(solution)/shard_map/ppermute | solution.py:606
  150.9 28.1 %collective-permute-start.9 = (bf16[1,768,768]{2,1,0:T(8,128)(2,1)S(1)}, bf16[1,768,768]{2,1,0:T(8,128)(2,1)S(1)}, u32[]{:S(2)}, u32[]{:S(2)}) collective-permute-start(bf16[1,768,768]{2,1,0:T(8,128)(2,1)S(1)} %get-tuple-element.264), channel_id=1, source_target_pairs={{0,8},{4,12},{8,0},{12,4},{16,24},{20,28},{24,16},{28,20},{1,9},{5... | collective-permute-start | bytes 3538952 | tf_op jit(solution)/shard_map/ppermute | solution.py:606
  169.0 35.7 %collective-permute-start.17 = (bf16[2,256,768]{2,1,0:T(8,128)(2,1)}, bf16[2,256,768]{2,1,0:T(8,128)(2,1)}, u32[]{:S(2)}, u32[]{:S(2)}) collective-permute-start(bf16[2,256,768]{2,1,0:T(8,128)(2,1)} %get-tuple-element.294), channel_id=1, source_target_pairs={{0,4},{4,0},{8,12},{12,8},{16,20},{20,16},{24,28},{28,24},{1,5},{5... | collective-permute-start | bytes 2359304 | tf_op jit(solution)/shard_map/ppermute | solution.py:606
  219.7 24.4 %collective-permute-start.20 = (bf16[1,192,768]{2,1,0:T(8,128)(2,1)S(1)}, bf16[1,192,768]{2,1,0:T(8,128)(2,1)S(1)}, u32[]{:S(2)}, u32[]{:S(2)}) collective-permute-start(bf16[1,192,768]{2,1,0:T(8,128)(2,1)S(1)} %get-tuple-element.314), channel_id=1, source_target_pairs={{0,2},{1,3},{2,0},{3,1},{4,6},{5,7},{6,4},{7,5},{8,10},{9,11},{10,... | collective-permute-start | bytes 884744 | tf_op jit(solution)/shard_map/ppermute | solution.py:609
  225.4 18.7 %collective-permute-start.21 = (bf16[4,96,768]{2,1,0:T(8,128)(2,1)S(1)}, bf16[4,96,768]{2,1,0:T(8,128)(2,1)S(1)}, u32[]{:S(2)}, u32[]{:S(2)}) collective-permute-start(bf16[4,96,768]{2,1,0:T(8,128)(2,1)S(1)} %get-tuple-element.315), channel_id=1, source_target_pairs={{0,8},{4,12},{8,0},{12,4},{16,24},{20,28},{24,16},{28,20},{1,9},{5... | collective-permute-start | bytes 1769480 | tf_op jit(solution)/shard_map/ppermute | solution.py:606
  263.8 21.6 %collective-permute-start.29 = (bf16[1,384,768]{2,1,0:T(8,128)(2,1)S(1)}, bf16[1,384,768]{2,1,0:T(8,128)(2,1)S(1)}, u32[]{:S(2)}, u32[]{:S(2)}) collective-permute-start(bf16[1,384,768]{2,1,0:T(8,128)(2,1)S(1)} %maximum_select_fusion.3), channel_id=1, source_target_pairs={{0,1},{1,0},{2,3},{3,2},{4,5},{5,4},{6,7},{7,6},{8,9},{9,8},{10,11... | collective-permute-start | bytes 1769480 | tf_op jit(solution)/shard_map/ppermute | solution.py:609
  264.1 21.3 %collective-permute-start.27 = (bf16[4,48,768]{2,1,0:T(8,128)(2,1)S(1)}, bf16[4,48,768]{2,1,0:T(8,128)(2,1)S(1)}, u32[]{:S(2)}, u32[]{:S(2)}) collective-permute-start(bf16[4,48,768]{2,1,0:T(8,128)(2,1)S(1)} %get-tuple-element.339), channel_id=1, source_target_pairs={{0,1},{1,0},{2,3},{3,2},{4,5},{5,4},{6,7},{7,6},{8,9},{9,8},{10,11... | collective-permute-start | bytes 884744 | tf_op jit(solution)/shard_map/ppermute | solution.py:609
  302.2 28.7 %collective-permute-start.42 = (bf16[1,768,768]{2,1,0:T(8,128)(2,1)S(1)}, bf16[1,768,768]{2,1,0:T(8,128)(2,1)S(1)}, u32[]{:S(2)}, u32[]{:S(2)}) collective-permute-start(bf16[1,768,768]{2,1,0:T(8,128)(2,1)S(1)} %maximum_select_fusion.2.refs_0_), channel_id=1, source_target_pairs={{0,16},{4,20},{8,24},{12,28},{16,0},{20,4},{24,8},{28,12},{1,17},{... | collective-permute-start | bytes 3538952 | tf_op jit(solution)/shard_map/ppermute | solution.py:606
  303.4 27.5 %collective-permute-start.43 = (bf16[1,768,768]{2,1,0:T(8,128)(2,1)S(1)}, bf16[1,768,768]{2,1,0:T(8,128)(2,1)S(1)}, u32[]{:S(2)}, u32[]{:S(2)}) collective-permute-start(bf16[1,768,768]{2,1,0:T(8,128)(2,1)S(1)} %maximum_select_fusion.2.refs_0_), channel_id=1, source_target_pairs={{0,4},{4,0},{8,12},{12,8},{16,20},{20,16},{24,28},{28,24},{1,5},{5... | collective-permute-start | bytes 3538952 | tf_op jit(solution)/shard_map/ppermute | solution.py:606
  303.9 28.4 %collective-permute-start.40 = (bf16[1,768,768]{2,1,0:T(8,128)(2,1)S(1)}, bf16[1,768,768]{2,1,0:T(8,128)(2,1)S(1)}, u32[]{:S(2)}, u32[]{:S(2)}) collective-permute-start(bf16[1,768,768]{2,1,0:T(8,128)(2,1)S(1)} %maximum_select_fusion.1.refs_0_), channel_id=1, source_target_pairs={{0,8},{4,12},{8,0},{12,4},{16,24},{20,28},{24,16},{28,20},{1,9},{5... | collective-permute-start | bytes 3538952 | tf_op jit(solution)/shard_map/ppermute | solution.py:606
  304.5 27.8 %collective-permute-start.41 = (bf16[1,768,768]{2,1,0:T(8,128)(2,1)S(1)}, bf16[1,768,768]{2,1,0:T(8,128)(2,1)S(1)}, u32[]{:S(2)}, u32[]{:S(2)}) collective-permute-start(bf16[1,768,768]{2,1,0:T(8,128)(2,1)S(1)} %maximum_select_fusion.1.refs_0_), channel_id=1, source_target_pairs={{0,4},{4,0},{8,12},{12,8},{16,20},{20,16},{24,28},{28,24},{1,5},{5... | collective-permute-start | bytes 3538952 | tf_op jit(solution)/shard_map/ppermute | solution.py:606
  334.6 29.1 %collective-permute-start.36 = (bf16[384,768]{1,0:T(8,128)(2,1)S(1)}, bf16[384,768]{1,0:T(8,128)(2,1)S(1)}, u32[]{:S(2)}, u32[]{:S(2)}) collective-permute-start(bf16[384,768]{1,0:T(8,128)(2,1)S(1)} %copy-done.35), channel_id=1, source_target_pairs={{0,0},{4,1},{1,2},{5,3},{2,4},{6,5},{3,6},{7,7},{8,8},{12,9},{9,10... | collective-permute-start | bytes 1769480 | tf_op jit(solution)/shard_map/ppermute | solution.py:624
  342.1 21.7 %collective-permute-start.37 = (bf16[384,768]{1,0:T(8,128)(2,1)S(1)}, bf16[384,768]{1,0:T(8,128)(2,1)S(1)}, u32[]{:S(2)}, u32[]{:S(2)}) collective-permute-start(bf16[384,768]{1,0:T(8,128)(2,1)S(1)} %copy-done.34), channel_id=1, source_target_pairs={{1,0},{5,1},{0,2},{4,3},{3,4},{7,5},{2,6},{6,7},{9,8},{13,9},{8,10... | collective-permute-start | bytes 1769480 | tf_op jit(solution)/shard_map/ppermute | solution.py:624
  344.1 19.0 %collective-permute-start.51 = (bf16[4,96,768]{2,1,0:T(8,128)(2,1)S(1)}, bf16[4,96,768]{2,1,0:T(8,128)(2,1)S(1)}, u32[]{:S(2)}, u32[]{:S(2)}) collective-permute-start(bf16[4,96,768]{2,1,0:T(8,128)(2,1)S(1)} %maximum_select_fusion.6.refs_4_), channel_id=1, source_target_pairs={{0,4},{4,0},{8,12},{12,8},{16,20},{20,16},{24,28},{28,24},{1,5},{5... | collective-permute-start | bytes 1769480 | tf_op jit(solution)/shard_map/ppermute | solution.py:606
  344.3 18.8 %collective-permute-start.48 = (bf16[4,96,768]{2,1,0:T(8,128)(2,1)S(1)}, bf16[4,96,768]{2,1,0:T(8,128)(2,1)S(1)}, u32[]{:S(2)}, u32[]{:S(2)}) collective-permute-start(bf16[4,96,768]{2,1,0:T(8,128)(2,1)S(1)} %maximum_select_fusion.5.refs_0_), channel_id=1, source_target_pairs={{0,8},{4,12},{8,0},{12,4},{16,24},{20,28},{24,16},{28,20},{1,9},{5... | collective-permute-start | bytes 1769480 | tf_op jit(solution)/shard_map/ppermute | solution.py:606
  (69 other events, 745.9 us)

commit v4 on v3

--- a/solution.py
+++ b/solution.py
@@ -91,21 +91,22 @@
     return jnp.where(longest == 0, 1, 0), jnp.where(longest == 2, 1, 2), longest
 
 
-def pack_kernel(sizes, blocks, first, second, sems):
+def pack_kernel(sizes, blocks, *refs):
+    *targets, sems = refs
     half = blocks.shape[1]
     pair = lax.axis_index("seq") // 2
     low_own, high_own, longest = ranks(sizes)
     copies = []
-    for number, target in enumerate((first, second)):
+    for number in range(2):
         side = pair if number == 0 else 1 - pair
         own = jnp.where(side == 0, low_own, high_own)
-        spots = [2 * own, 2 * own + 1, 2 * longest + side, 2 * longest + 1 - side]
-        for place in range(target.shape[0] // half):
+        near = (2 * own, 2 * own + 1, 2 * longest + side)
+        moves = [(spot, targets[number], place) for place, spot in enumerate(near)]
+        moves += [(2 * longest + 1 - side, target, 0) for target in targets[2 + number : 3 + number]]
+        for place, (spot, target, at) in enumerate(moves):
             copies.append(
                 pltpu.make_async_copy(
-                    blocks.at[spots[place]],
-                    target.at[pl.ds(place * half, half)],
-                    sems.at[4 * number + place],
+                    blocks.at[spot], target.at[pl.ds(at * half, half)], sems.at[4 * number + place]
                 )
             )
     for copy in copies:
@@ -118,18 +119,19 @@
     return (array, pl.BlockSpec(memory_space=pl.ANY))
 
 
-def pack(array, sizes, parts):
+def pack(array, sizes, far):
     seqs, span, width = array.shape
     half = span // 2
-    message = fresh((parts * half, width), array.dtype)
+    outs = [fresh((3 * half, width), array.dtype)] * 2
+    if far:
+        outs += [fresh((half, width), array.dtype)] * 2
     return call(
         pack_kernel,
         (1,),
         sizes,
         [in_place(array.reshape(2 * seqs, half, width))],
-        [whole(message), whole(message)],
+        [whole(out) for out in outs],
         [pltpu.SemaphoreType.DMA((8,))],
-        room=12,
     )
 
 
@@ -187,38 +189,50 @@
     place, first, second, gain, shift, w_query, w_key, w_value, b_query, b_key, b_value,
     cosine, sine, query, both, normed,
 ):
-    span = first.shape[0] // 2
+    span = 2 * first.shape[0] // 3
     half = span // 2
     for slot, message in enumerate((first, second)):
-        rows = [
-            slice(slot * span, (slot + 1) * span),
-            slice(2 * span + slot * half, 2 * span + (slot + 1) * half),
-            slice(3 * span + slot * half, 3 * span + (slot + 1) * half),
-        ]
-        parts = [slice(0, span), slice(span, span + half), slice(span + half, 2 * span)]
+        own = slice(slot * span, (slot + 1) * span)
+        mixed = slice(2 * span + slot * half, 2 * span + (slot + 1) * half)
         hat, _ = whiten(message[...].astype(full))
         item = (hat * gain[...] + shift[...]).astype(low)
-        starts = [(place[slot], span), (place[2 + slot], half), (place[4 + slot], half)]
-        at = [pl.ds(pl.multiple_of(start, half), size) for start, size in starts]
-        cos = jnp.concatenate([cosine[index, :] for index in at], axis=0)
-        sin = jnp.concatenate([sine[index, :] for index in at], axis=0)
-        for row, part in zip(rows, parts):
-            normed[row, :] = item[part]
+        normed[own, :] = item[:span]
+        normed[mixed, :] = item[span:]
+        at = pl.ds(pl.multiple_of(place[slot], half), span)
+        at_mixed = pl.ds(pl.multiple_of(place[2 + slot], half), half)
+        cos = jnp.concatenate([cosine[at, :], cosine[at_mixed, :]], axis=0)
+        sin = jnp.concatenate([sine[at, :], sine[at_mixed, :]], axis=0)
         raw = (matmul(item, w_key[...]) + b_key[...]).astype(low).astype(full)
         for index, turned in enumerate(turn_heads(raw, cos, sin)):
             spot = slice(index * PAIR, (index + 1) * PAIR)
-            for row, part in zip(rows, parts):
-                both[0, row, spot] = turned[part]
+            both[0, own, spot] = turned[:span]
+            both[0, mixed, spot] = turned[span:]
         raw = (matmul(item, w_value[...]) + b_value[...]).astype(low)
-        for row, part in zip(rows, parts):
-            both[1, row, :] = raw[part]
-        near = span + half
-        raw = (matmul(item[:near], w_query[...]) + b_query[...]).astype(low).astype(full)
-        for index, turned in enumerate(turn_heads(raw, cos[:near], sin[:near])):
+        both[1, own, :] = raw[:span]
+        both[1, mixed, :] = raw[span:]
+        raw = (matmul(item, w_query[...]) + b_query[...]).astype(low).astype(full)
+        for index, turned in enumerate(turn_heads(raw, cos, sin)):
             spot = slice(index * PAIR, (index + 1) * PAIR)
             turned = turned * low(HEAD**-0.5)
-            for row, part in zip(rows[:2], parts[:2]):
-                query[row, spot] = turned[part]
+            query[own, spot] = turned[:span]
+            query[mixed, spot] = turned[span:]
+
+
+def project_far_kernel(
+    place, first, second, gain, shift, w_key, w_value, b_key, b_value, cosine, sine, both, normed
+):
+    half = first.shape[0]
+    message = jnp.concatenate([first[...], second[...]], axis=0)
+    hat, _ = whiten(message.astype(full))
+    item = (hat * gain[...] + shift[...]).astype(low)
+    normed[...] = item
+    at = [pl.ds(pl.multiple_of(place[4 + slot], half), half) for slot in range(2)]
+    cos = jnp.concatenate([cosine[at[0], :], cosine[at[1], :]], axis=0)
+    sin = jnp.concatenate([sine[at[0], :], sine[at[1], :]], axis=0)
+    raw = (matmul(item, w_key[...]) + b_key[...]).astype(low).astype(full)
+    for index, turned in enumerate(turn_heads(raw, cos, sin)):
+        both[0, :, index * PAIR : (index + 1) * PAIR] = turned
+    both[1] = (matmul(item, w_value[...]) + b_value[...]).astype(low)
 
 
 def load_pieces(place, pieces, keys, values):
@@ -381,7 +395,7 @@
     w_up, b_up, w_down, middle, result, grad_normed, normed, cot, sent, grad_b_up,
     hidden, grad_hidden,
 ):
-    span = first.shape[0] // 2
+    span = 2 * first.shape[0] // 3
 
     @pl.when(pl.program_id(0) == 0)
     def _():
@@ -509,21 +523,22 @@
 
 
 def weight_kernel(
-    core, normed, query_own, query_mixed, own_kept, own_received, mixed_kept,
+    core, normed, normed_far, query_own, query_mixed, own_kept, own_received, mixed_kept,
     mixed_received, far, kept, sent, both, rows_out, grad_weight,
 ):
     item = jnp.concatenate([query_own[...], query_mixed[...]], axis=0)
     count = item.shape[0]
     rows_out[0:1, :] = jnp.sum(item.astype(full), axis=0, keepdims=True)
-    grad_weight[...] = matmul_left(normed[:count, :], item).astype(low)
+    grad_weight[...] = matmul_left(normed[...], item).astype(low)
     keep_core_half(core[0], grad_weight, kept.at[0:1], sent.at[0:1])
+    rows = jnp.concatenate([normed[...], normed_far[...]], axis=0)
     for index in range(2):
         own = own_kept[index].astype(full) + own_received[index].astype(full)
         mixed = mixed_kept[index].astype(full) + mixed_received[index].astype(full)
         item = jnp.concatenate([own.astype(low), mixed.astype(low), far[index]], axis=0)
         both[index] = item[:count]
         rows_out[1 + index : 2 + index, :] = jnp.sum(item.astype(full), axis=0, keepdims=True)
-        grad_weight[...] = matmul_left(normed[...], item).astype(low)
+        grad_weight[...] = matmul_left(rows, item).astype(low)
         keep_core_half(
             core[0], grad_weight, kept.at[1 + index : 2 + index], sent.at[1 + index : 2 + index]
         )
@@ -534,7 +549,7 @@
     core, query_own, query_mixed, both, far, w_query, w_key, w_value, first,
     second, gain, grad_middle, to_first, to_second, rows_out,
 ):
-    span = first.shape[0] // 2
+    span = 2 * first.shape[0] // 3
     grad_query = jnp.concatenate([query_own[...], query_mixed[...]], axis=0)
     grad = matmul_right(grad_query, w_query[...])
     for index, weight in enumerate((w_key, w_value)):
@@ -612,20 +627,28 @@
         moves = []
         for at in range(groups):
             for z in range(4):
-                to = (at & ~1) | (z & 1)
+                to = (at & ~1) | ((z & 1) ^ 1 ^ turn)
                 to_z = 2 * (at & 1) + (turn ^ (z >> 1))
                 moves.append((at * 4 + z, to * 4 + to_z))
         return moves
 
+    def cross(value):
+        moves = [
+            (at * 4 + z, (at ^ 1) * 4 + (z ^ 1)) for at in range(groups) for z in range(4)
+        ]
+        return lax.ppermute(value, ("dp", "seq"), moves)
+
     def send(value, turn):
         return lax.ppermute(value, ("dp", "seq"), route(turn))
 
     def send_back(value, turn):
         return lax.ppermute(value, ("dp", "seq"), [(b, a) for a, b in route(turn)])
 
-    first, second = pack(inputs, lengths, 4)
-    cot_first, cot_second = pack(after(cotangent, first), lengths, 3)
+    first, second, *far_rows = pack(inputs, lengths, True)
+    cot_first, cot_second = pack(after(cotangent, first), lengths, False)
     first, second = send(first, 0), send(second, 1)
+    first, second, far_rows = lax.optimization_barrier((first, second, far_rows))
+    far_rows = [send(item, turn) for turn, item in enumerate(far_rows)]
     low_own, high_own, mixed_at = ranks(lengths)
     index = jnp.arange(2 * seqs)
     seq_at = index // 2
@@ -642,16 +665,16 @@
 
     def starts(at_side, at_core):
         slots = jnp.arange(2)
-        quarter = 2 * (slots ^ at_side) + at_core
+        quarter = 2 * (slots ^ at_side) + (at_core ^ 1 ^ slots)
         return quarter * span, quarter * span + at_side * half
 
     own_at, mixed_start = starts(side, core)
     own_sibling, mixed_sibling = starts(side, 1 - core)
     far_start = own_at + (1 - side) * half
-    far_sibling = own_sibling + (1 - side) * half
+    far_sibling_start = own_sibling + (1 - side) * half
     own_place = jnp.concatenate([own_length[None], own_at, own_sibling, own_at])
     mixed_place = jnp.concatenate(
-        [mixed_length[None], mixed_start, mixed_sibling, far_start, far_sibling, mixed_start]
+        [mixed_length[None], mixed_start, mixed_sibling, far_start, far_sibling_start, mixed_start]
     )
     project_place = jnp.concatenate([own_at, mixed_start, far_start])
 
@@ -670,7 +693,6 @@
     def wholes(*items):
         return [whole(item) for item in items]
 
-    extent = tokens + span
     bias_rows = [row(item) for item in (b_query, b_key, b_value, b_out, b_up, b_down)]
     tiles_first = jnp.stack([2 * (1 - core), 2 * (1 - core) + 1])
     tiles_last = jnp.stack([2 * core, 2 * core + 1, core])
@@ -703,11 +725,20 @@
             cosine, sine,
         ),
         wholes(
-            fresh((tokens, width), low), fresh((2, extent, width), low), fresh((extent, width), low)
+            fresh((tokens, width), low), fresh((2, tokens, width), low), fresh((tokens, width), low)
         ),
     )
+    both, far_rows = lax.optimization_barrier((both, far_rows))
     both_sibling = flip(both, 1)
-    cot_first, cot_second, _ = lax.optimization_barrier((cot_first, cot_second, first))
+    far, normed_far = call(
+        project_far_kernel,
+        (1,),
+        after(project_place, query),
+        wholes(*far_rows, gain1, shift1, w_key, w_value, b_key, b_value, cosine, sine),
+        wholes(fresh((2, span, width), low), fresh((span, width), low)),
+    )
+    far_sibling = flip(far, 1)
+    cot_first, cot_second, _ = lax.optimization_barrier((cot_first, cot_second, far))
     cot_first, cot_second = send(cot_first, 0), send(cot_second, 1)
 
     def columns(array, rows, at, size=PAIR, base=0):
@@ -722,8 +753,8 @@
         return [
             columns(both, span, 2, *given),
             columns(both_sibling, span, 2, *given),
-            columns(both, span, 3, *given),
-            columns(both_sibling, span, 3, *given),
+            columns(far, span, 0, *given),
+            columns(far_sibling, span, 0, *given),
         ]
 
     def attend(place, rows, at, pieces):
@@ -744,7 +775,7 @@
             [pltpu.VMEM((count, size), low), pltpu.VMEM((count, size), low)],
                 )
 
-    own, own_logsum = attend(own_place, 2 * span, 0, own_pieces)
+    own, own_logsum = attend(after(own_place, far), 2 * span, 0, own_pieces)
     mixed, mixed_logsum = attend(after(mixed_place, own), span, 2, mixed_pieces)
 
     def wide(array):
@@ -949,7 +980,7 @@
         wholes(far_grad, far_received, w_key, w_value),
         wholes(fresh((2, span, width), low), fresh((span, width), low)),
     )
-    grad_far = flip_depth(grad_far, 1)
+    grad_far = cross(grad_far)
 
     query_own, own_kept, own_sent = attend_back(
         after(own_place, far_both), 2 * span, 0, own_pieces, grad_own, own, own_logsum, 2 * PAIR, 0,
@@ -962,7 +993,7 @@
         (1,),
         after(core_only, grad_far, *tile_sum.here()),
         wholes(
-            normed, query_own, query_mixed, own_kept, own_received, mixed_here_grad,
+            normed, normed_far, query_own, query_mixed, own_kept, own_received, mixed_here_grad,
             mixed_received, far_both,
         ),
         wholes(

time: 386 us -> 373 us (0.966)
  starting transfers between devices: 54.5 us -> 46.3 us
  waiting for transfers between devices: 111 us -> 103 us
  Pallas kernels: 161 us -> 166 us
    ppermute x4 -> x6, waiting for transfers between devices: 15.8 us -> 8.74 us  [send(): return lax.ppermute(value, ('dp', 'seq'), route(turn))]
    ppermute x4, starting transfers between devices: 6.77 us -> 1.58 us  [send_back(): return lax.ppermute(value, ('dp', 'seq'), [(b, a) for a, b in route(turn)])]
    pallas_call x25 -> x26, Pallas kernels: 161 us -> 166 us  [call(): pl.pallas_call(kernel, grid_spec=pltpu.PrefetchScalarGridSpec(num_scalar_...]
    ppermute x4 -> x6, starting transfers between devices: 8.87 us -> 7.02 us  [send(): return lax.ppermute(value, ('dp', 'seq'), route(turn))]
    ppermute x35 -> x36, waiting for transfers between devices: 45.6 us -> 43.9 us  [flip(): return lax.ppermute(value, 'dp', [(i, i ^ bit) for i in range(groups)])]
    ppermute x35 -> x36, starting transfers between devices: 26.2 us -> 25 us  [flip(): return lax.ppermute(value, 'dp', [(i, i ^ bit) for i in range(groups)])]
    ppermute x11 -> x10, waiting for transfers between devices: 49.9 us -> 50.8 us  [flip_depth(): return lax.ppermute(value, 'seq', [(i, i ^ bit) for i in range(4)])]
    unnamed x78 -> x86, local copies, waits for them, and re-layouts: 13.1 us -> 13.2 us
  transfers between devices with their start and end apart: 54 -> 57, of which waited for: 21 -> 23; matrix products, arithmetic and copies ran while one was open for 7% -> 7% of each run, Pallas kernels for 33% -> 38%
where the time goes in v4:
time: 373 us; the launch traced here: 367 us
  Pallas kernels  166 us (45%)
  waiting for transfers between devices  103 us (28%)
  starting transfers between devices  46.3 us (12%)
  local copies, waits for them, and re-layouts  32.6 us (9%)
  between operations  9.63 us (3%)
  other arithmetic  9.36 us (3%)
    pallas_call x26, Pallas kernels, call(): pl.pallas_call(kernel, grid_spec=pltpu.PrefetchScalarGridSpec(num_scalar_...  166 us
    ppermute x10, waiting for transfers between devices, flip_depth(): return lax.ppermute(value, 'seq', [(i, i ^ bit) for i in range(4)])  50.8 us
    ppermute x36, waiting for transfers between devices, flip(): return lax.ppermute(value, 'dp', [(i, i ^ bit) for i in range(groups)])  43.9 us
    ppermute x36, starting transfers between devices, flip(): return lax.ppermute(value, 'dp', [(i, i ^ bit) for i in range(groups)])  25 us
    unnamed x86, local copies, waits for them, and re-layouts  13.2 us
    ppermute x10, starting transfers between devices, flip_depth(): return lax.ppermute(value, 'seq', [(i, i ^ bit) for i in range(4)])  12.6 us
    ppermute x6, waiting for transfers between devices, send(): return lax.ppermute(value, ('dp', 'seq'), route(turn))  8.74 us
  transfers between devices with their start and end apart: 57, of which 23 were waited for; matrix products, arithmetic and copies ran while one was open for 7% of the time, Pallas kernels for 38%

profile of v4, /device:TPU:0, one launch (start us, length us, event | category | flops | bytes accessed | tf_op | source)
XLA Modules:
  0.0 367.3 jit_solution(4780146444835791698)
XLA Ops:
  37.9 8.7 %shard_map.341 = (bf16[768,768]{1,0:T(8,128)(2,1)}, bf16[2,768,768]{2,1,0:T(8,128)(2,1)}, bf16[768,768]{1,0:T(8,128)(2,1)}) custom-call(s32[6]{0:T(128)} %pad_add_fusion.place, bf16[384,768]{1,0:T(8,128)(2,1)} %copy-done.34, bf16[384,768]{1,0:T(8,128)(2,1)} %copy-done.35, f32[1,768]{1,0:T(1,128)} %reshape.383.gain, f32[1,768]{1,0:T(1,128)} %reshape.384.shift, ...), custom_call_target="tpu_custom_call" | custom-call | flops 20000000000 | bytes 40000000 | tf_op jit(solution)/shard_map/pallas_call | solution.py:59
  48.3 4.8 %shard_map.342 = (bf16[2,256,768]{2,1,0:T(8,128)(2,1)}, bf16[256,768]{1,0:T(8,128)(2,1)}) custom-call(s32[6]{0:T(128)} %pad_add_fusion.place, bf16[128,768]{1,0:T(8,128)(2,1)} %copy-done.41, bf16[128,768]{1,0:T(8,128)(2,1)} %copy-done.42, f32[1,768]{1,0:T(1,128)} %reshape.383.gain, f32[1,768]{1,0:T(1,128)} %reshape.384.shift, bf16[768,768]{1,0:T(8,128)(2,1)} %w_key.7, ...), custom_call_target="tpu_custom_call" | custom-call | flops 20000000000 | bytes 40000000 | tf_op jit(solution)/shard_map/pallas_call | solution.py:59
  56.7 7.9 %shard_map.343 = (bf16[512,768]{1,0:T(8,128)(2,1)}, f32[6,8,512]{2,1,0:T(8,128)}) custom-call(s32[7]{0:T(128)} %pad_add_fusion.1.place, bf16[768,768]{1,0:T(8,128)(2,1)} %get-tuple-element.245.query, bf16[2,768,768]{2,1,0:T(8,128)(2,1)} %get-tuple-element.254.refs_0_, bf16[2,768,768]{2,1,0:T(8,128)(2,1)} %copy-done.32), custom_call_target="tpu_custom_call" | custom-call | flops 20000000000 | bytes 40000000 | tf_op jit(solution)/shard_map/pallas_call | solution.py:59
  65.5 10.5 %shard_map.344 = (bf16[256,768]{1,0:T(8,128)(2,1)}, f32[6,8,256]{2,1,0:T(8,128)}) custom-call(s32[11]{0:T(128)} %concatenate.138.place, bf16[768,768]{1,0:T(8,128)(2,1)} %get-tuple-element.245.query, bf16[2,768,768]{2,1,0:T(8,128)(2,1)} %get-tuple-element.254.refs_0_, bf16[2,768,768]{2,1,0:T(8,128)(2,1)} %copy-done.32, ...), custom_call_target="tpu_custom_call" | custom-call | flops 20000000000 | bytes 40000000 | tf_op jit(solution)/shard_map/pallas_call | solution.py:59
  76.0 5.6 %collective-permute-done.8.cot_second = bf16[384,768]{1,0:T(8,128)(2,1)} collective-permute-done((bf16[384,768]{1,0:T(8,128)(2,1)}, bf16[384,768]{1,0:T(8,128)(2,1)}, u32[]{:S(2)}, u32[]{:S(2)}) %collective-permute-start.8) | collective-permute-done | bytes 589856 | tf_op jit(solution)/shard_map/ppermute | solution.py:642
  81.6 20.2 %shard_map.345 = (f32[768,768]{1,0:T(8,128)}, f32[768,768]{1,0:T(8,128)}, f32[768,768]{1,0:T(8,128)}, bf16[768,768]{1,0:T(8,128)(2,1)}, bf16[768,768]{1,0:T(8,12...) custom-call(s32[2]{0:T(128)} %get-tuple-element.259.tiles, ...), custom_call_target="tpu_custom_call" | custom-call | flops 20000000000 | bytes 40000000 | tf_op jit(solution)/shard_map/pallas_call | solution.py:59
  101.9 25.0 %shard_map.346 = (bf16[2,2,768,768]{3,2,1,0:T(8,128)(2,1)}, f32[2,8,768]{2,1,0:T(8,128)}, bf16[384,768]{1,0:T(8,128)(2,1)}, bf16[384,768]{1,0:T(8,128)(2,1)}, f3...) custom-call(s32[3]{0:T(128)} %get-tuple-element.230.tiles, ...), custom_call_target="tpu_custom_call" | custom-call | flops 20000000000 | bytes 40000000 | tf_op jit(solution)/shard_map/pallas_call | solution.py:59
  131.9 4.9 %shard_map.347 = (bf16[1,768,768]{2,1,0:T(8,128)(2,1)S(1)}, bf16[1,768,768]{2,1,0:T(8,128)(2,1)}, bf16[1,768,768]{2,1,0:T(8,128)(2,1)S(1)}, bf16[1,768,768]{2,1,0:T(8,128)(2,1)S(1)}) custom-call(s32[3]{0:T(128)S(1)} %get-tuple-element.406.order, bf16[2,2,768,768]{3,2,1,0:T(8,128)(2,1)S(1)} %copy-done.2, bf16[2,2,768,768]{3,2,1,0:T(8,128)(2,1)} %collective-permute-done.10.received), custom_call_target="tpu_custom_call" | custom-call | flops 20000000000 | bytes 40000000 | tf_op jit(solution)/shard_map/pallas_call | solution.py:59
  141.8 16.4 %shard_map.348 = (bf16[256,768]{1,0:T(8,128)(2,1)}, bf16[2,256,768]{2,1,0:T(8,128)(2,1)}, bf16[2,256,768]{2,1,0:T(8,128)(2,1)}, bf16[2,256,768]{2,1,0:T(8,128)(2,1)}, bf16[2,256,768]{2,1,0:T(8,128)(2,1)}) custom-call(s32[11]{0:T(128)} %concatenate.138.place, bf16[768,768]{1,0:T(8,128)(2,1)} %get-tuple-element.245.query, ...), custom_call_target="tpu_custom_call" | custom-call | flops 20000000000 | bytes 40000000 | tf_op jit(solution)/shard_map/pallas_call | solution.py:59
  161.8 5.1 %collective-permute-done.12.refs_1_ = bf16[1,768,768]{2,1,0:T(8,128)(2,1)S(1)} collective-permute-done((bf16[1,768,768]{2,1,0:T(8,128)(2,1)}, bf16[1,768,768]{2,1,0:T(8,128)(2,1)S(1)}, u32[]{:S(2)}, u32[]{:S(2)}) %collective-permute-start.12) | collective-permute-done | bytes 1179680 | tf_op jit(solution)/shard_map/ppermute | solution.py:621
  176.9 11.0 %shard_map.352 = (bf16[512,768]{1,0:T(8,128)(2,1)}, bf16[2,512,768]{2,1,0:T(8,128)(2,1)}, bf16[2,512,768]{2,1,0:T(8,128)(2,1)}) custom-call(s32[7]{0:T(128)} %pad_add_fusion.1.place, bf16[768,768]{1,0:T(8,128)(2,1)} %get-tuple-element.245.query, bf16[512,768]{1,0:T(8,128)(2,1)} %get-tuple-element.304.grad, bf16[512,768]{1,0:T(8,128)(2,1)} %get-tuple-element.255.own.mixed, ...), custom_call_target="tpu_custom_call" | custom-call | flops 20000000000 | bytes 40000000 | tf_op jit(solution)/shard_map/pallas_call | solution.py:59
  193.6 9.7 %shard_map.354 = (bf16[3,384,768]{2,1,0:T(8,128)(2,1)}, bf16[3,384,768]{2,1,0:T(8,128)(2,1)}, bf16[2,768,768]{2,1,0:T(8,128)(2,1)}, f32[8,768]{1,0:T(8,128)}) custom-call(s32[1]{0:T(128)} %bitcast.8.order.core, bf16[768,768]{1,0:T(8,128)(2,1)} %get-tuple-element.315.normed, bf16[256,768]{1,0:T(8,128)(2,1)} %get-tuple-element.316.normed_far, ...), custom_call_target="tpu_custom_call" | custom-call | flops 20000000000 | bytes 40000000 | tf_op jit(solution)/shard_map/pallas_call | solution.py:59
  207.7 6.1 %collective-permute-start.23 = (bf16[1,192,768]{2,1,0:T(8,128)(2,1)S(1)}, bf16[1,192,768]{2,1,0:T(8,128)(2,1)S(1)}, u32[]{:S(2)}, u32[]{:S(2)}) collective-permute-start(bf16[1,192,768]{2,1,0:T(8,128)(2,1)S(1)} %get-tuple-element.340), channel_id=1, source_target_pairs={{0,2},{1,3},{2,0},{3,1},{4,6},{5,7},{6,4},{7,5},{8,10},{9,11},{10,... | collective-permute-start | bytes 884744 | tf_op jit(solution)/shard_map/ppermute | solution.py:624
  216.8 5.1 %collective-permute-start.24 = (bf16[4,96,768]{2,1,0:T(8,128)(2,1)S(1)}, bf16[4,96,768]{2,1,0:T(8,128)(2,1)S(1)}, u32[]{:S(2)}, u32[]{:S(2)}) collective-permute-start(bf16[4,96,768]{2,1,0:T(8,128)(2,1)S(1)} %get-tuple-element.341), channel_id=1, source_target_pairs={{0,8},{4,12},{8,0},{12,4},{16,24},{20,28},{24,16},{28,20},{1,9},{5... | collective-permute-start | bytes 1769480 | tf_op jit(solution)/shard_map/ppermute | solution.py:621
  221.8 9.2 %shard_map.357 = (bf16[384,768]{1,0:T(8,128)(2,1)}, bf16[384,768]{1,0:T(8,128)(2,1)}, f32[8,768]{1,0:T(8,128)}) custom-call(s32[1]{0:T(128)} %bitcast.8.order.core, bf16[512,768]{1,0:T(8,128)(2,1)} %get-tuple-element.306.query_own, bf16[256,768]{1,0:T(8,128)(2,1)} %get-tuple-element.282.query_mixed, bf16[2,768,768]{2,1,0:T(8,128)(2,1)} %get-tuple-element.336.both, ...), custom_call_target="tpu_custom_call" | custom-call | flops 20000000000 | bytes 40000000 | tf_op jit(solution)/shard_map/pallas_call | solution.py:59
  242.8 8.4 %collective-permute-done.29 = bf16[1,192,768]{2,1,0:T(8,128)(2,1)} collective-permute-done((bf16[1,192,768]{2,1,0:T(8,128)(2,1)}, bf16[1,192,768]{2,1,0:T(8,128)(2,1)}, u32[]{:S(2)}, u32[]{:S(2)}) %collective-permute-start.29) | collective-permute-done | bytes 294944 | tf_op jit(solution)/shard_map/ppermute | solution.py:624
  259.1 14.5 %collective-permute-done.30.refs_1_ = bf16[4,48,768]{2,1,0:T(8,128)(2,1)S(1)} collective-permute-done((bf16[4,48,768]{2,1,0:T(8,128)(2,1)S(1)}, bf16[4,48,768]{2,1,0:T(8,128)(2,1)S(1)}, u32[]{:S(2)}, u32[]{:S(2)}) %collective-permute-start.30) | collective-permute-done | bytes 294944 | tf_op jit(solution)/shard_map/ppermute | solution.py:624
  277.4 11.6 %collective-permute-done.34 = f32[14,768]{1,0:T(8,128)S(1)} collective-permute-done((f32[14,768]{1,0:T(8,128)S(1)}, f32[14,768]{1,0:T(8,128)S(1)}, u32[]{:S(2)}, u32[]{:S(2)}) %collective-permute-start.34) | collective-permute-done | bytes 43040 | tf_op jit(solution)/shard_map/ppermute | solution.py:621
  296.8 8.4 %collective-permute-done.37 = bf16[4,24,768]{2,1,0:T(8,128)(2,1)S(1)} collective-permute-done((bf16[4,24,768]{2,1,0:T(8,128)(2,1)S(1)}, bf16[4,24,768]{2,1,0:T(8,128)(2,1)S(1)}, u32[]{:S(2)}, u32[]{:S(2)}) %collective-permute-start.37) | collective-permute-done | bytes 147488 | tf_op jit(solution)/shard_map/ppermute | solution.py:624
  305.4 4.9 %collective-permute-done.42 = f32[14,768]{1,0:T(8,128)S(1)} collective-permute-done((f32[14,768]{1,0:T(8,128)S(1)}, f32[14,768]{1,0:T(8,128)S(1)}, u32[]{:S(2)}, u32[]{:S(2)}) %collective-permute-start.42) | collective-permute-done | bytes 43040 | tf_op jit(solution)/shard_map/ppermute | solution.py:624
  310.2 8.1 %collective-permute-done.41 = bf16[4,48,768]{2,1,0:T(8,128)(2,1)S(1)} collective-permute-done((bf16[4,48,768]{2,1,0:T(8,128)(2,1)S(1)}, bf16[4,48,768]{2,1,0:T(8,128)(2,1)S(1)}, u32[]{:S(2)}, u32[]{:S(2)}) %collective-permute-start.41) | collective-permute-done | bytes 294944 | tf_op jit(solution)/shard_map/ppermute | solution.py:624
  322.8 6.4 %collective-permute-done.47 = bf16[4,48,768]{2,1,0:T(8,128)(2,1)S(1)} collective-permute-done((bf16[4,48,768]{2,1,0:T(8,128)(2,1)S(1)}, bf16[4,48,768]{2,1,0:T(8,128)(2,1)S(1)}, u32[]{:S(2)}, u32[]{:S(2)}) %collective-permute-start.47) | collective-permute-done | bytes 294944 | tf_op jit(solution)/shard_map/ppermute | solution.py:621
  338.1 8.4 %collective-permute-done.53.refs_5_ = bf16[4,96,768]{2,1,0:T(8,128)(2,1)S(1)} collective-permute-done((bf16[4,96,768]{2,1,0:T(8,128)(2,1)S(1)}, bf16[4,96,768]{2,1,0:T(8,128)(2,1)S(1)}, u32[]{:S(2)}, u32[]{:S(2)}) %collective-permute-start.53) | collective-permute-done | bytes 589856 | tf_op jit(solution)/shard_map/ppermute | solution.py:621
  360.3 6.5 %shard_map.364 = (f32[768,768]{1,0:T(8,128)}, f32[768,768]{1,0:T(8,128)}, f32[768,768]{1,0:T(8,128)}, f32[768,768]{1,0:T(8,128)}) custom-call(s32[3]{0:T(128)S(1)} %copy-done.1, bf16[4,96,768]{2,1,0:T(8,128)(2,1)S(1)} %maximum_select_fusion.5.refs_0_, bf16[4,96,768]{2,1,0:T(8,128)(2,1)S(1)} %collective-permute-done.51.refs_1_, ...), custom_call_target="tpu_custom_call" | custom-call | flops 20000000000 | bytes 40000000 | tf_op jit(solution)/shard_map/pallas_call | solution.py:59
  (266 shorter events, 130.4 us)
Async XLA Ops:
  0.7 23.2 %collective-permute-start = (s32[3]{0:T(128)}, s32[3]{0:T(128)S(1)}, u32[]{:S(2)}, u32[]{:S(2)}) collective-permute-start(s32[3]{0:T(128)} %sizes.3), channel_id=1, source_target_pairs={{0,4},{4,0},{8,12},{12,8},{16,20},{20,16},{24,28},{28,24},{1,5},{5... | collective-permute-start | bytes 44 | tf_op jit(solution)/shard_map/ppermute | solution.py:621
  4.6 29.0 %collective-permute-start.1 = (bf16[384,768]{1,0:T(8,128)(2,1)}, bf16[384,768]{1,0:T(8,128)(2,1)S(1)}, u32[]{:S(2)}, u32[]{:S(2)}) collective-permute-start(bf16[384,768]{1,0:T(8,128)(2,1)} %get-tuple-element.226), channel_id=1, source_target_pairs={{0,4},{1,0},{2,5},{3,1},{4,6},{5,2},{6,7},{7,3},{8,12},{9,8},{10,1... | collective-permute-start | bytes 1769480 | tf_op jit(solution)/shard_map/ppermute | solution.py:642
  4.8 31.1 %collective-permute-start.2 = (bf16[384,768]{1,0:T(8,128)(2,1)}, bf16[384,768]{1,0:T(8,128)(2,1)S(1)}, u32[]{:S(2)}, u32[]{:S(2)}) collective-permute-start(bf16[384,768]{1,0:T(8,128)(2,1)} %get-tuple-element.233), channel_id=1, source_target_pairs={{0,1},{1,5},{2,0},{3,4},{4,3},{5,7},{6,2},{7,6},{8,9},{9,13},{10,8... | collective-permute-start | bytes 1769480 | tf_op jit(solution)/shard_map/ppermute | solution.py:642
  53.0 23.0 %collective-permute-start.7 = (bf16[384,768]{1,0:T(8,128)(2,1)}, bf16[384,768]{1,0:T(8,128)(2,1)}, u32[]{:S(2)}, u32[]{:S(2)}) collective-permute-start(bf16[384,768]{1,0:T(8,128)(2,1)} %get-tuple-element.261), channel_id=1, source_target_pairs={{0,4},{1,0},{2,5},{3,1},{4,6},{5,2},{6,7},{7,3},{8,12},{9,8},{10,1... | collective-permute-start | bytes 1769480 | tf_op jit(solution)/shard_map/ppermute | solution.py:642
  53.5 28.1 %collective-permute-start.8 = (bf16[384,768]{1,0:T(8,128)(2,1)}, bf16[384,768]{1,0:T(8,128)(2,1)}, u32[]{:S(2)}, u32[]{:S(2)}) collective-permute-start(bf16[384,768]{1,0:T(8,128)(2,1)} %get-tuple-element.262), channel_id=1, source_target_pairs={{0,1},{1,5},{2,0},{3,4},{4,3},{5,7},{6,2},{7,6},{8,9},{9,13},{10,8... | collective-permute-start | bytes 1769480 | tf_op jit(solution)/shard_map/ppermute | solution.py:642
  101.8 27.8 %collective-permute-start.10 = (bf16[2,2,768,768]{3,2,1,0:T(8,128)(2,1)}, bf16[2,2,768,768]{3,2,1,0:T(8,128)(2,1)}, u32[]{:S(2)}, u32[]{:S(2)}) collective-permute-start(bf16[2,2,768,768]{3,2,1,0:T(8,128)(2,1)} %get-tuple-element.276), channel_id=1, source_target_pairs={{0,4},{4,0},{8,12},{12,8},{16,20},{20,16},{24,28},{28,24},{1,5},{5... | collective-permute-start | bytes 14155784 | tf_op jit(solution)/shard_map/ppermute | solution.py:621
  126.9 31.4 %collective-permute-start.9 = (bf16[384,768]{1,0:T(8,128)(2,1)}, bf16[384,768]{1,0:T(8,128)(2,1)}, u32[]{:S(2)}, u32[]{:S(2)}) collective-permute-start(bf16[384,768]{1,0:T(8,128)(2,1)} %get-tuple-element.273), channel_id=1, source_target_pairs={{4,0},{0,1},{5,2},{1,3},{6,4},{2,5},{7,6},{3,7},{12,8},{8,9},{13,1... | collective-permute-start | bytes 1769480 | tf_op jit(solution)/shard_map/ppermute | solution.py:645
  127.0 31.4 %collective-permute-start.11 = (bf16[384,768]{1,0:T(8,128)(2,1)}, bf16[384,768]{1,0:T(8,128)(2,1)}, u32[]{:S(2)}, u32[]{:S(2)}) collective-permute-start(bf16[384,768]{1,0:T(8,128)(2,1)} %get-tuple-element.284), channel_id=1, source_target_pairs={{1,0},{5,1},{0,2},{4,3},{3,4},{7,5},{2,6},{6,7},{9,8},{13,9},{8,10... | collective-permute-start | bytes 1769480 | tf_op jit(solution)/shard_map/ppermute | solution.py:645
  127.1 86.7 %collective-permute-start.22 = (bf16[1,384,768]{2,1,0:T(8,128)(2,1)}, bf16[1,384,768]{2,1,0:T(8,128)(2,1)}, u32[]{:S(2)}, u32[]{:S(2)}) collective-permute-start(bf16[1,384,768]{2,1,0:T(8,128)(2,1)} %get-tuple-element.328), channel_id=1, source_target_pairs={{0,4},{4,0},{8,12},{12,8},{16,20},{20,16},{24,28},{28,24},{1,5},{5... | collective-permute-start | bytes 1769480 | tf_op jit(solution)/shard_map/ppermute | solution.py:621
  138.8 28.1 %collective-permute-start.12 = (bf16[1,768,768]{2,1,0:T(8,128)(2,1)}, bf16[1,768,768]{2,1,0:T(8,128)(2,1)S(1)}, u32[]{:S(2)}, u32[]{:S(2)}) collective-permute-start(bf16[1,768,768]{2,1,0:T(8,128)(2,1)} %get-tuple-element.289), channel_id=1, source_target_pairs={{0,8},{4,12},{8,0},{12,4},{16,24},{20,28},{24,16},{28,20},{1,9},{5... | collective-permute-start | bytes 3538952 | tf_op jit(solution)/shard_map/ppermute | solution.py:621
  140.3 27.6 %collective-permute-start.13 = (bf16[1,768,768]{2,1,0:T(8,128)(2,1)S(1)}, bf16[1,768,768]{2,1,0:T(8,128)(2,1)S(1)}, u32[]{:S(2)}, u32[]{:S(2)}) collective-permute-start(bf16[1,768,768]{2,1,0:T(8,128)(2,1)S(1)} %get-tuple-element.290), channel_id=1, source_target_pairs={{0,16},{4,20},{8,24},{12,28},{16,0},{20,4},{24,8},{28,12},{1,17},{... | collective-permute-start | bytes 3538952 | tf_op jit(solution)/shard_map/ppermute | solution.py:621
  158.4 35.2 %collective-permute-start.20 = (bf16[2,256,768]{2,1,0:T(8,128)(2,1)}, bf16[2,256,768]{2,1,0:T(8,128)(2,1)}, u32[]{:S(2)}, u32[]{:S(2)}) collective-permute-start(bf16[2,256,768]{2,1,0:T(8,128)(2,1)} %get-tuple-element.320), channel_id=1, source_target_pairs={{0,4},{4,0},{8,12},{12,8},{16,20},{20,16},{24,28},{28,24},{1,5},{5... | collective-permute-start | bytes 2359304 | tf_op jit(solution)/shard_map/ppermute | solution.py:621
  207.7 24.8 %collective-permute-start.23 = (bf16[1,192,768]{2,1,0:T(8,128)(2,1)S(1)}, bf16[1,192,768]{2,1,0:T(8,128)(2,1)S(1)}, u32[]{:S(2)}, u32[]{:S(2)}) collective-permute-start(bf16[1,192,768]{2,1,0:T(8,128)(2,1)S(1)} %get-tuple-element.340), channel_id=1, source_target_pairs={{0,2},{1,3},{2,0},{3,1},{4,6},{5,7},{6,4},{7,5},{8,10},{9,11},{10,... | collective-permute-start | bytes 884744 | tf_op jit(solution)/shard_map/ppermute | solution.py:624
  216.8 17.8 %collective-permute-start.24 = (bf16[4,96,768]{2,1,0:T(8,128)(2,1)S(1)}, bf16[4,96,768]{2,1,0:T(8,128)(2,1)S(1)}, u32[]{:S(2)}, u32[]{:S(2)}) collective-permute-start(bf16[4,96,768]{2,1,0:T(8,128)(2,1)S(1)} %get-tuple-element.341), channel_id=1, source_target_pairs={{0,8},{4,12},{8,0},{12,4},{16,24},{20,28},{24,16},{28,20},{1,9},{5... | collective-permute-start | bytes 1769480 | tf_op jit(solution)/shard_map/ppermute | solution.py:621
  252.6 21.0 %collective-permute-start.32 = (bf16[1,384,768]{2,1,0:T(8,128)(2,1)S(1)}, bf16[1,384,768]{2,1,0:T(8,128)(2,1)S(1)}, u32[]{:S(2)}, u32[]{:S(2)}) collective-permute-start(bf16[1,384,768]{2,1,0:T(8,128)(2,1)S(1)} %maximum_select_fusion.3), channel_id=1, source_target_pairs={{0,1},{1,0},{2,3},{3,2},{4,5},{5,4},{6,7},{7,6},{8,9},{9,8},{10,11... | collective-permute-start | bytes 1769480 | tf_op jit(solution)/shard_map/ppermute | solution.py:624
  253.0 20.7 %collective-permute-start.30 = (bf16[4,48,768]{2,1,0:T(8,128)(2,1)S(1)}, bf16[4,48,768]{2,1,0:T(8,128)(2,1)S(1)}, u32[]{:S(2)}, u32[]{:S(2)}) collective-permute-start(bf16[4,48,768]{2,1,0:T(8,128)(2,1)S(1)} %get-tuple-element.365), channel_id=1, source_target_pairs={{0,1},{1,0},{2,3},{3,2},{4,5},{5,4},{6,7},{7,6},{8,9},{9,8},{10,11... | collective-permute-start | bytes 884744 | tf_op jit(solution)/shard_map/ppermute | solution.py:624
  289.5 28.8 %collective-permute-start.45 = (bf16[1,768,768]{2,1,0:T(8,128)(2,1)S(1)}, bf16[1,768,768]{2,1,0:T(8,128)(2,1)S(1)}, u32[]{:S(2)}, u32[]{:S(2)}) collective-permute-start(bf16[1,768,768]{2,1,0:T(8,128)(2,1)S(1)} %maximum_select_fusion.2.refs_0_), channel_id=1, source_target_pairs={{0,16},{4,20},{8,24},{12,28},{16,0},{20,4},{24,8},{28,12},{1,17},{... | collective-permute-start | bytes 3538952 | tf_op jit(solution)/shard_map/ppermute | solution.py:621
  290.5 27.8 %collective-permute-start.46 = (bf16[1,768,768]{2,1,0:T(8,128)(2,1)S(1)}, bf16[1,768,768]{2,1,0:T(8,128)(2,1)S(1)}, u32[]{:S(2)}, u32[]{:S(2)}) collective-permute-start(bf16[1,768,768]{2,1,0:T(8,128)(2,1)S(1)} %maximum_select_fusion.2.refs_0_), channel_id=1, source_target_pairs={{0,4},{4,0},{8,12},{12,8},{16,20},{20,16},{24,28},{28,24},{1,5},{5... | collective-permute-start | bytes 3538952 | tf_op jit(solution)/shard_map/ppermute | solution.py:621
  291.0 28.4 %collective-permute-start.43 = (bf16[1,768,768]{2,1,0:T(8,128)(2,1)S(1)}, bf16[1,768,768]{2,1,0:T(8,128)(2,1)S(1)}, u32[]{:S(2)}, u32[]{:S(2)}) collective-permute-start(bf16[1,768,768]{2,1,0:T(8,128)(2,1)S(1)} %maximum_select_fusion.1.refs_0_), channel_id=1, source_target_pairs={{0,8},{4,12},{8,0},{12,4},{16,24},{20,28},{24,16},{28,20},{1,9},{5... | collective-permute-start | bytes 3538952 | tf_op jit(solution)/shard_map/ppermute | solution.py:621
  291.6 27.8 %collective-permute-start.44 = (bf16[1,768,768]{2,1,0:T(8,128)(2,1)S(1)}, bf16[1,768,768]{2,1,0:T(8,128)(2,1)S(1)}, u32[]{:S(2)}, u32[]{:S(2)}) collective-permute-start(bf16[1,768,768]{2,1,0:T(8,128)(2,1)S(1)} %maximum_select_fusion.1.refs_0_), channel_id=1, source_target_pairs={{0,4},{4,0},{8,12},{12,8},{16,20},{20,16},{24,28},{28,24},{1,5},{5... | collective-permute-start | bytes 3538952 | tf_op jit(solution)/shard_map/ppermute | solution.py:621
  322.2 29.5 %collective-permute-start.39 = (bf16[384,768]{1,0:T(8,128)(2,1)S(1)}, bf16[384,768]{1,0:T(8,128)(2,1)S(1)}, u32[]{:S(2)}, u32[]{:S(2)}) collective-permute-start(bf16[384,768]{1,0:T(8,128)(2,1)S(1)} %copy-done.37), channel_id=1, source_target_pairs={{4,0},{0,1},{5,2},{1,3},{6,4},{2,5},{7,6},{3,7},{12,8},{8,9},{13,1... | collective-permute-start | bytes 1769480 | tf_op jit(solution)/shard_map/ppermute | solution.py:645
  329.2 22.5 %collective-permute-start.40 = (bf16[384,768]{1,0:T(8,128)(2,1)S(1)}, bf16[384,768]{1,0:T(8,128)(2,1)S(1)}, u32[]{:S(2)}, u32[]{:S(2)}) collective-permute-start(bf16[384,768]{1,0:T(8,128)(2,1)S(1)} %copy-done.36), channel_id=1, source_target_pairs={{1,0},{5,1},{0,2},{4,3},{3,4},{7,5},{2,6},{6,7},{9,8},{13,9},{8,10... | collective-permute-start | bytes 1769480 | tf_op jit(solution)/shard_map/ppermute | solution.py:645
  331.6 19.3 %collective-permute-start.54 = (bf16[4,96,768]{2,1,0:T(8,128)(2,1)S(1)}, bf16[4,96,768]{2,1,0:T(8,128)(2,1)S(1)}, u32[]{:S(2)}, u32[]{:S(2)}) collective-permute-start(bf16[4,96,768]{2,1,0:T(8,128)(2,1)S(1)} %maximum_select_fusion.6.refs_4_), channel_id=1, source_target_pairs={{0,4},{4,0},{8,12},{12,8},{16,20},{20,16},{24,28},{28,24},{1,5},{5... | collective-permute-start | bytes 1769480 | tf_op jit(solution)/shard_map/ppermute | solution.py:621
  332.5 18.5 %collective-permute-start.51 = (bf16[4,96,768]{2,1,0:T(8,128)(2,1)S(1)}, bf16[4,96,768]{2,1,0:T(8,128)(2,1)S(1)}, u32[]{:S(2)}, u32[]{:S(2)}) collective-permute-start(bf16[4,96,768]{2,1,0:T(8,128)(2,1)S(1)} %maximum_select_fusion.5.refs_0_), channel_id=1, source_target_pairs={{0,8},{4,12},{8,0},{12,4},{16,24},{20,28},{24,16},{28,20},{1,9},{5... | collective-permute-start | bytes 1769480 | tf_op jit(solution)/shard_map/ppermute | solution.py:621
  (76 other events, 792.9 us)

commit v5 on v4

--- a/solution.py
+++ b/solution.py
@@ -883,7 +883,7 @@
         )
         return [tuple(parts[2 * place : 2 * place + 2]) for place in range(len(sizes))]
 
-    def chain(parts, orders):
+    def chain(parts, orders, early):
         for step in range(len(bits)):
             if step > 0:
                 parts = stage(values, [bit_of(order[step]) for order in orders], step)
@@ -910,14 +910,18 @@
                 ordered(bit_of(order[step]), *item) for item, order in zip(values, orders)
             ]
         values = yield [
-            [item, flip(item, order[0]), flip(item, 1)] for item, order in zip(values, orders)
+            [item, flip(item, order[0])] + ([flip(item, 1)] if early else [])
+            for item, order in zip(values, orders)
         ]
-        values = yield [[*item, flip(item[1], 1)] for item in values]
+        values = yield [
+            [*item, flip(item[1], 1)] if early else [*item, flip(item[0], 1), flip(item[1], 1)]
+            for item in values
+        ]
         yield values
 
     class Chain:
-        def __init__(self, left, right):
-            self.steps = chain([left, right], [bits, reverse])
+        def __init__(self, left, right, early):
+            self.steps = chain([left, right], [bits, reverse], early)
             self.state = next(self.steps)
             self.left = 2 * len(bits) + 5
 
@@ -942,7 +946,7 @@
         wholes(part, part, part, part),
         room=40,
     )
-    tile_sum = Chain(tuple(parts[:2]), tuple(parts[2:]))
+    tile_sum = Chain(tuple(parts[:2]), tuple(parts[2:]), True)
 
     def attend_back(place, rows, at, pieces, grad, out, logsum, size, base, steps):
         given = pieces(size, base)
@@ -1016,7 +1020,7 @@
         wholes(part, part, part, part),
         room=32,
     )
-    weight_sum = Chain(tuple(parts[:2]), tuple(parts[2:]))
+    weight_sum = Chain(tuple(parts[:2]), tuple(parts[2:]), False)
     back_first, back_second, rows_input = call(
         input_kernel,
         (1,),
@@ -1079,9 +1083,16 @@
 
     grad_w_down = expand(left, 1, (hidden_width, width), lambda i, _: (i, 0))
     grad_w_up = expand(right, 2, (width, hidden_width), lambda i, _: (0, i))
-    gates = [grad_w_down, grad_w_up]
-    while weight_sum.left > 0 or small_sum.left > 0:
-        advance([weight_sum, small_sum], *gates)
+    while small_sum.left > 0:
+        advance([small_sum])
+    total = small_sum.state[0][0]
+    small = [total[at] for at in range(4)] + [total[4:8].reshape(-1)]
+    small += [total[at] for at in range(8, 13)]
+    small.append(total[13, :CLASSES].astype(jnp.int32))
+    small = lax.optimization_barrier(small)
+    gates = [grad_w_down, grad_w_up, *small]
+    while weight_sum.left > 0:
+        advance([weight_sum], *gates)
         gates = []
     grad_inputs = unpack(back[0], back[1], order_back, seqs)
     left, right = weight_sum.state
@@ -1093,28 +1104,26 @@
         [(fresh(square, full), pl.BlockSpec((width // 8, width), lambda i, _: (i, 0)))] * 4,
         room=32,
     )
-    small = small_sum.state[0][0]
-
     return (
         result,
         grad_inputs,
-        small[11],
-        small[12],
+        small[8],
+        small[9],
         grad_w_query,
-        small[8],
+        small[5],
         grad_w_key,
-        small[9],
+        small[6],
         grad_w_value,
-        small[10],
+        small[7],
         grad_w_out,
         small[1],
         small[2],
         small[3],
         grad_w_up,
-        small[4:8].reshape(-1),
+        small[4],
         grad_w_down,
         small[0],
-        small[13, :CLASSES].astype(jnp.int32),
+        small[10],
     )
 
 

time: 373 us -> 370 us (level)
  waiting for transfers between devices: 103 us -> 92 us
  other arithmetic: 9.36 us -> 13.1 us
    ppermute x36, waiting for transfers between devices: 43.9 us -> 32.1 us  [flip(): return lax.ppermute(value, 'dp', [(i, i ^ bit) for i in range(groups)])]
    unnamed x86 -> x94, local copies, waits for them, and re-layouts: 13.2 us -> 15 us
  transfers between devices with their start and end apart: 57 -> 57, of which waited for: 23 -> 23; matrix products, arithmetic and copies ran while one was open for 7% -> 8% of each run, Pallas kernels for 38% -> 39%
where the time goes in v5:
time: 370 us; the launch traced here: 365 us
  Pallas kernels  167 us (45%)
  waiting for transfers between devices  92 us (25%)
  starting transfers between devices  49.1 us (13%)
  local copies, waits for them, and re-layouts  34 us (9%)
  other arithmetic  13.1 us (4%)
  between operations  9.64 us (3%)
    pallas_call x26, Pallas kernels, call(): pl.pallas_call(kernel, grid_spec=pltpu.PrefetchScalarGridSpec(num_scalar_...  167 us
    ppermute x10, waiting for transfers between devices, flip_depth(): return lax.ppermute(value, 'seq', [(i, i ^ bit) for i in range(4)])  51 us
    ppermute x36, waiting for transfers between devices, flip(): return lax.ppermute(value, 'dp', [(i, i ^ bit) for i in range(groups)])  32.1 us
    ppermute x36, starting transfers between devices, flip(): return lax.ppermute(value, 'dp', [(i, i ^ bit) for i in range(groups)])  23 us
    ppermute x10, starting transfers between devices, flip_depth(): return lax.ppermute(value, 'seq', [(i, i ^ bit) for i in range(4)])  15.4 us
    unnamed x94, local copies, waits for them, and re-layouts  15 us
    ppermute x6, waiting for transfers between devices, send(): return lax.ppermute(value, ('dp', 'seq'), route(turn))  8.82 us
  transfers between devices with their start and end apart: 57, of which 23 were waited for; matrix products, arithmetic and copies ran while one was open for 8% of the time, Pallas kernels for 39%

profile of v5, /device:TPU:0, one launch (start us, length us, event | category | flops | bytes accessed | tf_op | source)
XLA Modules:
  0.0 365.0 jit_solution(6775140517651687140)
XLA Ops:
  37.9 8.7 %shard_map.341 = (bf16[768,768]{1,0:T(8,128)(2,1)}, bf16[2,768,768]{2,1,0:T(8,128)(2,1)}, bf16[768,768]{1,0:T(8,128)(2,1)}) custom-call(s32[6]{0:T(128)} %pad_add_fusion.place, bf16[384,768]{1,0:T(8,128)(2,1)} %copy-done.40, bf16[384,768]{1,0:T(8,128)(2,1)} %copy-done.41, f32[1,768]{1,0:T(1,128)} %reshape.383.gain, f32[1,768]{1,0:T(1,128)} %reshape.384.shift, ...), custom_call_target="tpu_custom_call" | custom-call | flops 20000000000 | bytes 40000000 | tf_op jit(solution)/shard_map/pallas_call | solution.py:59
  48.3 4.7 %shard_map.342 = (bf16[2,256,768]{2,1,0:T(8,128)(2,1)}, bf16[256,768]{1,0:T(8,128)(2,1)}) custom-call(s32[6]{0:T(128)} %pad_add_fusion.place, bf16[128,768]{1,0:T(8,128)(2,1)} %copy-done.45, bf16[128,768]{1,0:T(8,128)(2,1)} %copy-done.46, f32[1,768]{1,0:T(1,128)} %reshape.383.gain, f32[1,768]{1,0:T(1,128)} %reshape.384.shift, bf16[768,768]{1,0:T(8,128)(2,1)} %w_key.7, ...), custom_call_target="tpu_custom_call" | custom-call | flops 20000000000 | bytes 40000000 | tf_op jit(solution)/shard_map/pallas_call | solution.py:59
  56.7 7.8 %shard_map.343 = (bf16[512,768]{1,0:T(8,128)(2,1)}, f32[6,8,512]{2,1,0:T(8,128)}) custom-call(s32[7]{0:T(128)} %pad_add_fusion.1.place, bf16[768,768]{1,0:T(8,128)(2,1)} %get-tuple-element.254.query, bf16[2,768,768]{2,1,0:T(8,128)(2,1)} %get-tuple-element.263.refs_0_, bf16[2,768,768]{2,1,0:T(8,128)(2,1)} %copy-done.38), custom_call_target="tpu_custom_call" | custom-call | flops 20000000000 | bytes 40000000 | tf_op jit(solution)/shard_map/pallas_call | solution.py:59
  65.4 10.5 %shard_map.344 = (bf16[256,768]{1,0:T(8,128)(2,1)}, f32[6,8,256]{2,1,0:T(8,128)}) custom-call(s32[11]{0:T(128)} %concatenate.138.place, bf16[768,768]{1,0:T(8,128)(2,1)} %get-tuple-element.254.query, bf16[2,768,768]{2,1,0:T(8,128)(2,1)} %get-tuple-element.263.refs_0_, bf16[2,768,768]{2,1,0:T(8,128)(2,1)} %copy-done.38, ...), custom_call_target="tpu_custom_call" | custom-call | flops 20000000000 | bytes 40000000 | tf_op jit(solution)/shard_map/pallas_call | solution.py:59
  75.9 5.6 %collective-permute-done.8.cot_second = bf16[384,768]{1,0:T(8,128)(2,1)} collective-permute-done((bf16[384,768]{1,0:T(8,128)(2,1)}, bf16[384,768]{1,0:T(8,128)(2,1)}, u32[]{:S(2)}, u32[]{:S(2)}) %collective-permute-start.8) | collective-permute-done | bytes 589856 | tf_op jit(solution)/shard_map/ppermute | solution.py:642
  81.6 20.2 %shard_map.345 = (f32[768,768]{1,0:T(8,128)}, f32[768,768]{1,0:T(8,128)}, f32[768,768]{1,0:T(8,128)}, bf16[768,768]{1,0:T(8,128)(2,1)}, bf16[768,768]{1,0:T(8,12...) custom-call(s32[2]{0:T(128)} %get-tuple-element.268.tiles, ...), custom_call_target="tpu_custom_call" | custom-call | flops 20000000000 | bytes 40000000 | tf_op jit(solution)/shard_map/pallas_call | solution.py:59
  101.9 25.0 %shard_map.346 = (bf16[2,2,768,768]{3,2,1,0:T(8,128)(2,1)}, f32[2,8,768]{2,1,0:T(8,128)}, bf16[384,768]{1,0:T(8,128)(2,1)}, bf16[384,768]{1,0:T(8,128)(2,1)}, f3...) custom-call(s32[3]{0:T(128)} %get-tuple-element.239.tiles, ...), custom_call_target="tpu_custom_call" | custom-call | flops 20000000000 | bytes 40000000 | tf_op jit(solution)/shard_map/pallas_call | solution.py:59
  131.9 4.9 %shard_map.347 = (bf16[1,768,768]{2,1,0:T(8,128)(2,1)S(1)}, bf16[1,768,768]{2,1,0:T(8,128)(2,1)}, bf16[1,768,768]{2,1,0:T(8,128)(2,1)S(1)}, bf16[1,768,768]{2,1,0:T(8,128)(2,1)S(1)}) custom-call(s32[3]{0:T(128)S(1)} %get-tuple-element.417.order, bf16[2,2,768,768]{3,2,1,0:T(8,128)(2,1)S(1)} %copy-done.6, bf16[2,2,768,768]{3,2,1,0:T(8,128)(2,1)} %collective-permute-done.10.received), custom_call_target="tpu_custom_call" | custom-call | flops 20000000000 | bytes 40000000 | tf_op jit(solution)/shard_map/pallas_call | solution.py:59
  141.8 16.5 %shard_map.348 = (bf16[256,768]{1,0:T(8,128)(2,1)}, bf16[2,256,768]{2,1,0:T(8,128)(2,1)}, bf16[2,256,768]{2,1,0:T(8,128)(2,1)}, bf16[2,256,768]{2,1,0:T(8,128)(2,1)}, bf16[2,256,768]{2,1,0:T(8,128)(2,1)}) custom-call(s32[11]{0:T(128)} %concatenate.138.place, bf16[768,768]{1,0:T(8,128)(2,1)} %get-tuple-element.254.query, ...), custom_call_target="tpu_custom_call" | custom-call | flops 20000000000 | bytes 40000000 | tf_op jit(solution)/shard_map/pallas_call | solution.py:59
  161.8 5.2 %collective-permute-done.12.refs_1_ = bf16[1,768,768]{2,1,0:T(8,128)(2,1)S(1)} collective-permute-done((bf16[1,768,768]{2,1,0:T(8,128)(2,1)}, bf16[1,768,768]{2,1,0:T(8,128)(2,1)S(1)}, u32[]{:S(2)}, u32[]{:S(2)}) %collective-permute-start.12) | collective-permute-done | bytes 1179680 | tf_op jit(solution)/shard_map/ppermute | solution.py:621
  176.9 11.0 %shard_map.352 = (bf16[512,768]{1,0:T(8,128)(2,1)}, bf16[2,512,768]{2,1,0:T(8,128)(2,1)}, bf16[2,512,768]{2,1,0:T(8,128)(2,1)}) custom-call(s32[7]{0:T(128)} %pad_add_fusion.1.place, bf16[768,768]{1,0:T(8,128)(2,1)} %get-tuple-element.254.query, bf16[512,768]{1,0:T(8,128)(2,1)} %get-tuple-element.313.grad, bf16[512,768]{1,0:T(8,128)(2,1)} %get-tuple-element.264.own.mixed, ...), custom_call_target="tpu_custom_call" | custom-call | flops 20000000000 | bytes 40000000 | tf_op jit(solution)/shard_map/pallas_call | solution.py:59
  191.6 8.4 %collective-permute-start.17 = (bf16[1,384,768]{2,1,0:T(8,128)(2,1)S(1)}, bf16[1,384,768]{2,1,0:T(8,128)(2,1)S(1)}, u32[]{:S(2)}, u32[]{:S(2)}) collective-permute-start(bf16[1,384,768]{2,1,0:T(8,128)(2,1)S(1)} %get-tuple-element.321), channel_id=1, source_target_pairs={{0,1},{1,0},{2,3},{3,2},{4,5},{5,4},{6,7},{7,6},{8,9},{9,8},{10,11... | collective-permute-start | bytes 1769480 | tf_op jit(solution)/shard_map/ppermute | solution.py:624
  200.0 9.7 %shard_map.354 = (bf16[3,384,768]{2,1,0:T(8,128)(2,1)}, bf16[3,384,768]{2,1,0:T(8,128)(2,1)}, bf16[2,768,768]{2,1,0:T(8,128)(2,1)}, f32[8,768]{1,0:T(8,128)}) custom-call(s32[1]{0:T(128)} %bitcast.8.order.core, bf16[768,768]{1,0:T(8,128)(2,1)} %get-tuple-element.324.normed, bf16[256,768]{1,0:T(8,128)(2,1)} %get-tuple-element.325.normed_far, ...), custom_call_target="tpu_custom_call" | custom-call | flops 20000000000 | bytes 40000000 | tf_op jit(solution)/shard_map/pallas_call | solution.py:59
  209.8 3.8 %collective-permute-done.17.refs_1_ = bf16[1,384,768]{2,1,0:T(8,128)(2,1)S(1)} collective-permute-done((bf16[1,384,768]{2,1,0:T(8,128)(2,1)S(1)}, bf16[1,384,768]{2,1,0:T(8,128)(2,1)S(1)}, u32[]{:S(2)}, u32[]{:S(2)}) %collective-permute-start.17) | collective-permute-done | bytes 589856 | tf_op jit(solution)/shard_map/ppermute | solution.py:624
  221.8 9.2 %shard_map.357 = (bf16[384,768]{1,0:T(8,128)(2,1)}, bf16[384,768]{1,0:T(8,128)(2,1)}, f32[8,768]{1,0:T(8,128)}) custom-call(s32[1]{0:T(128)} %bitcast.8.order.core, bf16[512,768]{1,0:T(8,128)(2,1)} %get-tuple-element.315.query_own, bf16[256,768]{1,0:T(8,128)(2,1)} %get-tuple-element.291.query_mixed, bf16[2,768,768]{2,1,0:T(8,128)(2,1)} %get-tuple-element.345.both, ...), custom_call_target="tpu_custom_call" | custom-call | flops 20000000000 | bytes 40000000 | tf_op jit(solution)/shard_map/pallas_call | solution.py:59
  243.8 7.3 %collective-permute-done.29 = bf16[1,192,768]{2,1,0:T(8,128)(2,1)S(1)} collective-permute-done((bf16[1,192,768]{2,1,0:T(8,128)(2,1)}, bf16[1,192,768]{2,1,0:T(8,128)(2,1)S(1)}, u32[]{:S(2)}, u32[]{:S(2)}) %collective-permute-start.29) | collective-permute-done | bytes 294944 | tf_op jit(solution)/shard_map/ppermute | solution.py:624
  258.9 14.5 %collective-permute-done.30.refs_1_ = bf16[4,48,768]{2,1,0:T(8,128)(2,1)S(1)} collective-permute-done((bf16[4,48,768]{2,1,0:T(8,128)(2,1)S(1)}, bf16[4,48,768]{2,1,0:T(8,128)(2,1)S(1)}, u32[]{:S(2)}, u32[]{:S(2)}) %collective-permute-start.30) | collective-permute-done | bytes 294944 | tf_op jit(solution)/shard_map/ppermute | solution.py:624
  277.6 11.3 %collective-permute-done.34 = f32[14,768]{1,0:T(8,128)S(1)} collective-permute-done((f32[14,768]{1,0:T(8,128)S(1)}, f32[14,768]{1,0:T(8,128)S(1)}, u32[]{:S(2)}, u32[]{:S(2)}) %collective-permute-start.34) | collective-permute-done | bytes 43040 | tf_op jit(solution)/shard_map/ppermute | solution.py:621
  298.5 9.3 %collective-permute-done.37 = bf16[4,24,768]{2,1,0:T(8,128)(2,1)S(1)} collective-permute-done((bf16[4,24,768]{2,1,0:T(8,128)(2,1)S(1)}, bf16[4,24,768]{2,1,0:T(8,128)(2,1)S(1)}, u32[]{:S(2)}, u32[]{:S(2)}) %collective-permute-start.37) | collective-permute-done | bytes 147488 | tf_op jit(solution)/shard_map/ppermute | solution.py:624
  308.0 4.9 %collective-permute-done.42 = f32[14,768]{1,0:T(8,128)S(1)} collective-permute-done((f32[14,768]{1,0:T(8,128)S(1)}, f32[14,768]{1,0:T(8,128)S(1)}, u32[]{:S(2)}, u32[]{:S(2)}) %collective-permute-start.42) | collective-permute-done | bytes 43040 | tf_op jit(solution)/shard_map/ppermute | solution.py:624
  312.9 7.7 %collective-permute-done.41 = bf16[4,48,768]{2,1,0:T(8,128)(2,1)S(1)} collective-permute-done((bf16[4,48,768]{2,1,0:T(8,128)(2,1)S(1)}, bf16[4,48,768]{2,1,0:T(8,128)(2,1)S(1)}, u32[]{:S(2)}, u32[]{:S(2)}) %collective-permute-start.41) | collective-permute-done | bytes 294944 | tf_op jit(solution)/shard_map/ppermute | solution.py:624
  341.7 6.1 %shard_map.363 = f32[768,3072]{1,0:T(8,128)} custom-call(s32[3]{0:T(128)S(1)} %copy-done.1, bf16[1,768,768]{2,1,0:T(8,128)(2,1)S(1)} %maximum_select_fusion.2.refs_0_, bf16[1,768,768]{2,1,0:T(8,128)(2,1)} %collective-permute-done.45.refs_1_, bf16[1,768,768]{2,1,0:T(8,128)(2,1)S(1)} %copy-done.3, bf16[1,768,768]{2,1,0:T(8,128)(2,1)} %collective-permute-done.50.refs_3_), custom_call_target="tpu_custom_call" | custom-call | flops 20000000000 | bytes 40000000 | tf_op jit(solution)/shard_map/pallas_call | solution.py:59
  347.8 5.7 %shard_map.362 = f32[3072,768]{1,0:T(8,128)} custom-call(s32[3]{0:T(128)S(1)} %copy-done.1, bf16[1,768,768]{2,1,0:T(8,128)(2,1)S(1)} %maximum_select_fusion.1.refs_0_, bf16[1,768,768]{2,1,0:T(8,128)(2,1)} %collective-permute-done.43.refs_1_, bf16[1,768,768]{2,1,0:T(8,128)(2,1)S(1)} %copy-done.5, bf16[1,768,768]{2,1,0:T(8,128)(2,1)S(1)} %collective-permute-done.49.refs_3_), custom_call_target="tpu_custom_call" | custom-call | flops 20000000000 | bytes 40000000 | tf_op jit(solution)/shard_map/pallas_call | solution.py:59
  359.3 5.3 %shard_map.364 = (f32[768,768]{1,0:T(8,128)}, f32[768,768]{1,0:T(8,128)}, f32[768,768]{1,0:T(8,128)}, f32[768,768]{1,0:T(8,128)}) custom-call(s32[3]{0:T(128)S(1)} %copy-done.1, bf16[4,96,768]{2,1,0:T(8,128)(2,1)S(1)} %maximum_select_fusion.5.refs_0_, bf16[4,96,768]{2,1,0:T(8,128)(2,1)S(1)} %collective-permute-done.51.refs_1_, ...), custom_call_target="tpu_custom_call" | custom-call | flops 20000000000 | bytes 40000000 | tf_op jit(solution)/shard_map/pallas_call | solution.py:59
  (274 shorter events, 132.0 us)
Async XLA Ops:
  0.7 23.2 %collective-permute-start = (s32[3]{0:T(128)}, s32[3]{0:T(128)S(1)}, u32[]{:S(2)}, u32[]{:S(2)}) collective-permute-start(s32[3]{0:T(128)} %sizes.3), channel_id=1, source_target_pairs={{0,4},{4,0},{8,12},{12,8},{16,20},{20,16},{24,28},{28,24},{1,5},{5... | collective-permute-start | bytes 44 | tf_op jit(solution)/shard_map/ppermute | solution.py:621
  4.6 29.0 %collective-permute-start.1 = (bf16[384,768]{1,0:T(8,128)(2,1)}, bf16[384,768]{1,0:T(8,128)(2,1)S(1)}, u32[]{:S(2)}, u32[]{:S(2)}) collective-permute-start(bf16[384,768]{1,0:T(8,128)(2,1)} %get-tuple-element.235), channel_id=1, source_target_pairs={{0,4},{1,0},{2,5},{3,1},{4,6},{5,2},{6,7},{7,3},{8,12},{9,8},{10,1... | collective-permute-start | bytes 1769480 | tf_op jit(solution)/shard_map/ppermute | solution.py:642
  4.8 31.1 %collective-permute-start.2 = (bf16[384,768]{1,0:T(8,128)(2,1)}, bf16[384,768]{1,0:T(8,128)(2,1)S(1)}, u32[]{:S(2)}, u32[]{:S(2)}) collective-permute-start(bf16[384,768]{1,0:T(8,128)(2,1)} %get-tuple-element.242), channel_id=1, source_target_pairs={{0,1},{1,5},{2,0},{3,4},{4,3},{5,7},{6,2},{7,6},{8,9},{9,13},{10,8... | collective-permute-start | bytes 1769480 | tf_op jit(solution)/shard_map/ppermute | solution.py:642
  53.0 22.9 %collective-permute-start.7 = (bf16[384,768]{1,0:T(8,128)(2,1)}, bf16[384,768]{1,0:T(8,128)(2,1)}, u32[]{:S(2)}, u32[]{:S(2)}) collective-permute-start(bf16[384,768]{1,0:T(8,128)(2,1)} %get-tuple-element.270), channel_id=1, source_target_pairs={{0,4},{1,0},{2,5},{3,1},{4,6},{5,2},{6,7},{7,3},{8,12},{9,8},{10,1... | collective-permute-start | bytes 1769480 | tf_op jit(solution)/shard_map/ppermute | solution.py:642
  53.5 28.1 %collective-permute-start.8 = (bf16[384,768]{1,0:T(8,128)(2,1)}, bf16[384,768]{1,0:T(8,128)(2,1)}, u32[]{:S(2)}, u32[]{:S(2)}) collective-permute-start(bf16[384,768]{1,0:T(8,128)(2,1)} %get-tuple-element.271), channel_id=1, source_target_pairs={{0,1},{1,5},{2,0},{3,4},{4,3},{5,7},{6,2},{7,6},{8,9},{9,13},{10,8... | collective-permute-start | bytes 1769480 | tf_op jit(solution)/shard_map/ppermute | solution.py:642
  101.8 27.7 %collective-permute-start.10 = (bf16[2,2,768,768]{3,2,1,0:T(8,128)(2,1)}, bf16[2,2,768,768]{3,2,1,0:T(8,128)(2,1)}, u32[]{:S(2)}, u32[]{:S(2)}) collective-permute-start(bf16[2,2,768,768]{3,2,1,0:T(8,128)(2,1)} %get-tuple-element.285), channel_id=1, source_target_pairs={{0,4},{4,0},{8,12},{12,8},{16,20},{20,16},{24,28},{28,24},{1,5},{5... | collective-permute-start | bytes 14155784 | tf_op jit(solution)/shard_map/ppermute | solution.py:621
  126.9 31.3 %collective-permute-start.9 = (bf16[384,768]{1,0:T(8,128)(2,1)}, bf16[384,768]{1,0:T(8,128)(2,1)}, u32[]{:S(2)}, u32[]{:S(2)}) collective-permute-start(bf16[384,768]{1,0:T(8,128)(2,1)} %get-tuple-element.282), channel_id=1, source_target_pairs={{4,0},{0,1},{5,2},{1,3},{6,4},{2,5},{7,6},{3,7},{12,8},{8,9},{13,1... | collective-permute-start | bytes 1769480 | tf_op jit(solution)/shard_map/ppermute | solution.py:645
  127.0 31.4 %collective-permute-start.11 = (bf16[384,768]{1,0:T(8,128)(2,1)}, bf16[384,768]{1,0:T(8,128)(2,1)}, u32[]{:S(2)}, u32[]{:S(2)}) collective-permute-start(bf16[384,768]{1,0:T(8,128)(2,1)} %get-tuple-element.293), channel_id=1, source_target_pairs={{1,0},{5,1},{0,2},{4,3},{3,4},{7,5},{2,6},{6,7},{9,8},{13,9},{8,10... | collective-permute-start | bytes 1769480 | tf_op jit(solution)/shard_map/ppermute | solution.py:645
  127.7 90.7 %collective-permute-start.22 = (bf16[1,384,768]{2,1,0:T(8,128)(2,1)}, bf16[1,384,768]{2,1,0:T(8,128)(2,1)}, u32[]{:S(2)}, u32[]{:S(2)}) collective-permute-start(bf16[1,384,768]{2,1,0:T(8,128)(2,1)} %get-tuple-element.337), channel_id=1, source_target_pairs={{0,4},{4,0},{8,12},{12,8},{16,20},{20,16},{24,28},{28,24},{1,5},{5... | collective-permute-start | bytes 1769480 | tf_op jit(solution)/shard_map/ppermute | solution.py:621
  138.8 28.2 %collective-permute-start.12 = (bf16[1,768,768]{2,1,0:T(8,128)(2,1)}, bf16[1,768,768]{2,1,0:T(8,128)(2,1)S(1)}, u32[]{:S(2)}, u32[]{:S(2)}) collective-permute-start(bf16[1,768,768]{2,1,0:T(8,128)(2,1)} %get-tuple-element.298), channel_id=1, source_target_pairs={{0,8},{4,12},{8,0},{12,4},{16,24},{20,28},{24,16},{28,20},{1,9},{5... | collective-permute-start | bytes 3538952 | tf_op jit(solution)/shard_map/ppermute | solution.py:621
  140.7 27.6 %collective-permute-start.13 = (bf16[1,768,768]{2,1,0:T(8,128)(2,1)S(1)}, bf16[1,768,768]{2,1,0:T(8,128)(2,1)S(1)}, u32[]{:S(2)}, u32[]{:S(2)}) collective-permute-start(bf16[1,768,768]{2,1,0:T(8,128)(2,1)S(1)} %get-tuple-element.299), channel_id=1, source_target_pairs={{0,16},{4,20},{8,24},{12,28},{16,0},{20,4},{24,8},{28,12},{1,17},{... | collective-permute-start | bytes 3538952 | tf_op jit(solution)/shard_map/ppermute | solution.py:621
  158.4 41.6 %collective-permute-start.20 = (bf16[2,256,768]{2,1,0:T(8,128)(2,1)}, bf16[2,256,768]{2,1,0:T(8,128)(2,1)}, u32[]{:S(2)}, u32[]{:S(2)}) collective-permute-start(bf16[2,256,768]{2,1,0:T(8,128)(2,1)} %get-tuple-element.329), channel_id=1, source_target_pairs={{0,4},{4,0},{8,12},{12,8},{16,20},{20,16},{24,28},{28,24},{1,5},{5... | collective-permute-start | bytes 2359304 | tf_op jit(solution)/shard_map/ppermute | solution.py:621
  191.6 22.0 %collective-permute-start.17 = (bf16[1,384,768]{2,1,0:T(8,128)(2,1)S(1)}, bf16[1,384,768]{2,1,0:T(8,128)(2,1)S(1)}, u32[]{:S(2)}, u32[]{:S(2)}) collective-permute-start(bf16[1,384,768]{2,1,0:T(8,128)(2,1)S(1)} %get-tuple-element.321), channel_id=1, source_target_pairs={{0,1},{1,0},{2,3},{3,2},{4,5},{5,4},{6,7},{7,6},{8,9},{9,8},{10,11... | collective-permute-start | bytes 1769480 | tf_op jit(solution)/shard_map/ppermute | solution.py:624
  214.9 17.6 %collective-permute-start.23 = (bf16[1,192,768]{2,1,0:T(8,128)(2,1)S(1)}, bf16[1,192,768]{2,1,0:T(8,128)(2,1)S(1)}, u32[]{:S(2)}, u32[]{:S(2)}) collective-permute-start(bf16[1,192,768]{2,1,0:T(8,128)(2,1)S(1)} %get-tuple-element.349), channel_id=1, source_target_pairs={{0,2},{1,3},{2,0},{3,1},{4,6},{5,7},{6,4},{7,5},{8,10},{9,11},{10,... | collective-permute-start | bytes 884744 | tf_op jit(solution)/shard_map/ppermute | solution.py:624
  252.4 21.0 %collective-permute-start.32 = (bf16[1,384,768]{2,1,0:T(8,128)(2,1)S(1)}, bf16[1,384,768]{2,1,0:T(8,128)(2,1)S(1)}, u32[]{:S(2)}, u32[]{:S(2)}) collective-permute-start(bf16[1,384,768]{2,1,0:T(8,128)(2,1)S(1)} %maximum_select_fusion.3), channel_id=1, source_target_pairs={{0,1},{1,0},{2,3},{3,2},{4,5},{5,4},{6,7},{7,6},{8,9},{9,8},{10,11... | collective-permute-start | bytes 1769480 | tf_op jit(solution)/shard_map/ppermute | solution.py:624
  252.8 20.7 %collective-permute-start.30 = (bf16[4,48,768]{2,1,0:T(8,128)(2,1)S(1)}, bf16[4,48,768]{2,1,0:T(8,128)(2,1)S(1)}, u32[]{:S(2)}, u32[]{:S(2)}) collective-permute-start(bf16[4,48,768]{2,1,0:T(8,128)(2,1)S(1)} %get-tuple-element.374), channel_id=1, source_target_pairs={{0,1},{1,0},{2,3},{3,2},{4,5},{5,4},{6,7},{7,6},{8,9},{9,8},{10,11... | collective-permute-start | bytes 884744 | tf_op jit(solution)/shard_map/ppermute | solution.py:624
  274.0 14.8 %collective-permute-start.35 = (bf16[1,384,768]{2,1,0:T(8,128)(2,1)S(1)}, bf16[1,384,768]{2,1,0:T(8,128)(2,1)S(1)}, u32[]{:S(2)}, u32[]{:S(2)}) collective-permute-start(bf16[1,384,768]{2,1,0:T(8,128)(2,1)S(1)} %get-tuple-element.397), channel_id=1, source_target_pairs={{0,16},{4,20},{8,24},{12,28},{16,0},{20,4},{24,8},{28,12},{1,17},{... | collective-permute-start | bytes 1769480 | tf_op jit(solution)/shard_map/ppermute | solution.py:621
  291.4 29.3 %collective-permute-start.45 = (bf16[1,768,768]{2,1,0:T(8,128)(2,1)S(1)}, bf16[1,768,768]{2,1,0:T(8,128)(2,1)}, u32[]{:S(2)}, u32[]{:S(2)}) collective-permute-start(bf16[1,768,768]{2,1,0:T(8,128)(2,1)S(1)} %maximum_select_fusion.2.refs_0_), channel_id=1, source_target_pairs={{0,16},{4,20},{8,24},{12,28},{16,0},{20,4},{24,8},{28,12},{1,17},{... | collective-permute-start | bytes 3538952 | tf_op jit(solution)/shard_map/ppermute | solution.py:621
  292.2 28.4 %collective-permute-start.46 = (bf16[1,768,768]{2,1,0:T(8,128)(2,1)S(1)}, bf16[1,768,768]{2,1,0:T(8,128)(2,1)S(1)}, u32[]{:S(2)}, u32[]{:S(2)}) collective-permute-start(bf16[1,768,768]{2,1,0:T(8,128)(2,1)S(1)} %maximum_select_fusion.2.refs_0_), channel_id=1, source_target_pairs={{0,4},{4,0},{8,12},{12,8},{16,20},{20,16},{24,28},{28,24},{1,5},{5... | collective-permute-start | bytes 3538952 | tf_op jit(solution)/shard_map/ppermute | solution.py:621
  292.7 28.6 %collective-permute-start.43 = (bf16[1,768,768]{2,1,0:T(8,128)(2,1)S(1)}, bf16[1,768,768]{2,1,0:T(8,128)(2,1)}, u32[]{:S(2)}, u32[]{:S(2)}) collective-permute-start(bf16[1,768,768]{2,1,0:T(8,128)(2,1)S(1)} %maximum_select_fusion.1.refs_0_), channel_id=1, source_target_pairs={{0,8},{4,12},{8,0},{12,4},{16,24},{20,28},{24,16},{28,20},{1,9},{5... | collective-permute-start | bytes 3538952 | tf_op jit(solution)/shard_map/ppermute | solution.py:621
  294.2 27.1 %collective-permute-start.44 = (bf16[1,768,768]{2,1,0:T(8,128)(2,1)S(1)}, bf16[1,768,768]{2,1,0:T(8,128)(2,1)S(1)}, u32[]{:S(2)}, u32[]{:S(2)}) collective-permute-start(bf16[1,768,768]{2,1,0:T(8,128)(2,1)S(1)} %maximum_select_fusion.1.refs_0_), channel_id=1, source_target_pairs={{0,4},{4,0},{8,12},{12,8},{16,20},{20,16},{24,28},{28,24},{1,5},{5... | collective-permute-start | bytes 3538952 | tf_op jit(solution)/shard_map/ppermute | solution.py:621
  322.8 32.4 %collective-permute-start.39 = (bf16[384,768]{1,0:T(8,128)(2,1)}, bf16[384,768]{1,0:T(8,128)(2,1)}, u32[]{:S(2)}, u32[]{:S(2)}) collective-permute-start(bf16[384,768]{1,0:T(8,128)(2,1)} %get-tuple-element.393), channel_id=1, source_target_pairs={{4,0},{0,1},{5,2},{1,3},{6,4},{2,5},{7,6},{3,7},{12,8},{8,9},{13,1... | collective-permute-start | bytes 1769480 | tf_op jit(solution)/shard_map/ppermute | solution.py:645
  333.6 22.2 %collective-permute-start.40 = (bf16[384,768]{1,0:T(8,128)(2,1)}, bf16[384,768]{1,0:T(8,128)(2,1)S(1)}, u32[]{:S(2)}, u32[]{:S(2)}) collective-permute-start(bf16[384,768]{1,0:T(8,128)(2,1)} %get-tuple-element.394), channel_id=1, source_target_pairs={{1,0},{5,1},{0,2},{4,3},{3,4},{7,5},{2,6},{6,7},{9,8},{13,9},{8,10... | collective-permute-start | bytes 1769480 | tf_op jit(solution)/shard_map/ppermute | solution.py:645
  337.2 16.3 %collective-permute-start.52 = (bf16[4,96,768]{2,1,0:T(8,128)(2,1)S(1)}, bf16[4,96,768]{2,1,0:T(8,128)(2,1)S(1)}, u32[]{:S(2)}, u32[]{:S(2)}) collective-permute-start(bf16[4,96,768]{2,1,0:T(8,128)(2,1)S(1)} %maximum_select_fusion.6.refs_4_), channel_id=1, source_target_pairs={{0,16},{4,20},{8,24},{12,28},{16,0},{20,4},{24,8},{28,12},{1,17},{... | collective-permute-start | bytes 1769480 | tf_op jit(solution)/shard_map/ppermute | solution.py:621
  (80 other events, 769.2 us)

commit v6 on v5

--- a/solution.py
+++ b/solution.py
@@ -1039,9 +1039,7 @@
         jnp.concatenate([b_up_kept, b_up_sent]),
         jnp.concatenate([b_up_sent, b_up_kept]),
     )
-    small = jnp.concatenate(
-        [rows_middle[:4], rows_up, rows_weight[:3], rows_input[:2], counts], axis=0
-    )
+    small = jnp.concatenate([rows_middle, rows_weight, rows_input, rows_up, counts], axis=0)
 
     class Small:
         def __init__(self):
@@ -1086,9 +1084,9 @@
     while small_sum.left > 0:
         advance([small_sum])
     total = small_sum.state[0][0]
-    small = [total[at] for at in range(4)] + [total[4:8].reshape(-1)]
-    small += [total[at] for at in range(8, 13)]
-    small.append(total[13, :CLASSES].astype(jnp.int32))
+    small = [total[at] for at in range(4)] + [total[24:28].reshape(-1)]
+    small += [total[at] for at in (8, 9, 10, 16, 17)]
+    small.append(total[28, :CLASSES].astype(jnp.int32))
     small = lax.optimization_barrier(small)
     gates = [grad_w_down, grad_w_up, *small]
     while weight_sum.left > 0:

time: 370 us -> 373 us (level)
  waiting for transfers between devices: 92 us -> 99.3 us
  local copies, waits for them, and re-layouts: 34 us -> 29.1 us
    ppermute x10, starting transfers between devices: 15.4 us -> 10.7 us  [flip_depth(): return lax.ppermute(value, 'seq', [(i, i ^ bit) for i in range(4)])]
    ppermute x36, starting transfers between devices: 23 us -> 27.7 us  [flip(): return lax.ppermute(value, 'dp', [(i, i ^ bit) for i in range(groups)])]
    ppermute x36, waiting for transfers between devices: 32.1 us -> 36.7 us  [flip(): return lax.ppermute(value, 'dp', [(i, i ^ bit) for i in range(groups)])]
    unnamed x94 -> x98, local copies, waits for them, and re-layouts: 15 us -> 14.6 us
  transfers between devices with their start and end apart: 57 -> 57, of which waited for: 23 -> 22; matrix products, arithmetic and copies ran while one was open for 8% -> 6% of each run, Pallas kernels for 39% -> 39%
where the time goes in v6:
time: 373 us; the launch traced here: 366 us
  Pallas kernels  167 us (45%)
  waiting for transfers between devices  99.3 us (27%)
  starting transfers between devices  47.4 us (13%)
  local copies, waits for them, and re-layouts  29.1 us (8%)
  other arithmetic  13.3 us (4%)
  between operations  9.82 us (3%)
    pallas_call x26, Pallas kernels, call(): pl.pallas_call(kernel, grid_spec=pltpu.PrefetchScalarGridSpec(num_scalar_...  167 us
    ppermute x10, waiting for transfers between devices, flip_depth(): return lax.ppermute(value, 'seq', [(i, i ^ bit) for i in range(4)])  53.9 us
    ppermute x36, waiting for transfers between devices, flip(): return lax.ppermute(value, 'dp', [(i, i ^ bit) for i in range(groups)])  36.7 us
    ppermute x36, starting transfers between devices, flip(): return lax.ppermute(value, 'dp', [(i, i ^ bit) for i in range(groups)])  27.7 us
    unnamed x98, local copies, waits for them, and re-layouts  14.6 us
    ppermute x10, starting transfers between devices, flip_depth(): return lax.ppermute(value, 'seq', [(i, i ^ bit) for i in range(4)])  10.7 us
    ppermute x6, waiting for transfers between devices, send(): return lax.ppermute(value, ('dp', 'seq'), route(turn))  8.72 us
  transfers between devices with their start and end apart: 57, of which 22 were waited for; matrix products, arithmetic and copies ran while one was open for 6% of the time, Pallas kernels for 39%

profile of v6, /device:TPU:0, one launch (start us, length us, event | category | flops | bytes accessed | tf_op | source)
XLA Modules:
  0.0 366.2 jit_solution(14773700480098564767)
XLA Ops:
  37.9 8.7 %shard_map.341 = (bf16[768,768]{1,0:T(8,128)(2,1)}, bf16[2,768,768]{2,1,0:T(8,128)(2,1)}, bf16[768,768]{1,0:T(8,128)(2,1)}) custom-call(s32[6]{0:T(128)} %pad_add_fusion.place, bf16[384,768]{1,0:T(8,128)(2,1)} %copy-done.42, bf16[384,768]{1,0:T(8,128)(2,1)} %copy-done.43, f32[1,768]{1,0:T(1,128)} %reshape.383.gain, f32[1,768]{1,0:T(1,128)} %reshape.384.shift, ...), custom_call_target="tpu_custom_call" | custom-call | flops 20000000000 | bytes 40000000 | tf_op jit(solution)/shard_map/pallas_call | solution.py:59
  48.7 4.8 %shard_map.342 = (bf16[2,256,768]{2,1,0:T(8,128)(2,1)}, bf16[256,768]{1,0:T(8,128)(2,1)}) custom-call(s32[6]{0:T(128)} %pad_add_fusion.place, bf16[128,768]{1,0:T(8,128)(2,1)} %copy-done.47, bf16[128,768]{1,0:T(8,128)(2,1)} %copy-done.48, f32[1,768]{1,0:T(1,128)} %reshape.383.gain, f32[1,768]{1,0:T(1,128)} %reshape.384.shift, bf16[768,768]{1,0:T(8,128)(2,1)} %w_key.7, ...), custom_call_target="tpu_custom_call" | custom-call | flops 20000000000 | bytes 40000000 | tf_op jit(solution)/shard_map/pallas_call | solution.py:59
  57.2 7.9 %shard_map.343 = (bf16[512,768]{1,0:T(8,128)(2,1)}, f32[6,8,512]{2,1,0:T(8,128)}) custom-call(s32[7]{0:T(128)} %pad_add_fusion.1.place, bf16[768,768]{1,0:T(8,128)(2,1)} %get-tuple-element.254.query, bf16[2,768,768]{2,1,0:T(8,128)(2,1)} %get-tuple-element.263.refs_0_, bf16[2,768,768]{2,1,0:T(8,128)(2,1)} %copy-done.40), custom_call_target="tpu_custom_call" | custom-call | flops 20000000000 | bytes 40000000 | tf_op jit(solution)/shard_map/pallas_call | solution.py:59
  65.9 10.5 %shard_map.344 = (bf16[256,768]{1,0:T(8,128)(2,1)}, f32[6,8,256]{2,1,0:T(8,128)}) custom-call(s32[11]{0:T(128)} %concatenate.138.place, bf16[768,768]{1,0:T(8,128)(2,1)} %get-tuple-element.254.query, bf16[2,768,768]{2,1,0:T(8,128)(2,1)} %get-tuple-element.263.refs_0_, bf16[2,768,768]{2,1,0:T(8,128)(2,1)} %copy-done.40, ...), custom_call_target="tpu_custom_call" | custom-call | flops 20000000000 | bytes 40000000 | tf_op jit(solution)/shard_map/pallas_call | solution.py:59
  76.5 5.5 %collective-permute-done.8.cot_second = bf16[384,768]{1,0:T(8,128)(2,1)} collective-permute-done((bf16[384,768]{1,0:T(8,128)(2,1)}, bf16[384,768]{1,0:T(8,128)(2,1)}, u32[]{:S(2)}, u32[]{:S(2)}) %collective-permute-start.8) | collective-permute-done | bytes 589856 | tf_op jit(solution)/shard_map/ppermute | solution.py:642
  82.0 20.2 %shard_map.345 = (f32[768,768]{1,0:T(8,128)}, f32[768,768]{1,0:T(8,128)}, f32[768,768]{1,0:T(8,128)}, bf16[768,768]{1,0:T(8,128)(2,1)}, bf16[768,768]{1,0:T(8,12...) custom-call(s32[2]{0:T(128)} %get-tuple-element.268.tiles, ...), custom_call_target="tpu_custom_call" | custom-call | flops 20000000000 | bytes 40000000 | tf_op jit(solution)/shard_map/pallas_call | solution.py:59
  102.4 25.0 %shard_map.346 = (bf16[2,2,768,768]{3,2,1,0:T(8,128)(2,1)}, f32[2,8,768]{2,1,0:T(8,128)}, bf16[384,768]{1,0:T(8,128)(2,1)}, bf16[384,768]{1,0:T(8,128)(2,1)}, f3...) custom-call(s32[3]{0:T(128)} %get-tuple-element.239.tiles, ...), custom_call_target="tpu_custom_call" | custom-call | flops 20000000000 | bytes 40000000 | tf_op jit(solution)/shard_map/pallas_call | solution.py:59
  131.0 4.9 %shard_map.347 = (bf16[1,768,768]{2,1,0:T(8,128)(2,1)S(1)}, bf16[1,768,768]{2,1,0:T(8,128)(2,1)}, bf16[1,768,768]{2,1,0:T(8,128)(2,1)S(1)}, bf16[1,768,768]{2,1,0:T(8,128)(2,1)S(1)}) custom-call(s32[3]{0:T(128)S(1)} %get-tuple-element.417.order, bf16[2,2,768,768]{3,2,1,0:T(8,128)(2,1)S(1)} %copy-done.6, bf16[2,2,768,768]{3,2,1,0:T(8,128)(2,1)} %collective-permute-done.10.received), custom_call_target="tpu_custom_call" | custom-call | flops 20000000000 | bytes 40000000 | tf_op jit(solution)/shard_map/pallas_call | solution.py:59
  140.9 16.4 %shard_map.348 = (bf16[256,768]{1,0:T(8,128)(2,1)}, bf16[2,256,768]{2,1,0:T(8,128)(2,1)}, bf16[2,256,768]{2,1,0:T(8,128)(2,1)}, bf16[2,256,768]{2,1,0:T(8,128)(2,1)}, bf16[2,256,768]{2,1,0:T(8,128)(2,1)}) custom-call(s32[11]{0:T(128)} %concatenate.138.place, bf16[768,768]{1,0:T(8,128)(2,1)} %get-tuple-element.254.query, ...), custom_call_target="tpu_custom_call" | custom-call | flops 20000000000 | bytes 40000000 | tf_op jit(solution)/shard_map/pallas_call | solution.py:59
  160.9 5.3 %collective-permute-done.12.refs_1_ = bf16[1,768,768]{2,1,0:T(8,128)(2,1)S(1)} collective-permute-done((bf16[1,768,768]{2,1,0:T(8,128)(2,1)}, bf16[1,768,768]{2,1,0:T(8,128)(2,1)S(1)}, u32[]{:S(2)}, u32[]{:S(2)}) %collective-permute-start.12) | collective-permute-done | bytes 1179680 | tf_op jit(solution)/shard_map/ppermute | solution.py:621
  176.0 11.0 %shard_map.352 = (bf16[512,768]{1,0:T(8,128)(2,1)}, bf16[2,512,768]{2,1,0:T(8,128)(2,1)}, bf16[2,512,768]{2,1,0:T(8,128)(2,1)}) custom-call(s32[7]{0:T(128)} %pad_add_fusion.1.place, bf16[768,768]{1,0:T(8,128)(2,1)} %get-tuple-element.254.query, bf16[512,768]{1,0:T(8,128)(2,1)} %get-tuple-element.313.grad, bf16[512,768]{1,0:T(8,128)(2,1)} %get-tuple-element.264.own.mixed, ...), custom_call_target="tpu_custom_call" | custom-call | flops 20000000000 | bytes 40000000 | tf_op jit(solution)/shard_map/pallas_call | solution.py:59
  194.4 9.7 %shard_map.354 = (bf16[3,384,768]{2,1,0:T(8,128)(2,1)}, bf16[3,384,768]{2,1,0:T(8,128)(2,1)}, bf16[2,768,768]{2,1,0:T(8,128)(2,1)}, f32[8,768]{1,0:T(8,128)}) custom-call(s32[1]{0:T(128)} %bitcast.8.order.core, bf16[768,768]{1,0:T(8,128)(2,1)} %get-tuple-element.324.normed, bf16[256,768]{1,0:T(8,128)(2,1)} %get-tuple-element.325.normed_far, ...), custom_call_target="tpu_custom_call" | custom-call | flops 20000000000 | bytes 40000000 | tf_op jit(solution)/shard_map/pallas_call | solution.py:59
  213.7 7.4 %collective-permute-start.24 = (bf16[4,96,768]{2,1,0:T(8,128)(2,1)S(1)}, bf16[4,96,768]{2,1,0:T(8,128)(2,1)S(1)}, u32[]{:S(2)}, u32[]{:S(2)}) collective-permute-start(bf16[4,96,768]{2,1,0:T(8,128)(2,1)S(1)} %get-tuple-element.350), channel_id=1, source_target_pairs={{0,8},{4,12},{8,0},{12,4},{16,24},{20,28},{24,16},{28,20},{1,9},{5... | collective-permute-start | bytes 1769480 | tf_op jit(solution)/shard_map/ppermute | solution.py:621
  221.1 9.2 %shard_map.357 = (bf16[384,768]{1,0:T(8,128)(2,1)}, bf16[384,768]{1,0:T(8,128)(2,1)}, f32[8,768]{1,0:T(8,128)}) custom-call(s32[1]{0:T(128)} %bitcast.8.order.core, bf16[512,768]{1,0:T(8,128)(2,1)} %get-tuple-element.315.query_own, bf16[256,768]{1,0:T(8,128)(2,1)} %get-tuple-element.291.query_mixed, bf16[2,768,768]{2,1,0:T(8,128)(2,1)} %get-tuple-element.345.both, ...), custom_call_target="tpu_custom_call" | custom-call | flops 20000000000 | bytes 40000000 | tf_op jit(solution)/shard_map/pallas_call | solution.py:59
  241.4 8.3 %collective-permute-done.29 = bf16[1,192,768]{2,1,0:T(8,128)(2,1)S(1)} collective-permute-done((bf16[1,192,768]{2,1,0:T(8,128)(2,1)}, bf16[1,192,768]{2,1,0:T(8,128)(2,1)S(1)}, u32[]{:S(2)}, u32[]{:S(2)}) %collective-permute-start.29) | collective-permute-done | bytes 294944 | tf_op jit(solution)/shard_map/ppermute | solution.py:624
  258.1 14.5 %collective-permute-done.30.refs_1_ = bf16[4,48,768]{2,1,0:T(8,128)(2,1)S(1)} collective-permute-done((bf16[4,48,768]{2,1,0:T(8,128)(2,1)S(1)}, bf16[4,48,768]{2,1,0:T(8,128)(2,1)S(1)}, u32[]{:S(2)}, u32[]{:S(2)}) %collective-permute-start.30) | collective-permute-done | bytes 294944 | tf_op jit(solution)/shard_map/ppermute | solution.py:624
  276.1 13.6 %collective-permute-done.34 = f32[29,768]{1,0:T(8,128)S(1)} collective-permute-done((f32[29,768]{1,0:T(8,128)S(1)}, f32[29,768]{1,0:T(8,128)S(1)}, u32[]{:S(2)}, u32[]{:S(2)}) %collective-permute-start.34) | collective-permute-done | bytes 89120 | tf_op jit(solution)/shard_map/ppermute | solution.py:621
  295.2 4.4 %collective-permute-done.38 = f32[29,768]{1,0:T(8,128)S(1)} collective-permute-done((f32[29,768]{1,0:T(8,128)S(1)}, f32[29,768]{1,0:T(8,128)S(1)}, u32[]{:S(2)}, u32[]{:S(2)}) %collective-permute-start.38) | collective-permute-done | bytes 89120 | tf_op jit(solution)/shard_map/ppermute | solution.py:624
  299.6 9.4 %collective-permute-done.37 = bf16[4,24,768]{2,1,0:T(8,128)(2,1)S(1)} collective-permute-done((bf16[4,24,768]{2,1,0:T(8,128)(2,1)S(1)}, bf16[4,24,768]{2,1,0:T(8,128)(2,1)S(1)}, u32[]{:S(2)}, u32[]{:S(2)}) %collective-permute-start.37) | collective-permute-done | bytes 147488 | tf_op jit(solution)/shard_map/ppermute | solution.py:624
  309.1 5.5 %collective-permute-done.42 = f32[29,768]{1,0:T(8,128)S(1)} collective-permute-done((f32[29,768]{1,0:T(8,128)S(1)}, f32[29,768]{1,0:T(8,128)S(1)}, u32[]{:S(2)}, u32[]{:S(2)}) %collective-permute-start.42) | collective-permute-done | bytes 89120 | tf_op jit(solution)/shard_map/ppermute | solution.py:624
  314.6 8.0 %collective-permute-done.41 = bf16[4,48,768]{2,1,0:T(8,128)(2,1)S(1)} collective-permute-done((bf16[4,48,768]{2,1,0:T(8,128)(2,1)S(1)}, bf16[4,48,768]{2,1,0:T(8,128)(2,1)S(1)}, u32[]{:S(2)}, u32[]{:S(2)}) %collective-permute-start.41) | collective-permute-done | bytes 294944 | tf_op jit(solution)/shard_map/ppermute | solution.py:624
  342.6 6.1 %shard_map.363 = f32[768,3072]{1,0:T(8,128)} custom-call(s32[3]{0:T(128)S(1)} %copy-done.1, bf16[1,768,768]{2,1,0:T(8,128)(2,1)S(1)} %maximum_select_fusion.2.refs_0_, bf16[1,768,768]{2,1,0:T(8,128)(2,1)} %collective-permute-done.45.refs_1_, bf16[1,768,768]{2,1,0:T(8,128)(2,1)S(1)} %copy-done.3, bf16[1,768,768]{2,1,0:T(8,128)(2,1)} %collective-permute-done.50.refs_3_), custom_call_target="tpu_custom_call" | custom-call | flops 20000000000 | bytes 40000000 | tf_op jit(solution)/shard_map/pallas_call | solution.py:59
  348.6 5.7 %shard_map.362 = f32[3072,768]{1,0:T(8,128)} custom-call(s32[3]{0:T(128)S(1)} %copy-done.1, bf16[1,768,768]{2,1,0:T(8,128)(2,1)S(1)} %maximum_select_fusion.1.refs_0_, bf16[1,768,768]{2,1,0:T(8,128)(2,1)} %collective-permute-done.43.refs_1_, bf16[1,768,768]{2,1,0:T(8,128)(2,1)S(1)} %copy-done.5, bf16[1,768,768]{2,1,0:T(8,128)(2,1)S(1)} %collective-permute-done.49.refs_3_), custom_call_target="tpu_custom_call" | custom-call | flops 20000000000 | bytes 40000000 | tf_op jit(solution)/shard_map/pallas_call | solution.py:59
  360.5 5.3 %shard_map.364 = (f32[768,768]{1,0:T(8,128)}, f32[768,768]{1,0:T(8,128)}, f32[768,768]{1,0:T(8,128)}, f32[768,768]{1,0:T(8,128)}) custom-call(s32[3]{0:T(128)S(1)} %copy-done.1, bf16[4,96,768]{2,1,0:T(8,128)(2,1)S(1)} %maximum_select_fusion.5.refs_0_, bf16[4,96,768]{2,1,0:T(8,128)(2,1)S(1)} %collective-permute-done.51.refs_1_, ...), custom_call_target="tpu_custom_call" | custom-call | flops 20000000000 | bytes 40000000 | tf_op jit(solution)/shard_map/pallas_call | solution.py:59
  (275 shorter events, 129.2 us)
Async XLA Ops:
  0.7 23.3 %collective-permute-start = (s32[3]{0:T(128)}, s32[3]{0:T(128)S(1)}, u32[]{:S(2)}, u32[]{:S(2)}) collective-permute-start(s32[3]{0:T(128)} %sizes.3), channel_id=1, source_target_pairs={{0,4},{4,0},{8,12},{12,8},{16,20},{20,16},{24,28},{28,24},{1,5},{5... | collective-permute-start | bytes 44 | tf_op jit(solution)/shard_map/ppermute | solution.py:621
  4.6 29.5 %collective-permute-start.1 = (bf16[384,768]{1,0:T(8,128)(2,1)}, bf16[384,768]{1,0:T(8,128)(2,1)S(1)}, u32[]{:S(2)}, u32[]{:S(2)}) collective-permute-start(bf16[384,768]{1,0:T(8,128)(2,1)} %get-tuple-element.235), channel_id=1, source_target_pairs={{0,4},{1,0},{2,5},{3,1},{4,6},{5,2},{6,7},{7,3},{8,12},{9,8},{10,1... | collective-permute-start | bytes 1769480 | tf_op jit(solution)/shard_map/ppermute | solution.py:642
  4.8 31.1 %collective-permute-start.2 = (bf16[384,768]{1,0:T(8,128)(2,1)}, bf16[384,768]{1,0:T(8,128)(2,1)S(1)}, u32[]{:S(2)}, u32[]{:S(2)}) collective-permute-start(bf16[384,768]{1,0:T(8,128)(2,1)} %get-tuple-element.242), channel_id=1, source_target_pairs={{0,1},{1,5},{2,0},{3,4},{4,3},{5,7},{6,2},{7,6},{8,9},{9,13},{10,8... | collective-permute-start | bytes 1769480 | tf_op jit(solution)/shard_map/ppermute | solution.py:642
  53.5 23.0 %collective-permute-start.7 = (bf16[384,768]{1,0:T(8,128)(2,1)}, bf16[384,768]{1,0:T(8,128)(2,1)}, u32[]{:S(2)}, u32[]{:S(2)}) collective-permute-start(bf16[384,768]{1,0:T(8,128)(2,1)} %get-tuple-element.270), channel_id=1, source_target_pairs={{0,4},{1,0},{2,5},{3,1},{4,6},{5,2},{6,7},{7,3},{8,12},{9,8},{10,1... | collective-permute-start | bytes 1769480 | tf_op jit(solution)/shard_map/ppermute | solution.py:642
  54.0 28.0 %collective-permute-start.8 = (bf16[384,768]{1,0:T(8,128)(2,1)}, bf16[384,768]{1,0:T(8,128)(2,1)}, u32[]{:S(2)}, u32[]{:S(2)}) collective-permute-start(bf16[384,768]{1,0:T(8,128)(2,1)} %get-tuple-element.271), channel_id=1, source_target_pairs={{0,1},{1,5},{2,0},{3,4},{4,3},{5,7},{6,2},{7,6},{8,9},{9,13},{10,8... | collective-permute-start | bytes 1769480 | tf_op jit(solution)/shard_map/ppermute | solution.py:642
  102.3 26.4 %collective-permute-start.10 = (bf16[2,2,768,768]{3,2,1,0:T(8,128)(2,1)}, bf16[2,2,768,768]{3,2,1,0:T(8,128)(2,1)}, u32[]{:S(2)}, u32[]{:S(2)}) collective-permute-start(bf16[2,2,768,768]{3,2,1,0:T(8,128)(2,1)} %get-tuple-element.285), channel_id=1, source_target_pairs={{0,4},{4,0},{8,12},{12,8},{16,20},{20,16},{24,28},{28,24},{1,5},{5... | collective-permute-start | bytes 14155784 | tf_op jit(solution)/shard_map/ppermute | solution.py:621
  127.4 30.0 %collective-permute-start.9 = (bf16[384,768]{1,0:T(8,128)(2,1)}, bf16[384,768]{1,0:T(8,128)(2,1)}, u32[]{:S(2)}, u32[]{:S(2)}) collective-permute-start(bf16[384,768]{1,0:T(8,128)(2,1)} %get-tuple-element.282), channel_id=1, source_target_pairs={{4,0},{0,1},{5,2},{1,3},{6,4},{2,5},{7,6},{3,7},{12,8},{8,9},{13,1... | collective-permute-start | bytes 1769480 | tf_op jit(solution)/shard_map/ppermute | solution.py:645
  127.4 30.0 %collective-permute-start.11 = (bf16[384,768]{1,0:T(8,128)(2,1)}, bf16[384,768]{1,0:T(8,128)(2,1)}, u32[]{:S(2)}, u32[]{:S(2)}) collective-permute-start(bf16[384,768]{1,0:T(8,128)(2,1)} %get-tuple-element.293), channel_id=1, source_target_pairs={{1,0},{5,1},{0,2},{4,3},{3,4},{7,5},{2,6},{6,7},{9,8},{13,9},{8,10... | collective-permute-start | bytes 1769480 | tf_op jit(solution)/shard_map/ppermute | solution.py:645
  127.5 83.2 %collective-permute-start.22 = (bf16[1,384,768]{2,1,0:T(8,128)(2,1)}, bf16[1,384,768]{2,1,0:T(8,128)(2,1)}, u32[]{:S(2)}, u32[]{:S(2)}) collective-permute-start(bf16[1,384,768]{2,1,0:T(8,128)(2,1)} %get-tuple-element.337), channel_id=1, source_target_pairs={{0,4},{4,0},{8,12},{12,8},{16,20},{20,16},{24,28},{28,24},{1,5},{5... | collective-permute-start | bytes 1769480 | tf_op jit(solution)/shard_map/ppermute | solution.py:621
  137.9 28.3 %collective-permute-start.12 = (bf16[1,768,768]{2,1,0:T(8,128)(2,1)}, bf16[1,768,768]{2,1,0:T(8,128)(2,1)S(1)}, u32[]{:S(2)}, u32[]{:S(2)}) collective-permute-start(bf16[1,768,768]{2,1,0:T(8,128)(2,1)} %get-tuple-element.298), channel_id=1, source_target_pairs={{0,8},{4,12},{8,0},{12,4},{16,24},{20,28},{24,16},{28,20},{1,9},{5... | collective-permute-start | bytes 3538952 | tf_op jit(solution)/shard_map/ppermute | solution.py:621
  139.9 27.6 %collective-permute-start.13 = (bf16[1,768,768]{2,1,0:T(8,128)(2,1)S(1)}, bf16[1,768,768]{2,1,0:T(8,128)(2,1)S(1)}, u32[]{:S(2)}, u32[]{:S(2)}) collective-permute-start(bf16[1,768,768]{2,1,0:T(8,128)(2,1)S(1)} %get-tuple-element.299), channel_id=1, source_target_pairs={{0,16},{4,20},{8,24},{12,28},{16,0},{20,4},{24,8},{28,12},{1,17},{... | collective-permute-start | bytes 3538952 | tf_op jit(solution)/shard_map/ppermute | solution.py:621
  157.5 37.0 %collective-permute-start.20 = (bf16[2,256,768]{2,1,0:T(8,128)(2,1)}, bf16[2,256,768]{2,1,0:T(8,128)(2,1)}, u32[]{:S(2)}, u32[]{:S(2)}) collective-permute-start(bf16[2,256,768]{2,1,0:T(8,128)(2,1)} %get-tuple-element.329), channel_id=1, source_target_pairs={{0,4},{4,0},{8,12},{12,8},{16,20},{20,16},{24,28},{28,24},{1,5},{5... | collective-permute-start | bytes 2359304 | tf_op jit(solution)/shard_map/ppermute | solution.py:621
  190.7 17.2 %collective-permute-start.17 = (bf16[1,384,768]{2,1,0:T(8,128)(2,1)S(1)}, bf16[1,384,768]{2,1,0:T(8,128)(2,1)S(1)}, u32[]{:S(2)}, u32[]{:S(2)}) collective-permute-start(bf16[1,384,768]{2,1,0:T(8,128)(2,1)S(1)} %get-tuple-element.321), channel_id=1, source_target_pairs={{0,1},{1,0},{2,3},{3,2},{4,5},{5,4},{6,7},{7,6},{8,9},{9,8},{10,11... | collective-permute-start | bytes 1769480 | tf_op jit(solution)/shard_map/ppermute | solution.py:624
  208.2 22.2 %collective-permute-start.23 = (bf16[1,192,768]{2,1,0:T(8,128)(2,1)S(1)}, bf16[1,192,768]{2,1,0:T(8,128)(2,1)S(1)}, u32[]{:S(2)}, u32[]{:S(2)}) collective-permute-start(bf16[1,192,768]{2,1,0:T(8,128)(2,1)S(1)} %get-tuple-element.349), channel_id=1, source_target_pairs={{0,2},{1,3},{2,0},{3,1},{4,6},{5,7},{6,4},{7,5},{8,10},{9,11},{10,... | collective-permute-start | bytes 884744 | tf_op jit(solution)/shard_map/ppermute | solution.py:624
  213.7 19.8 %collective-permute-start.24 = (bf16[4,96,768]{2,1,0:T(8,128)(2,1)S(1)}, bf16[4,96,768]{2,1,0:T(8,128)(2,1)S(1)}, u32[]{:S(2)}, u32[]{:S(2)}) collective-permute-start(bf16[4,96,768]{2,1,0:T(8,128)(2,1)S(1)} %get-tuple-element.350), channel_id=1, source_target_pairs={{0,8},{4,12},{8,0},{12,4},{16,24},{20,28},{24,16},{28,20},{1,9},{5... | collective-permute-start | bytes 1769480 | tf_op jit(solution)/shard_map/ppermute | solution.py:621
  251.1 21.6 %collective-permute-start.32 = (bf16[1,384,768]{2,1,0:T(8,128)(2,1)S(1)}, bf16[1,384,768]{2,1,0:T(8,128)(2,1)S(1)}, u32[]{:S(2)}, u32[]{:S(2)}) collective-permute-start(bf16[1,384,768]{2,1,0:T(8,128)(2,1)S(1)} %maximum_select_fusion.3), channel_id=1, source_target_pairs={{0,1},{1,0},{2,3},{3,2},{4,5},{5,4},{6,7},{7,6},{8,9},{9,8},{10,11... | collective-permute-start | bytes 1769480 | tf_op jit(solution)/shard_map/ppermute | solution.py:624
  251.4 21.3 %collective-permute-start.30 = (bf16[4,48,768]{2,1,0:T(8,128)(2,1)S(1)}, bf16[4,48,768]{2,1,0:T(8,128)(2,1)S(1)}, u32[]{:S(2)}, u32[]{:S(2)}) collective-permute-start(bf16[4,48,768]{2,1,0:T(8,128)(2,1)S(1)} %get-tuple-element.374), channel_id=1, source_target_pairs={{0,1},{1,0},{2,3},{3,2},{4,5},{5,4},{6,7},{7,6},{8,9},{9,8},{10,11... | collective-permute-start | bytes 884744 | tf_op jit(solution)/shard_map/ppermute | solution.py:624
  273.2 16.5 %collective-permute-start.35 = (bf16[1,384,768]{2,1,0:T(8,128)(2,1)S(1)}, bf16[1,384,768]{2,1,0:T(8,128)(2,1)S(1)}, u32[]{:S(2)}, u32[]{:S(2)}) collective-permute-start(bf16[1,384,768]{2,1,0:T(8,128)(2,1)S(1)} %get-tuple-element.397), channel_id=1, source_target_pairs={{0,16},{4,20},{8,24},{12,28},{16,0},{20,4},{24,8},{28,12},{1,17},{... | collective-permute-start | bytes 1769480 | tf_op jit(solution)/shard_map/ppermute | solution.py:621
  292.2 30.4 %collective-permute-start.45 = (bf16[1,768,768]{2,1,0:T(8,128)(2,1)S(1)}, bf16[1,768,768]{2,1,0:T(8,128)(2,1)}, u32[]{:S(2)}, u32[]{:S(2)}) collective-permute-start(bf16[1,768,768]{2,1,0:T(8,128)(2,1)S(1)} %maximum_select_fusion.2.refs_0_), channel_id=1, source_target_pairs={{0,16},{4,20},{8,24},{12,28},{16,0},{20,4},{24,8},{28,12},{1,17},{... | collective-permute-start | bytes 3538952 | tf_op jit(solution)/shard_map/ppermute | solution.py:621
  293.1 29.6 %collective-permute-start.46 = (bf16[1,768,768]{2,1,0:T(8,128)(2,1)S(1)}, bf16[1,768,768]{2,1,0:T(8,128)(2,1)S(1)}, u32[]{:S(2)}, u32[]{:S(2)}) collective-permute-start(bf16[1,768,768]{2,1,0:T(8,128)(2,1)S(1)} %maximum_select_fusion.2.refs_0_), channel_id=1, source_target_pairs={{0,4},{4,0},{8,12},{12,8},{16,20},{20,16},{24,28},{28,24},{1,5},{5... | collective-permute-start | bytes 3538952 | tf_op jit(solution)/shard_map/ppermute | solution.py:621
  293.7 29.0 %collective-permute-start.43 = (bf16[1,768,768]{2,1,0:T(8,128)(2,1)S(1)}, bf16[1,768,768]{2,1,0:T(8,128)(2,1)}, u32[]{:S(2)}, u32[]{:S(2)}) collective-permute-start(bf16[1,768,768]{2,1,0:T(8,128)(2,1)S(1)} %maximum_select_fusion.1.refs_0_), channel_id=1, source_target_pairs={{0,8},{4,12},{8,0},{12,4},{16,24},{20,28},{24,16},{28,20},{1,9},{5... | collective-permute-start | bytes 3538952 | tf_op jit(solution)/shard_map/ppermute | solution.py:621
  294.3 28.4 %collective-permute-start.44 = (bf16[1,768,768]{2,1,0:T(8,128)(2,1)S(1)}, bf16[1,768,768]{2,1,0:T(8,128)(2,1)S(1)}, u32[]{:S(2)}, u32[]{:S(2)}) collective-permute-start(bf16[1,768,768]{2,1,0:T(8,128)(2,1)S(1)} %maximum_select_fusion.1.refs_0_), channel_id=1, source_target_pairs={{0,4},{4,0},{8,12},{12,8},{16,20},{20,16},{24,28},{28,24},{1,5},{5... | collective-permute-start | bytes 3538952 | tf_op jit(solution)/shard_map/ppermute | solution.py:621
  324.3 32.2 %collective-permute-start.39 = (bf16[384,768]{1,0:T(8,128)(2,1)}, bf16[384,768]{1,0:T(8,128)(2,1)}, u32[]{:S(2)}, u32[]{:S(2)}) collective-permute-start(bf16[384,768]{1,0:T(8,128)(2,1)} %get-tuple-element.393), channel_id=1, source_target_pairs={{4,0},{0,1},{5,2},{1,3},{6,4},{2,5},{7,6},{3,7},{12,8},{8,9},{13,1... | collective-permute-start | bytes 1769480 | tf_op jit(solution)/shard_map/ppermute | solution.py:645
  335.1 21.9 %collective-permute-start.40 = (bf16[384,768]{1,0:T(8,128)(2,1)}, bf16[384,768]{1,0:T(8,128)(2,1)S(1)}, u32[]{:S(2)}, u32[]{:S(2)}) collective-permute-start(bf16[384,768]{1,0:T(8,128)(2,1)} %get-tuple-element.394), channel_id=1, source_target_pairs={{1,0},{5,1},{0,2},{4,3},{3,4},{7,5},{2,6},{6,7},{9,8},{13,9},{8,10... | collective-permute-start | bytes 1769480 | tf_op jit(solution)/shard_map/ppermute | solution.py:645
  (82 other events, 753.4 us)
